TPU v7x, 32 devices: a whole 2x2x4 slice. The times are simulated.
32 devices in a mesh: row: 4 (over y, core), col: 8 (over z, x).
Axes of the slice: x: 2, y: 2, z: 4, core: 2. Of those that a mesh axis runs over, the one named last changes fastest.
Arguments:
- points: bfloat16 [65536, 512], P(('row', 'col')), may hold values from -6 to 6
- factor: bfloat16 [65536, 2048], P(('row', 'col')), may hold values from -0.078125 to 0.078125
- targets: bfloat16 [65536, 256], P(('row', 'col')), may hold values from -6 to 6
- pivot_slots: int32 [32, 32], P(('row', 'col')), may hold values from 0 to 2047, as said below
- pivot_counts: int32 [32], replicated, may hold values from 1 to 32, 512 in all
Outputs:
- new_columns: bfloat16 [512, 65536], P(None, ('row', 'col'))
- residual_next: float32 [65536, 256], P(('row', 'col'))
Inputs may be any that keep to these rules, and one draw needn't show every extreme that they name: `pivot_slots`: each row holds 32 different local row numbers; row d's first pivot_counts[d] entries are device d's pivots, the rest are unused. `pivot_counts`: the counts sum to 512; one of them is 32.
All inputs are finite; a program needn't handle non-finite values.
Results may differ from a plain program's by a relative error of at most 0.0029.
Values may be sent and summed in bfloat16 or wider, within the bound.
No kernel may reach another device: no remote copies, remote signals or barrier semaphores. Data moves between devices by JAX's collectives and lax.ppermute only.
A program may use at most 128 MiB of HBM per device.

v0:
```python
import jax
import jax.numpy as jnp
from jax import lax
from jax.sharding import PartitionSpec as P

BLOCK = 512


sharpness = 1.0
ridge_shift = 0.01
damping = 1.0
epsilon = 1e-06


def normalize(points):
    values = points.astype(jnp.float32)
    factor_scale = lax.rsqrt(jnp.mean(values * values, axis=1, keepdims=True) + epsilon)
    return (values * factor_scale).astype(jnp.bfloat16)


def kernel(left_rows, right_rows, feature_width):
    cosine = (
        lax.dot_general(
            left_rows, right_rows, (((1,), (1,)), ((), ())), preferred_element_type=jnp.float32
        )
        / feature_width
    )
    return jnp.exp(sharpness * (cosine - 1.0))


def compact_index(pivot_counts, block_size):
    owners_count = pivot_counts.shape[0]
    run_ends = jnp.cumsum(pivot_counts)
    run_starts = run_ends - pivot_counts
    position = jnp.arange(block_size, dtype=jnp.int32)
    owners = jnp.sum((position[:, None] >= run_ends[None, :]).astype(jnp.int32), axis=1)
    onehot = (owners[:, None] == jnp.arange(owners_count, dtype=jnp.int32)[None, :]).astype(
        jnp.int32
    )
    first_row = jnp.sum(onehot * run_starts[None, :], axis=1)
    return (owners, position - first_row)


def block_factor(pivot_scaled, pivot_factor):
    intersection = lax.dot_general(
        pivot_factor, pivot_factor, (((1,), (1,)), ((), ())), preferred_element_type=jnp.float32
    )
    diag_shift = ridge_shift + jnp.max(jnp.sum(jnp.abs(intersection), axis=1))
    ridged = (
        kernel(pivot_scaled, pivot_scaled, pivot_scaled.shape[1])
        - intersection
        + diag_shift * jnp.eye(intersection.shape[0], dtype=jnp.float32)
    )
    return jnp.linalg.cholesky(ridged)


def on_device(points, factor, targets, pivot_slots, pivot_counts):
    scaled = normalize(points)
    local_slots = pivot_slots[0]
    slot_cap = pivot_slots.shape[1]
    own_scaled = jnp.take(scaled, local_slots, axis=0)
    own_factor = jnp.take(factor, local_slots, axis=0)
    inner_scaled, inner_factor = (
        lax.all_gather(own_scaled, "col", axis=0, tiled=True),
        lax.all_gather(own_factor, "col", axis=0, tiled=True),
    )
    padded_scaled, padded_factor = (
        lax.all_gather(inner_scaled, "row", axis=0, tiled=True),
        lax.all_gather(inner_factor, "row", axis=0, tiled=True),
    )
    owners, slot_index = compact_index(pivot_counts, BLOCK)
    row_index = owners * slot_cap + slot_index
    pivot_scaled = jnp.take(padded_scaled, row_index, axis=0)
    pivot_factor = jnp.take(padded_factor, row_index, axis=0)
    lower_factor = block_factor(pivot_scaled, pivot_factor)
    downdated = kernel(pivot_scaled, scaled, scaled.shape[1]) - lax.dot_general(
        pivot_factor, factor, (((1,), (1,)), ((), ())), preferred_element_type=jnp.float32
    )
    new_columns = lax.linalg.triangular_solve(
        lower_factor, downdated, left_side=True, lower=True
    ).astype(jnp.bfloat16)
    cross_terms = jnp.concatenate(
        [
            lax.dot_general(
                factor, targets, (((0,), (0,)), ((), ())), preferred_element_type=jnp.float32
            ),
            lax.dot_general(
                new_columns, targets, (((1,), (0,)), ((), ())), preferred_element_type=jnp.float32
            ),
        ],
        axis=0,
    )
    col_norms = jnp.concatenate(
        [
            jnp.sum(jnp.square(factor.astype(jnp.float32)), axis=0),
            jnp.sum(jnp.square(new_columns.astype(jnp.float32)), axis=1),
        ],
        axis=0,
    )
    cross_whole, norm_whole = lax.psum((cross_terms, col_norms), ("row", "col"))
    coefficients = (cross_whole / (norm_whole + damping)[:, None]).astype(jnp.bfloat16)
    held_count = factor.shape[1]
    fitted = jnp.dot(factor, coefficients[:held_count], preferred_element_type=jnp.float32)
    fitted = fitted + lax.dot_general(
        new_columns,
        coefficients[held_count:],
        (((0,), (0,)), ((), ())),
        preferred_element_type=jnp.float32,
    )
    residual_next = targets.astype(jnp.float32) - fitted
    return (new_columns, residual_next)


def solution(mesh):
    return jax.shard_map(
        on_device,
        mesh=mesh,
        in_specs=(
            P(("row", "col"), None),
            P(("row", "col"), None),
            P(("row", "col"), None),
            P(("row", "col"), None),
            P(),
        ),
        out_specs=(P(None, ("row", "col")), P(("row", "col"), None)),
        check_vma=False,
    )
```

profile of v0, /device:TPU:0, one launch (start us, length us, event | category | flops | bytes accessed | tf_op | source)
XLA Modules:
  0.0 457.5 jit_solution(8331831617520132772)
XLA Ops:
  7.2 0.7 fusion.40
  7.9 0.7 compare_and_fusion
  8.5 5.2 %gather_fusion.2 = bf16[32,2048]{1,0:T(8,128)(2,1)S(1)} fusion(bf16[2048,2048]{1,0:T(8,128)(2,1)} %param.6, s32[1024]{0:T(1024)S(1)} %pad_clamp_fusion.1), kind=kCustom, calls=%fused_computation.2 | custom fusion | bytes 262272 | tf_op jit(solution)/shard_map/jit(_take)/gather | solution.py:62
  13.8 0.7 broadcast_select_fusion.6
  14.6 2.2 fusion
  17.3 0.6 gather_fusion
  18.0 35.1 %all_gather.12 = bf16[256,512]{1,0:T(8,128)(2,1)} all-gather(bf16[32,512]{1,0:T(8,128)(2,1)S(1)} %broadcast_select_fusion.7), channel_id=1, replica_groups=mesh['row'=4,'col'=8] {'col'}, dimensions={0}, use_global_device_ids=true | all-gather | bytes 294912 | tf_op jit(solution)/shard_map/all_gather | solution.py:64
  53.2 5.6 %all-gather.6.cloned.1.call-done = bf16[256,2048]{1,0:T(8,128)(2,1)} async-done(((bf16[32,2048]{1,0:T(8,128)(2,1)}), bf16[256,2048]{1,0:T(8,128)(2,1)}) %all-gather.6.cloned.1.call-update) | async-done | bytes 1048592 | tf_op jit(solution)/shard_map/all_gather | solution.py:65
  58.8 0.6 all-reduce.3.cloned.1.call-start
  59.9 7.2 %fusion.51 = f32[2048,256]{1,0:T(8,128)} fusion(bf16[2048,2048]{1,0:T(8,128)(2,1)} %param.6, bf16[2048,256]{1,0:T(8,128)(2,1)S(1)} %copy-done.6), kind=kOutput, calls=%fused_computation.122 | convolution fusion | flops 2147483648 | bytes 11534336 | tf_op jit(solution)/shard_map/dot_general | solution.py:84
  67.1 8.6 %all-gather.4.cloned.1.call-done = bf16[1024,512]{1,0:T(8,128)(2,1)} async-done(((bf16[256,512]{1,0:T(8,128)(2,1)}), bf16[1024,512]{1,0:T(8,128)(2,1)}) %all-gather.4.cloned.1.call-update) | async-done | bytes 1048592 | tf_op jit(solution)/shard_map/all_gather | solution.py:68
  75.7 4.0 gather_fusion.1
  79.7 32.0 %all-gather.8.cloned.1.call-done = bf16[1024,2048]{1,0:T(8,128)(2,1)} async-done(((bf16[256,2048]{1,0:T(8,128)(2,1)}), bf16[1024,2048]{1,0:T(8,128)(2,1)}) %all-gather.8.cloned.1.call-update) | async-done | bytes 4194320 | tf_op jit(solution)/shard_map/all_gather | solution.py:69
  111.8 8.0 %gather_fusion.3 = bf16[512,2048]{1,0:T(8,128)(2,1)} fusion(bf16[1024,2048]{1,0:T(8,128)(2,1)} %all-gather.8.cloned.1.call-done, s32[1024]{0:T(1024)S(1)} %pad_clamp_fusion), kind=kCustom, calls=%fused_computation.3 | custom fusion | bytes 4196352 | tf_op jit(solution)/shard_map/jit(_take)/gather | solution.py:74
  119.7 3.7 abs_reduce_fusion
  123.5 9.8 %fusion.21 = f32[512,2048]{1,0:T(8,128)} fusion(bf16[2048,2048]{1,0:T(8,128)(2,1)} %param.6, bf16[512,2048]{1,0:T(8,128)(2,1)S(1)} %copy-done.4, pred[512]{0:T(512)(128)(4,1)S(1)} %compare_and_fusion.1), kind=kOutput, calls=%fused_computation.51 | convolution fusion | flops 4296015872 | bytes 14680576 | tf_op jit(solution)/shard_map/dot_general | solution.py:76
  133.3 1.3 copy.20
  134.6 2.1 fusion.17
  136.7 1.3 copy.21
  138.1 0.6 reduce_max.9
  139.3 1.4 add_multiply_fusion
  140.8 1.0 copy-done.3
  141.7 11.7 %cholesky.103 = f32[128,128]{1,0:T(8,128)S(1)} custom-call(f32[128,128]{1,0:T(8,128)S(1)} %cholesky.263), custom_call_target="Cholesky" | custom-call | tf_op jit(solution)/shard_map/jit(cholesky)/cholesky | solution.py:54
  153.6 9.8 %custom-call.30 = f32[1,128,128]{1,2,0:T(8,128)S(1)} custom-call(f32[1,128,128]{2,1,0:T(8,128)S(1)} %get-tuple-element.37), custom_call_target="InvertDiagBlocksLowerTriangular" | custom-call | tf_op jit(solution)/shard_map/jit(cholesky)/cholesky | solution.py:54
  163.4 1.2 constant_dynamic-update-slice_fusion.3
  164.7 1.3 convolution_subtract_fusion.2
  165.9 11.7 %cholesky.215 = f32[128,128]{1,0:T(8,128)S(1)} custom-call(f32[128,128]{1,0:T(8,128)S(1)} %cholesky.267), custom_call_target="Cholesky" | custom-call | tf_op jit(solution)/shard_map/jit(cholesky)/cholesky | solution.py:54
  177.7 10.2 %custom-call.31 = f32[1,128,128]{1,2,0:T(8,128)S(1)} custom-call(f32[1,128,128]{2,1,0:T(8,128)S(1)} %get-tuple-element.34), custom_call_target="InvertDiagBlocksLowerTriangular" | custom-call | tf_op jit(solution)/shard_map/jit(cholesky)/cholesky | solution.py:54
  188.2 1.3 convolution_subtract_fusion.3
  189.5 11.7 %cholesky.236 = f32[128,128]{1,0:T(8,128)S(1)} custom-call(f32[128,128]{1,0:T(8,128)S(1)} %cholesky.272), custom_call_target="Cholesky" | custom-call | tf_op jit(solution)/shard_map/jit(cholesky)/cholesky | solution.py:54
  201.2 0.7 compare_reduce_fusion.1
  201.9 9.8 %custom-call.32 = f32[1,128,128]{1,2,0:T(8,128)S(1)} custom-call(f32[1,128,128]{2,1,0:T(8,128)S(1)} %get-tuple-element.31), custom_call_target="InvertDiagBlocksLowerTriangular" | custom-call | tf_op jit(solution)/shard_map/jit(cholesky)/cholesky | solution.py:54
  211.9 1.2 convolution_subtract_fusion.4
  213.1 11.8 %cholesky.253 = f32[128,128]{1,0:T(8,128)S(1)} custom-call(f32[128,128]{1,0:T(8,128)S(1)} %convolution_subtract_fusion.4), custom_call_target="Cholesky" | custom-call | tf_op jit(solution)/shard_map/jit(cholesky)/cholesky | solution.py:54
  225.0 0.6 compare_reduce_fusion
  225.6 0.6 compare_reduce_fusion.2
  228.7 1.1 select_select_fusion
  229.8 13.6 %while.1 = (s32[]{:T(128)}, f32[512,512]{1,0:T(8,128)}, s32[4,2]{0,1:T(2,128)S(1)}, f32[4,128,128]{2,1,0:T(8,128)}, s32[]{:T(128)}) while((s32[]{:T(128)}, f32[512,512]{1,0:T(8,128)}, s32[4,2]{0,1:T(2,128)S(1)}, f32[4,128,128]{2,1,0:T(8,128)}, s32[]{:T(128)}) %tuple.39), condition=%wide.while_cond, body=%wide.while_body.sunk | while | flops 2 | bytes 132705 | solution.py:79
  229.9 0.5 fusion.67
  230.4 2.8 bitcast_dynamic-update-slice_fusion.2
  233.9 2.8 bitcast_dynamic-update-slice_fusion.2
  237.3 2.8 bitcast_dynamic-update-slice_fusion.2
  240.7 2.7 bitcast_dynamic-update-slice_fusion.2
  243.5 40.1 %custom-call.33 = f32[4,128,128]{1,2,0:T(8,128)S(1)} custom-call(f32[4,128,128]{2,1,0:T(8,128)} %get-tuple-element.9), custom_call_target="InvertDiagBlocksLowerTriangular" | custom-call | tf_op jit(solution)/shard_map/triangular_solve | solution.py:79
  283.6 3.7 exponential_subtract_fusion
  287.3 1.1 fusion.50
  288.4 1.9 convolution_subtract_fusion.1
  290.3 1.1 fusion.49
  291.3 2.2 convolution_subtract_fusion
  293.5 1.0 fusion.48
  294.6 3.0 fusion.9
  297.6 1.1 convolution_convert_fusion
  298.6 0.6 multiply_reduce_fusion.1
  299.3 1.3 copy-done
  300.6 0.7 fusion.52
  301.6 1.7 pad_maximum_fusion
  303.3 0.9 copy.22
  304.2 5.1 %multiply_reduce_fusion = f32[2048]{0:T(1024)S(1)} fusion(bf16[2048,2048]{1,0:T(8,128)(2,1)} %param.6), kind=kLoop, calls=%fused_computation.6 | loop fusion | flops 12580864 | bytes 8396800 | tf_op jit(solution)/shard_map/reduce_sum | solution.py:95
  309.3 39.7 %psum.15 = f32[2560]{0:T(1024)S(1)} all-reduce(f32[2560]{0:T(1024)S(1)} %pad_maximum_fusion.2), channel_id=1, replica_groups=mesh['row'=4,'col'=8] {'row','col'}, use_global_device_ids=true, to_apply=%region_17.18 | all-reduce | flops 2560 | bytes 20480 | tf_op jit(solution)/shard_map/psum | solution.py:100
  349.1 91.0 %all-reduce.3.cloned.1.call-done = f32[2560,256]{1,0:T(8,128)} async-done(((f32[2560,256]{1,0:T(8,128)}), f32[2560,256]{1,0:T(8,128)}) %all-reduce.3.cloned.1.call-update) | async-done | bytes 2621456 | tf_op jit(solution)/shard_map/psum | solution.py:100
  440.0 2.1 divide_convert_fusion
  442.2 5.9 %convolution_bitcast_fusion = f32[2048,256]{0,1:T(8,128)S(1)} fusion(bf16[2048,2048]{1,0:T(8,128)(2,1)} %param.6, bf16[2560,256]{1,0:T(8,128)(2,1)S(1)} %divide_convert_fusion), kind=kOutput, calls=%fused_computation.21 | convolution fusion | flops 2147483648 | bytes 11534336 | tf_op jit(solution)/shard_map/dot_general | solution.py:103
  448.1 0.8 fusion.8
  448.9 1.8 copy.24
  (59 shorter events, 4.2 us)
Async XLA Ops:
  7.2 51.6 %all-gather.6.cloned.1.call-start = ((), (), s32[]{:S(2)}) async-start(), calls=%async_computation.1 | async-start | bytes 1179648 | tf_op jit(solution)/shard_map/all_gather | solution.py:65
  14.5 61.2 %all-gather.4.cloned.1.call-start = ((), (), s32[]{:S(2)}) async-start(), calls=%async_computation | async-start | bytes 1310720 | tf_op jit(solution)/shard_map/all_gather | solution.py:68
  14.6 2.3 copy-start.2
  16.8 42.5 %copy-start.8 = (s32[32]{0:T(128)S(1)}, s32[32]{0:T(128)}, u32[]{:S(2)}) copy-start(s32[32]{0:T(128)} %param.9) | copy-start | bytes 388
  16.9 43.0 %copy-start.6 = (bf16[2048,256]{1,0:T(8,128)(2,1)S(1)}, bf16[2048,256]{1,0:T(8,128)(2,1)}, u32[]{:S(2)}) copy-start(bf16[2048,256]{1,0:T(8,128)(2,1)} %param.7) | copy-start | bytes 3145732
  53.1 58.6 %all-gather.8.cloned.1.call-start = ((), (), s32[]{:S(2)}) async-start(), calls=%async_computation.2 | async-start | bytes 5242880 | tf_op jit(solution)/shard_map/all_gather | solution.py:69
  58.8 381.3 %all-reduce.3.cloned.1.call-start = ((), (), s32[]{:S(2)}) async-start(), calls=%async_computation.3 | async-start | bytes 5242880 | tf_op jit(solution)/shard_map/psum | solution.py:100
  119.7 3.8 copy-start.4
  140.7 1.0 copy-start.3
  297.6 3.0 copy-start.7
  299.3 1.3 copy-start
  299.3 2.3 copy-start.5
  442.2 5.9 %copy-start.1 = (bf16[512,2048]{1,0:T(8,128)(2,1)S(1)}, bf16[512,2048]{1,0:T(8,128)(2,1)}, u32[]{:S(2)}) copy-start(bf16[512,2048]{1,0:T(8,128)(2,1)} %copy-done) | copy-start | bytes 6291460
Sparse Core Ops, SparseCore 0:
  14.7 44.0 all-gather.5
  60.3 15.3 all-gather.3
  77.3 34.4 all-gather.7
  303.5 136.5 all-reduce.2
where the time goes:
time: 461 us; the launch traced here: 457 us
  other arithmetic  137 us (30%)
  waiting for transfers between devices  137 us (30%)
  blocking collectives  74.8 us (16%)
  matrix products  50.7 us (11%)
  local copies, waits for them, and re-layouts  39.5 us (9%)
  between operations  17.5 us (4%)
    psum x1, waiting for transfers between devices, on_device(): cross_whole, norm_whole = lax.psum((cross_terms, col_norms), ('row', 'col'))  91 us
    another operation x14, other arithmetic, block_factor(): return jnp.linalg.cholesky(ridged)  78.9 us
    another operation x3, other arithmetic, on_device(): lax.linalg.triangular_solve(lower_factor, downdated, left_side=True, lowe...  41.2 us
    psum x1, blocking collectives, on_device(): cross_whole, norm_whole = lax.psum((cross_terms, col_norms), ('row', 'col'))  39.7 us
    all_gather x1, blocking collectives, on_device(): lax.all_gather(own_scaled, 'col', axis=0, tiled=True)  35.1 us
    all_gather x1, waiting for transfers between devices, on_device(): lax.all_gather(inner_factor, 'row', axis=0, tiled=True)  32 us
    another operation x13, local copies, waits for them, and re-layouts  13.7 us
    another operation x7, matrix products, on_device(): lax.linalg.triangular_solve(lower_factor, downdated, left_side=True, lowe...  11.3 us
  transfers between devices with their start and end apart: 4, of which 4 were waited for; matrix products, arithmetic and copies ran while one was open for 5% of the time, Pallas kernels for 0%

commit v1 on v0

v1 whole, which is shorter than its diff:
```python
import functools

import jax
import jax.numpy as jnp
import numpy as np
from jax import lax
from jax.experimental import pallas as pl
from jax.experimental.pallas import tpu as pltpu
from jax.sharding import PartitionSpec as P

BLOCK = 512
TILE = 128

sharpness = 1.0
ridge_shift = 0.01
damping = 1.0
epsilon = 1e-06

f32 = jnp.float32
bf16 = jnp.bfloat16
AXES = ("row", "col")
VMEM = pl.BlockSpec(memory_space=pltpu.VMEM)
ANY = pl.BlockSpec(memory_space=pl.ANY)


def dot(a, b, da=1, db=0, exact=False):
    return lax.dot_general(
        a,
        b,
        (((da,), (db,)), ((), ())),
        precision=lax.Precision.HIGHEST if exact else None,
        preferred_element_type=f32,
    )


def split(v):
    high = v.astype(bf16)
    return high, (v - high.astype(f32)).astype(bf16)


def normalize(points):
    values = points.astype(f32)
    scale = lax.rsqrt(jnp.mean(values * values, axis=1, keepdims=True) + epsilon)
    return (values * scale).astype(bf16)


class Grid:
    def __init__(self, mesh):
        rows, cols = mesh.shape["row"], mesh.shape["col"]
        c = 2 if rows % 2 == 0 else 1
        x = max(k for k in range(1, cols + 1) if cols % k == 0 and k * k <= cols)
        self.n = {"y": rows // c, "c": c, "z": cols // x, "x": x}
        self.shape = tuple(self.n.values())
        self.size = rows * cols
        self.ids = np.arange(self.size).reshape(self.shape)

    def here(self):
        row, col = lax.axis_index("row"), lax.axis_index("col")
        c, x = self.n["c"], self.n["x"]
        return {"y": row // c, "c": row % c, "z": col // x, "x": col % x}

    def shift(self, value, dim, by):
        to = np.roll(self.ids, -by, axis=list(self.n).index(dim))
        return lax.ppermute(value, AXES, list(zip(self.ids.ravel(), to.ravel())))

    def spread(self, value, dim):
        return [self.shift(value, dim, s) for s in range(1, self.n[dim])]

    def reduce_scatter(self, chunks, dims):
        me, names = self.here(), list(self.n)
        for dim in dims:
            axis, n = names.index(dim), self.n[dim]

            def pick(k):
                return lax.dynamic_index_in_dim(chunks, k, names.index(dim), keepdims=True)

            total = pick(me[dim])
            for s in range(1, n):
                total = total + self.shift(pick((me[dim] + s) % n), dim, s)
            chunks = total
            del axis
        return chunks.reshape(chunks.shape[4:])

    def gather(self, chunk, dims):
        me, names = self.here(), list(self.n)
        whole = chunk[None, None, None, None]
        for dim in dims:
            axis, n = names.index(dim), self.n[dim]
            shape = list(whole.shape)
            shape[axis] = n
            out = jnp.zeros(shape, whole.dtype)
            for s in range(n):
                part = whole if s == 0 else self.shift(whole, dim, s)
                out = lax.dynamic_update_slice_in_dim(out, part, (me[dim] - s) % n, axis)
            whole = out
        return whole


ALIGN = 16


def own_rows_kernel(slots, points, factor, out, pbuf, fbuf, psem, fsem):
    cap = out.shape[0]
    width = points.shape[1]

    def copies(i):
        base = pl.multiple_of((slots[0, i] // ALIGN) * ALIGN, ALIGN)
        return (
            pltpu.make_async_copy(
                points.at[pl.ds(base, ALIGN), :], pbuf.at[pl.ds(i * ALIGN, ALIGN), :], psem.at[i]
            ),
            pltpu.make_async_copy(
                factor.at[pl.ds(base, ALIGN), :], fbuf.at[pl.ds(i * ALIGN, ALIGN), :], fsem.at[i]
            ),
        )

    for i in range(cap):
        for copy in copies(i):
            copy.start()
    r = lax.broadcasted_iota(jnp.int32, (cap, cap * ALIGN), 0)
    q = lax.broadcasted_iota(jnp.int32, (cap, cap * ALIGN), 1)
    target = jnp.full((cap, cap * ALIGN), -1, jnp.int32)
    for i in range(cap):
        target = jnp.where(r == i, slots[0, i] % ALIGN + i * ALIGN, target)
    pick = (q == target).astype(f32).astype(bf16)
    for i in range(cap):
        for copy in copies(i):
            copy.wait()
    rows = dot(pick, pbuf[...]).astype(bf16)
    out[:, :width] = normalize(rows)
    out[:, width:] = dot(pick, fbuf[...]).astype(bf16)


def own_rows(points, factor, slots):
    cap = slots.shape[1]
    wide = points.shape[1] + factor.shape[1]
    return pl.pallas_call(
        own_rows_kernel,
        out_shape=jax.ShapeDtypeStruct((cap, wide), bf16),
        in_specs=[pl.BlockSpec(memory_space=pltpu.SMEM), ANY, ANY],
        out_specs=VMEM,
        scratch_shapes=[
            pltpu.VMEM((cap * ALIGN, points.shape[1]), bf16),
            pltpu.VMEM((cap * ALIGN, factor.shape[1]), bf16),
            pltpu.SemaphoreType.DMA((cap,)),
            pltpu.SemaphoreType.DMA((cap,)),
        ],
        cost_estimate=pl.CostEstimate(flops=10**8, bytes_accessed=3 * 10**6, transcendentals=0),
    )(slots, points, factor)


def prepare_kernel(count, width, *refs):
    place, pieces = refs[0], refs[1 : 1 + count]
    scaled_ref, factor_ref, ridged_ref, rows, sems = refs[1 + count :]
    copies, at = [], 0
    for k, piece in enumerate(pieces):
        n = piece.shape[0]
        copies.append(pltpu.make_async_copy(piece, rows.at[pl.ds(at, n), :], sems.at[k]))
        at += n
    for copy in copies:
        copy.start()
    slot = lax.broadcasted_iota(jnp.int32, (BLOCK, at), 0)
    pick = (slot == place[...]).astype(f32).astype(bf16)
    for copy in copies:
        copy.wait()
    step = width
    for lo in range(0, rows.shape[1], step):
        part = dot(pick, rows[:, lo : lo + step]).astype(bf16)
        if lo == 0:
            scaled_ref[...] = part
        else:
            factor_ref[:, lo - width : lo - width + step] = part
    inter = dot(factor_ref[...], factor_ref[...], 1, 1)
    shift = ridge_shift + jnp.max(jnp.sum(jnp.abs(inter), axis=1, keepdims=True))
    cosine = dot(scaled_ref[...], scaled_ref[...], 1, 1) / width
    r = lax.broadcasted_iota(jnp.int32, (BLOCK, BLOCK), 0)
    c = lax.broadcasted_iota(jnp.int32, (BLOCK, BLOCK), 1)
    ridged_ref[...] = jnp.exp(sharpness * (cosine - 1.0)) - inter + jnp.where(r == c, shift, 0.0)


def prepare(place, pieces, width):
    wide = pieces[0].shape[1]
    total = sum(p.shape[0] for p in pieces)
    return pl.pallas_call(
        functools.partial(prepare_kernel, len(pieces), width),
        out_shape=(
            jax.ShapeDtypeStruct((BLOCK, width), bf16),
            jax.ShapeDtypeStruct((BLOCK, wide - width), bf16),
            jax.ShapeDtypeStruct((BLOCK, BLOCK), f32),
        ),
        in_specs=[VMEM] + [ANY] * len(pieces),
        out_specs=(VMEM,) * 3,
        scratch_shapes=[
            pltpu.VMEM((total, wide), bf16),
            pltpu.SemaphoreType.DMA((len(pieces),)),
        ],
        cost_estimate=pl.CostEstimate(
            flops=6 * 10**9, bytes_accessed=10**7, transcendentals=BLOCK * BLOCK
        ),
    )(place, *pieces)


def downdate_kernel(ps, pf, points, factor, targets, high_ref, low_ref, z_ref, acc):
    step = pl.program_id(0)
    cosine = dot(ps[...], normalize(points[...]), 1, 1) / ps.shape[1]
    down = jnp.exp(sharpness * (cosine - 1.0)) - dot(pf[...], factor[...], 1, 1)
    high, low = split(down)
    high_ref[...] = high
    low_ref[...] = low
    part = dot(high, targets[...]) + dot(low, targets[...])

    @pl.when(step == 0)
    def _():
        acc[...] = part

    @pl.when(step > 0)
    def _():
        acc[...] += part

    @pl.when(step == pl.num_programs(0) - 1)
    def _():
        z_ref[...] = acc[...].T


def downdate(ps, pf, points, factor, targets):
    pts, width, held, nt = points.shape[0], points.shape[1], factor.shape[1], targets.shape[1]
    blk = 256
    return pl.pallas_call(
        downdate_kernel,
        grid=(pts // blk,),
        out_shape=(
            jax.ShapeDtypeStruct((BLOCK, pts), bf16),
            jax.ShapeDtypeStruct((BLOCK, pts), bf16),
            jax.ShapeDtypeStruct((nt, BLOCK), f32),
        ),
        in_specs=[
            pl.BlockSpec((BLOCK, width), lambda i: (0, 0)),
            pl.BlockSpec((BLOCK, held), lambda i: (0, 0)),
            pl.BlockSpec((blk, width), lambda i: (i, 0)),
            pl.BlockSpec((blk, held), lambda i: (i, 0)),
            pl.BlockSpec((blk, nt), lambda i: (i, 0)),
        ],
        out_specs=(
            pl.BlockSpec((BLOCK, blk), lambda i: (0, i)),
            pl.BlockSpec((BLOCK, blk), lambda i: (0, i)),
            pl.BlockSpec((nt, BLOCK), lambda i: (0, 0)),
        ),
        scratch_shapes=[pltpu.VMEM((BLOCK, nt), f32)],
        cost_estimate=pl.CostEstimate(
            flops=6 * 10**9, bytes_accessed=16 * 10**6, transcendentals=BLOCK * pts
        ),
    )(ps, pf, points, factor, targets)


def across(v):
    return jnp.broadcast_to(v, (8, TILE))


def base8(tile, lane0):
    e = [[None] * 8 for _ in range(8)]
    for s in range(8):
        col = across(tile[:, lane0 + s : lane0 + s + 1])
        for t in range(s, 8):
            e[t][s] = across(col[t : t + 1, :])
    x = [[None] * 8 for _ in range(8)]
    low = [[None] * 8 for _ in range(8)]
    for s in range(8):
        r = lax.rsqrt(e[s][s])
        for t in range(s + 1, 8):
            low[t][s] = e[t][s] * r
        for u in range(s + 1, 8):
            for t in range(u, 8):
                e[t][u] = e[t][u] - low[t][s] * low[u][s]
        for c in range(s):
            acc = low[s][c] * x[c][c]
            for u in range(c + 1, s):
                acc = acc + low[s][u] * x[u][c]
            x[s][c] = -(r * acc)
        x[s][s] = r
    return x


def columns(x, rowid):
    out = []
    for s in range(8):
        c = jnp.where(rowid == s, x[s][s], 0.0)
        for t in range(s + 1, 8):
            c = jnp.where(rowid == t, x[t][s], c)
        out.append(c)
    return out


def diagonal_block(s_ref, w_ref):
    n, group = TILE, 32
    rowid = lax.broadcasted_iota(jnp.int32, (8, n), 0)
    ri = lax.broadcasted_iota(jnp.int32, (n, n), 0)
    ci = lax.broadcasted_iota(jnp.int32, (n, n), 1)
    w_ref[...] = jnp.where(ri == ci, 1.0, 0.0).astype(f32)
    for g in range(0, n, group):
        tiles = [s_ref[g + 8 * i : g + 8 * i + 8, :] for i in range(4)]
        sides = [w_ref[g + 8 * i : g + 8 * i + 8, :] for i in range(4)]
        for j in range(4):
            lane0 = g + 8 * j
            x = base8(tiles[j], lane0)
            cols = columns(x, rowid)
            u = cols[0] * across(tiles[j][0:1, :])
            q = cols[0] * across(sides[j][0:1, :])
            for s in range(1, 8):
                u = u + cols[s] * across(tiles[j][s : s + 1, :])
                q = q + cols[s] * across(sides[j][s : s + 1, :])
            tiles[j], sides[j] = u, q
            for i in range(j + 1, 4):
                b = [across(tiles[i][:, lane0 + k : lane0 + k + 1]) for k in range(8)]
                t, v = tiles[i], sides[i]
                for s in range(8):
                    m = x[s][0] * b[0]
                    for k in range(1, s + 1):
                        m = m + x[s][k] * b[k]
                    t = t - m * across(u[s : s + 1, :])
                    v = v - m * across(q[s : s + 1, :])
                tiles[i], sides[i] = t, v
        ug = jnp.concatenate(tiles, 0)
        vg = jnp.concatenate(sides, 0)
        w_ref[g : g + group, :] = vg
        if g + group < n:
            lo = g + group
            upd = dot(ug, jnp.concatenate([ug, vg], 1), 0, 0, exact=True)
            s_ref[lo:, :] = s_ref[lo:, :] - upd[lo:, :n]
            w_ref[lo:, :] = w_ref[lo:, :] - upd[lo:, n:]


def factor_kernel(first, last, a_in, r_in, a_ref, r_ref, s_ref, w_ref):
    n, blocks = TILE, BLOCK // TILE
    a_ref[...] = a_in[...]
    r_ref[...] = r_in[...]
    for k in range(first, last):
        o = n * k
        s_ref[...] = a_ref[o : o + n, o : o + n]
        diagonal_block(s_ref, w_ref)
        inv = w_ref[...]
        if k:
            r_ref[o : o + n, :o] = dot(inv, r_ref[o : o + n, :o], exact=True)
        r_ref[o : o + n, o : o + n] = inv
        if k < blocks - 1:
            u = dot(inv, a_ref[o : o + n, o + n :], exact=True)
            wk = r_ref[o : o + n, : o + n]
            a_ref[o + n :, o + n :] = a_ref[o + n :, o + n :] - dot(u, u, 0, 0, exact=True)
            r_ref[o + n :, : o + n] = r_ref[o + n :, : o + n] - dot(u, wk, 0, 0, exact=True)


def factor_step(a, r, first, last):
    return pl.pallas_call(
        functools.partial(factor_kernel, first, last),
        out_shape=(jax.ShapeDtypeStruct(a.shape, f32),) * 2,
        in_specs=[VMEM] * 2,
        out_specs=(VMEM,) * 2,
        scratch_shapes=[pltpu.VMEM((TILE, TILE), f32)] * 2,
        input_output_aliases={0: 0, 1: 1},
        cost_estimate=pl.CostEstimate(
            flops=12 * 10**9, bytes_accessed=4 * 10**6, transcendentals=0
        ),
    )(a, r)


def columns_kernel(inv, z, high, low, new_ref, cross_ref, norm_ref, acc, ih, il):
    step = pl.program_id(0)

    @pl.when(step == 0)
    def _():
        ih[...], il[...] = split(inv[...])
        cross_ref[...] = dot(z[...], inv[...], 1, 1, exact=True)

    h = high[...]
    new = (dot(ih[...], h) + (dot(ih[...], low[...]) + dot(il[...], h))).astype(bf16)
    new_ref[...] = new
    wide = new.astype(f32)
    part = wide * wide

    @pl.when(step == 0)
    def _():
        acc[...] = part

    @pl.when(step > 0)
    def _():
        acc[...] += part

    @pl.when(step == pl.num_programs(0) - 1)
    def _():
        norm_ref[...] = jnp.sum(acc[...].T, axis=0, keepdims=True)


def make_columns(inv, z, high, low):
    pts, blk = high.shape[1], 256
    return pl.pallas_call(
        columns_kernel,
        grid=(pts // blk,),
        out_shape=(
            jax.ShapeDtypeStruct((BLOCK, pts), bf16),
            jax.ShapeDtypeStruct(z.shape, f32),
            jax.ShapeDtypeStruct((1, BLOCK), f32),
        ),
        in_specs=[
            pl.BlockSpec((BLOCK, BLOCK), lambda i: (0, 0)),
            pl.BlockSpec(z.shape, lambda i: (0, 0)),
            pl.BlockSpec((BLOCK, blk), lambda i: (0, i)),
            pl.BlockSpec((BLOCK, blk), lambda i: (0, i)),
        ],
        out_specs=(
            pl.BlockSpec((BLOCK, blk), lambda i: (0, i)),
            pl.BlockSpec(z.shape, lambda i: (0, 0)),
            pl.BlockSpec((1, BLOCK), lambda i: (0, 0)),
        ),
        scratch_shapes=[
            pltpu.VMEM((BLOCK, blk), f32),
            pltpu.VMEM((BLOCK, BLOCK), bf16),
            pltpu.VMEM((BLOCK, BLOCK), bf16),
        ],
        cost_estimate=pl.CostEstimate(
            flops=4 * 10**9, bytes_accessed=8 * 10**6, transcendentals=0
        ),
    )(inv, z, high, low)


def on_device(grid, points, factor, targets, pivot_slots, pivot_counts):
    n, me = grid.n, grid.here()
    cap, devices = pivot_slots.shape[1], grid.size
    held, nt, width = factor.shape[1], targets.shape[1], points.shape[1]

    own = own_rows(points, factor, pivot_slots)
    blocks = [own] + grid.spread(own, "z")
    zs = [(0, 0, s, 0) for s in range(n["z"])]
    half = (n["z"] + 1) // 2

    def moved(origin, dim):
        at = "yczx".index(dim)
        return [
            tuple(v + s if k == at else v for k, v in enumerate(o))
            for s in range(1, n[dim])
            for o in origin
        ]

    pieces, origins = [jnp.concatenate(blocks, 0)], list(zs)
    for part, origin, dims in (
        (blocks[:half], zs[:half], "xy"),
        (blocks[half:], zs[half:], "yx"),
    ):
        if not part:
            continue
        held_here, held_origin = jnp.concatenate(part, 0), origin
        for dim in dims:
            if n[dim] == 1:
                continue
            got = grid.spread(held_here, dim)
            arrived = jnp.concatenate(got, 0) if len(got) > 1 else got[0]
            new_origin = moved(held_origin, dim)
            pieces.append(arrived)
            origins += new_origin
            held_here = jnp.concatenate([held_here, arrived], 0)
            held_origin = held_origin + new_origin
    zdone = pieces[0]
    mine = list(pieces)
    for s in range(1, n["c"]):
        pieces += [grid.shift(p, "c", s) for p in mine]
        origins += [(o[0], o[1] + s, o[2], o[3]) for o in origins[: len(origins)]]

    shifts = np.array(origins)
    dev = jnp.zeros((len(origins),), jnp.int32)
    for k, dim in enumerate("yczx"):
        dev = dev * n[dim] + (me[dim] - shifts[:, k]) % n[dim]
    ends = jnp.cumsum(pivot_counts)
    onehot = dev[:, None] == jnp.arange(devices, dtype=jnp.int32)[None, :]
    count = jnp.sum(jnp.where(onehot, pivot_counts[None, :], 0), axis=1)
    start = jnp.sum(jnp.where(onehot, (ends - pivot_counts)[None, :], 0), axis=1)
    slot = jnp.arange(cap, dtype=jnp.int32)[None, :]
    place = jnp.where(slot < count[:, None], start[:, None] + slot, -1).reshape(1, -1)

    cross = dot(factor, targets, 0, 0)
    squares = jnp.sum(jnp.square(factor.astype(f32)), axis=0)
    m = held // devices
    extra = 8 * -(-m // (8 * nt))
    chunks = jnp.concatenate(
        [
            cross.reshape(devices, m, nt),
            jnp.pad(squares.reshape(devices, m), ((0, 0), (0, extra * nt - m))).reshape(
                devices, extra, nt
            ),
        ],
        axis=1,
    )
    chunks, zdone = lax.optimization_barrier((chunks, zdone))
    chunk = grid.reduce_scatter(chunks.reshape(grid.shape + chunks.shape[1:]), "czxy")
    norm = chunk[m:].reshape(-1)[:m]
    coef = (chunk[:m] / (norm + damping)[:, None]).astype(bf16)
    coef_held = grid.gather(coef, "zxyc").reshape(held, nt)

    ps, pf, ridged = prepare(place, pieces, width)
    high, low, z = downdate(ps, pf, points, factor, targets)
    t = nt // devices
    z_own = grid.reduce_scatter(z.reshape(grid.shape + (t, BLOCK)), "cxyz")

    inverse = jnp.zeros((BLOCK, BLOCK), f32)
    middle = BLOCK // TILE // 2
    ridged, inverse = factor_step(ridged, inverse, 0, middle)
    ridged, inverse = factor_step(ridged, inverse, middle, BLOCK // TILE)

    new_columns, cross_own, norm_own = make_columns(inverse, z_own, high, low)
    nh, nl = split(norm_own)
    nl2 = (norm_own - nh.astype(f32) - nl.astype(f32)).astype(bf16)
    late = jnp.concatenate([cross_own.astype(bf16), nh, nl, nl2], axis=0)
    late = jnp.pad(late, ((0, -late.shape[0] % 16), (0, 0)))
    every = lax.all_to_all(
        jnp.broadcast_to(late[None], (devices,) + late.shape), AXES, 0, 0, tiled=True
    ).astype(f32)
    norm_new = jnp.sum(every[:, t : t + 3], axis=(0, 1))
    coef_new = (every[:, :t].reshape(nt, BLOCK) / (norm_new + damping)[None, :]).astype(bf16)

    fitted = jnp.dot(factor, coef_held, preferred_element_type=f32)
    fitted = fitted + dot(new_columns, coef_new, 0, 1)
    return new_columns, targets.astype(f32) - fitted


def solution(mesh):
    spec = P(AXES, None)
    return jax.shard_map(
        functools.partial(on_device, Grid(mesh)),
        mesh=mesh,
        in_specs=(spec, spec, spec, spec, P()),
        out_specs=(P(None, AXES), spec),
        check_vma=False,
    )
```

time: 461 us -> 193 us (0.42)
  other arithmetic: 137 us -> 20.7 us
  waiting for transfers between devices: 137 us -> 33.2 us
  blocking collectives: 74.8 us -> 0 us
  Pallas kernels: 0 us -> 66.2 us
  starting transfers between devices: 0.69 us -> 43.5 us
  matrix products: 50.7 us -> 14 us
  local copies, waits for them, and re-layouts: 39.5 us -> 13.2 us
  between operations: 17.5 us -> 1.1 us
    another operation x19 -> x2, other arithmetic: 120 us -> 1.4 us  [the longest x14 78.9 us: block_factor(): return jnp.linalg.cholesky(ridged)]
    psum x1 -> x0, waiting for transfers between devices: 91 us -> none  [on_device(): cross_whole, norm_whole = lax.psum((cross_terms, col_norms), ('row', 'col'))]
    pallas_call x0 -> x6, Pallas kernels: none -> 66.2 us  [the longest x2 28.2 us: factor_step(): pl.pallas_call(functools.partial(factor_kernel, first, last), out_shape=(...]
    all_gather x3 -> x0, waiting for transfers between devices: 46.3 us -> none  [the longest x1 32 us: on_device(): lax.all_gather(inner_factor, 'row', axis=0, tiled=True)]
    psum x1 -> x0, blocking collectives: 39.7 us -> none  [on_device(): cross_whole, norm_whole = lax.psum((cross_terms, col_norms), ('row', 'col'))]
    ppermute x0 -> x30, starting transfers between devices: none -> 38.9 us  [shift(): return lax.ppermute(value, AXES, list(zip(self.ids.ravel(), to.ravel())))]
    all_gather x1 -> x0, blocking collectives: 35.1 us -> none  [on_device(): lax.all_gather(own_scaled, 'col', axis=0, tiled=True)]
    ppermute x0 -> x30, waiting for transfers between devices: none -> 22.7 us  [shift(): return lax.ppermute(value, AXES, list(zip(self.ids.ravel(), to.ravel())))]
  transfers between devices with their start and end apart: 4 -> 31, of which waited for: 4 -> 14; matrix products, arithmetic and copies ran while one was open for 5% -> 19% of each run, Pallas kernels for 0% -> 32%
where the time goes in v1:
time: 193 us; the launch traced here: 192 us
  Pallas kernels  66.2 us (34%)
  starting transfers between devices  43.5 us (23%)
  waiting for transfers between devices  33.2 us (17%)
  other arithmetic  20.7 us (11%)
  matrix products  14 us (7%)
  local copies, waits for them, and re-layouts  13.2 us (7%)
    ppermute x30, starting transfers between devices, shift(): return lax.ppermute(value, AXES, list(zip(self.ids.ravel(), to.ravel())))  38.9 us
    pallas_call x2, Pallas kernels, factor_step(): pl.pallas_call(functools.partial(factor_kernel, first, last), out_shape=(...  28.2 us
    ppermute x30, waiting for transfers between devices, shift(): return lax.ppermute(value, AXES, list(zip(self.ids.ravel(), to.ravel())))  22.7 us
    pallas_call x1, Pallas kernels, downdate(): pl.pallas_call(downdate_kernel, grid=(pts // blk,), out_shape=(jax.ShapeD...  14.8 us
    all_to_all x1, waiting for transfers between devices, on_device(): lax.all_to_all(jnp.broadcast_to(late[None], (devices,) + late.shape), AXE...  10.5 us
    pallas_call x1, Pallas kernels, make_columns(): pl.pallas_call(columns_kernel, grid=(pts // blk,), out_shape=(jax.ShapeDt...  10.2 us
    pallas_call x1, Pallas kernels, prepare(): pl.pallas_call(functools.partial(prepare_kernel, len(pieces), width), out...  8.54 us
    dot_general x2, matrix products, dot(): lax.dot_general(a, b, (((da,), (db,)), ((), ())), precision=lax.Precision...  7.88 us
  transfers between devices with their start and end apart: 31, of which 14 were waited for; matrix products, arithmetic and copies ran while one was open for 19% of the time, Pallas kernels for 32%

profile of v1, /device:TPU:0, one launch (start us, length us, event | category | flops | bytes accessed | tf_op | source)
XLA Modules:
  0.0 192.0 jit_solution(12087407543651851836)
XLA Ops:
  0.6 4.4 %shard_map.104 = bf16[32,2560]{1,0:T(8,128)(2,1)} custom-call(s32[1,32]{1,0:T(1,128)} %slots.1, bf16[2048,512]{1,0:T(8,128)(2,1)} %points.3, bf16[2048,2048]{1,0:T(8,128)(2,1)} %factor.3), custom_call_target="tpu_custom_call" | custom-call | flops 100000000 | bytes 3000000 | tf_op jit(solution)/shard_map/pallas_call | solution.py:137
  5.0 4.1 %collective-permute-start.1 = (bf16[32,2560]{1,0:T(8,128)(2,1)}, bf16[32,2560]{1,0:T(8,128)(2,1)S(1)}, u32[]{:S(2)}, u32[]{:S(2)}) collective-permute-start(bf16[32,2560]{1,0:T(8,128)(2,1)} %shard_map.104), channel_id=1, source_target_pairs={{0,4},{1,5},{2,6},{3,7},{4,0},{5,1},{6,2},{7,3},{8,12},{9,13},{10,... | collective-permute-start | bytes 491528 | tf_op jit(solution)/shard_map/ppermute | solution.py:64
  9.2 1.3 collective-permute-start.2
  10.5 0.7 collective-permute-start
  11.2 7.2 %fusion.28 = f32[2048,256]{1,0:T(8,128)} fusion(bf16[2048,2048]{1,0:T(8,128)(2,1)} %factor.3, bf16[2048,256]{1,0:T(8,128)(2,1)S(1)} %copy-done.2), kind=kOutput, calls=%fused_computation.91 | convolution fusion | flops 2147483648 | bytes 11534336 | tf_op jit(solution)/shard_map/dot_general | solution.py:27
  18.8 0.7 pad_maximum_fusion.6
  19.5 2.1 %collective-permute-start.5 = (bf16[64,2560]{1,0:T(8,128)(2,1)}, bf16[64,2560]{1,0:T(8,128)(2,1)}, u32[]{:S(2)}, u32[]{:S(2)}) collective-permute-start(bf16[64,2560]{1,0:T(8,128)(2,1)} %pad_maximum_fusion.6), channel_id=1, source_target_pairs={{0,16},{1,17},{2,18},{3,19},{4,20},{5,21},{6,22},{7,23},{8,24},{9,... | collective-permute-start | bytes 983048 | tf_op jit(solution)/shard_map/ppermute | solution.py:64
  21.8 0.8 pad_maximum_fusion.5
  22.6 1.5 collective-permute-start.3
  24.1 5.1 %multiply_reduce_fusion = f32[2048]{0:T(1024)S(1)} fusion(bf16[2048,2048]{1,0:T(8,128)(2,1)} %factor.3), kind=kLoop, calls=%fused_computation | loop fusion | flops 12580864 | bytes 8396800 | tf_op jit(solution)/shard_map/reduce_sum | solution.py:478
  29.4 1.8 pad_maximum_fusion
  31.5 2.4 %pad_maximum_fusion.4 = (bf16[128,2560]{1,0:T(8,128)(2,1)}, bf16[128,2560]{1,0:T(8,128)(2,1)}, bf16[128,2560]{1,0:T(8,128)(2,1)}) fusion(bf16[64,2560]{1,0:T(8,128)(2,1)} %collective-permute-done.5.refs_4_, bf16[32,2560]{1,0:T(8,128)(2,1)S(1)} %collective-permute-done.2, bf16[32,2560]{1,0:T(8,128)(2,1)S(1)} %collective-permute-done.1, ...), kind=kLoop, calls=%fused_computation.9 | loop fusion | flops 5570560 | bytes 3276800 | tf_op jit(solution)/shard_map/concatenate | solution.py:458
  34.1 1.5 collective-permute-start.6
  35.6 1.5 collective-permute-start.4
  37.1 0.7 copy.27
  37.8 0.8 reduce-window.9
  38.6 0.6 reduce
  39.2 0.7 sub.78
  39.9 0.7 fusion.17
  40.7 10.8 %collective-permute-done.6.refs_5_ = bf16[128,2560]{1,0:T(8,128)(2,1)} collective-permute-done((bf16[128,2560]{1,0:T(8,128)(2,1)}, bf16[128,2560]{1,0:T(8,128)(2,1)}, u32[]{:S(2)}, u32[]{:S(2)}) %collective-permute-start.6) | collective-permute-done | bytes 655392 | tf_op jit(solution)/shard_map/ppermute | solution.py:64
  51.5 1.2 collective-permute-done.4.refs_3_
  52.7 1.4 select_reduce_fusion.1
  54.1 0.7 add_select_fusion
  54.8 0.7 select_n.240.refs_0_
  56.0 1.4 dynamic-slice_add_fusion
  57.5 5.0 %collective-permute-start.19 = (f32[2,1,1,2,72,256]{5,4,3,2,1,0:T(8,128)S(1)}, f32[2,1,1,2,72,256]{5,4,3,2,1,0:T(8,128)S(1)}, u32[]{:S(2)}, u32[]{:S(2)}) collective-permute-start(f32[2,1,1,2,72,256]{5,4,3,2,1,0:T(8,128)S(1)} %get-tuple-element.40), channel_id=1, source_target_pairs={{0,2},{1,3},{2,4},{3,5},{4,6},{5,7},{6,0},{7,1},{8,10},{9,11},{10,... | collective-permute-start | bytes 884744 | tf_op jit(solution)/shard_map/ppermute | solution.py:64
  62.5 1.4 collective-permute-start.20
  64.0 2.6 %collective-permute-start.21 = (f32[2,1,1,2,72,256]{5,4,3,2,1,0:T(8,128)S(1)}, f32[2,1,1,2,72,256]{5,4,3,2,1,0:T(8,128)S(1)}, u32[]{:S(2)}, u32[]{:S(2)}) collective-permute-start(f32[2,1,1,2,72,256]{5,4,3,2,1,0:T(8,128)S(1)} %get-tuple-element.41), channel_id=1, source_target_pairs={{0,6},{1,7},{2,0},{3,1},{4,2},{5,3},{6,4},{7,5},{8,14},{9,15},{10,... | collective-permute-start | bytes 884744 | tf_op jit(solution)/shard_map/ppermute | solution.py:64
  66.6 8.5 %shard_map.105 = (bf16[512,512]{1,0:T(8,128)(2,1)}, bf16[512,2048]{1,0:T(8,128)(2,1)}, f32[512,512]{1,0:T(8,128)}) custom-call(s32[1,1024]{1,0:T(1,128)} %select_n.240.refs_0_, bf16[128,2560]{1,0:T(8,128)(2,1)} %get-tuple-element.44.refs_1_, bf16[64,2560]{1,0:T(8,128)(2,1)} %collective-permute-done.3.refs_2_, ...), custom_call_target="tpu_custom_call" | custom-call | flops 6000000000 | bytes 10000000 | tf_op jit(solution)/shard_map/pallas_call | solution.py:184
  75.1 14.8 %shard_map.108 = (bf16[512,2048]{1,0:T(8,128)(2,1)}, bf16[512,2048]{1,0:T(8,128)(2,1)}, f32[256,512]{1,0:T(8,128)}) custom-call(bf16[512,512]{1,0:T(8,128)(2,1)} %get-tuple-element.19.ps, bf16[512,2048]{1,0:T(8,128)(2,1)} %get-tuple-element.20.pf, bf16[2048,512]{1,0:T(8,128)(2,1)} %points.3, bf16[2048,2048]{1,0:T(8,128)(2,1)} %factor.3, ...), custom_call_target="tpu_custom_call" | custom-call | flops 6000000000 | bytes 16000000 | tf_op jit(solution)/shard_map/pallas_call | solution.py:228
  90.0 1.7 constant_dynamic-slice_fusion.11
  91.7 1.1 broadcast_in_dim.57.r_in
  92.8 14.6 %shard_map.106 = (f32[512,512]{1,0:T(8,128)}, f32[512,512]{1,0:T(8,128)}) custom-call(f32[512,512]{1,0:T(8,128)} %get-tuple-element.15.a_in, f32[512,512]{1,0:T(8,128)} %broadcast_in_dim.57.r_in), custom_call_target="tpu_custom_call", output_to_operand_aliasing={{0}: (0, {}), {1}: (1, {})} | custom-call | flops 12000000000 | bytes 4000000 | tf_op jit(solution)/shard_map/pallas_call | solution.py:352
  107.4 13.6 %shard_map.107 = (f32[512,512]{1,0:T(8,128)}, f32[512,512]{1,0:T(8,128)}) custom-call(f32[512,512]{1,0:T(8,128)} %get-tuple-element.16.a_in, f32[512,512]{1,0:T(8,128)} %get-tuple-element.17.r_in), custom_call_target="tpu_custom_call", output_to_operand_aliasing={{0}: (0, {}), {1}: (1, {})} | custom-call | flops 12000000000 | bytes 4000000 | tf_op jit(solution)/shard_map/pallas_call | solution.py:352
  121.1 0.9 collective-permute-start.22
  122.0 1.0 dynamic-slice_add_fusion.1
  123.0 4.5 %collective-permute-done.22 = f32[2,1,1,1,72,256]{5,4,3,2,1,0:T(8,128)S(1)} collective-permute-done((f32[2,1,1,1,72,256]{5,4,3,2,1,0:T(8,128)S(1)}, f32[2,1,1,1,72,256]{5,4,3,2,1,0:T(8,128)S(1)}, u32[]{:S(2)}, u32[]{:S(2)}) %collective-permute-start.22) | collective-permute-done | bytes 147488 | tf_op jit(solution)/shard_map/ppermute | solution.py:64
  127.5 1.6 collective-permute-start.23
  129.1 0.9 collective-permute-start.13
  129.9 2.0 %collective-permute-done.23 = f32[1,1,1,1,72,256]{5,4,3,2,1,0:T(8,128)S(1)} collective-permute-done((f32[1,1,1,1,72,256]{5,4,3,2,1,0:T(8,128)S(1)}, f32[1,1,1,1,72,256]{5,4,3,2,1,0:T(8,128)S(1)}, u32[]{:S(2)}, u32[]{:S(2)}) %collective-permute-start.23) | collective-permute-done | bytes 73760 | tf_op jit(solution)/shard_map/ppermute | solution.py:64
  132.1 0.9 collective-permute-start.25
  133.0 2.9 %collective-permute-start.26 = (bf16[1,1,1,1,64,256]{5,4,3,2,1,0:T(8,128)(2,1)S(1)}, bf16[1,1,1,1,64,256]{5,4,3,2,1,0:T(8,128)(2,1)S(1)}, u32[]{:S(2)}, u32[]{:S(2)}) collective-permute-start(bf16[1,1,1,1,64,256]{5,4,3,2,1,0:T(8,128)(2,1)S(1)} %get-tuple-element.39), channel_id=1, source_target_pairs={{0,6},{1,7},{2,0},{3,1},{4,2},{5,3},{6,4},{7,5},{8,14},{9,15},{10,... | collective-permute-start | bytes 98312 | tf_op jit(solution)/shard_map/ppermute | solution.py:64
  136.0 1.6 collective-permute-start.14
  138.4 0.8 collective-permute-start.27
  139.2 1.1 collective-permute-done.14
  140.4 0.9 collective-permute-start.15
  141.3 1.8 collective-permute-start.16
  143.1 2.3 %collective-permute-start.17 = (f32[1,1,1,1,8,512]{5,4,3,2,1,0:T(8,128)S(1)}, f32[1,1,1,1,8,512]{5,4,3,2,1,0:T(8,128)S(1)}, u32[]{:S(2)}, u32[]{:S(2)}) collective-permute-start(f32[1,1,1,1,8,512]{5,4,3,2,1,0:T(8,128)S(1)} %get-tuple-element.47), channel_id=1, source_target_pairs={{0,6},{1,7},{2,0},{3,1},{4,2},{5,3},{6,4},{7,5},{8,14},{9,15},{10,... | collective-permute-start | bytes 49160 | tf_op jit(solution)/shard_map/ppermute | solution.py:64
  145.4 0.6 collective-permute-done.15
  146.1 0.7 collective-permute-done.17
  147.5 10.2 %shard_map.109 = (bf16[512,2048]{1,0:T(8,128)(2,1)}, f32[8,512]{1,0:T(8,128)}, f32[1,512]{1,0:T(1,128)}) custom-call(f32[512,512]{1,0:T(8,128)} %get-tuple-element.18.inv, f32[8,512]{1,0:T(8,128)} %add_bitcast_fusion.z, bf16[512,2048]{1,0:T(8,128)(2,1)} %get-tuple-element.22.high, bf16[512,2048]{1,0:T(8,128)(2,1)} %get-tuple-element.23.low), custom_call_target="tpu_custom_call" | custom-call | flops 4000000000 | bytes 8000000 | tf_op jit(solution)/shard_map/pallas_call | solution.py:394
  157.7 0.8 convert_element_type.42
  158.5 0.7 fusion.27
  159.3 1.6 collective-permute-start.28
  160.9 0.9 broadcast_in_dim.62
  161.7 4.6 %all-to-all-start = ((bf16[32,16,512]{2,1,0:T(8,128)(2,1)}), bf16[32,16,512]{2,1,0:T(8,128)(2,1)S(1)}, u32[]{:S(2)}, u32[]{:S(2)}) async-start(bf16[32,16,512]{2,1,0:T(8,128)(2,1)} %broadcast_in_dim.62), calls=%async_computation | async-start | bytes 1048576 | tf_op jit(solution)/shard_map/all_to_all | solution.py:511
  166.9 1.4 copy.28
  168.3 1.1 broadcast_in_dim.58
  169.4 0.8 constant_dynamic-update-slice_fusion.1
  170.2 1.9 constant_dynamic-update-slice_fusion
  172.1 10.5 %all-to-all-done = bf16[32,16,512]{2,1,0:T(8,128)(2,1)S(1)} async-done(((bf16[32,16,512]{2,1,0:T(8,128)(2,1)}), bf16[32,16,512]{2,1,0:T(8,128)(2,1)S(1)}, u32[]{:S(2)}, u32[]{:S(2)}) %all-to-all-start) | async-done | bytes 524320 | tf_op jit(solution)/shard_map/all_to_all | solution.py:511
  182.8 0.7 fusion.4
  184.0 6.1 %fusion.1 = f32[2048,256]{0,1:T(8,128)S(1)} fusion(f32[2048,256]{0,1:T(8,128)S(1)} %fusion.4, bf16[2048,256]{1,0:T(8,128)(2,1)} %bitcast.5, bf16[2048,2048]{1,0:T(8,128)(2,1)} %factor.3, bf16[2048,256]{0,1:T(8,128)(2,1)S(1)} %copy-done.4), kind=kOutput, calls=%fused_computation.3 | convolution fusion | flops 2149056512 | bytes 14680064 | tf_op jit(solution)/shard_map/dot_general | solution.py:517
  190.2 1.8 copy.31
  (84 shorter events, 5.0 us)
Async XLA Ops:
  0.6 10.6 %copy-start.2 = (bf16[2048,256]{1,0:T(8,128)(2,1)S(1)}, bf16[2048,256]{1,0:T(8,128)(2,1)}, u32[]{:S(2)}) copy-start(bf16[2048,256]{1,0:T(8,128)(2,1)} %targets.1) | copy-start | bytes 3145732
  5.0 16.8 %copy-start.1 = (bf16[32,2560]{1,0:T(8,128)(2,1)S(1)}, bf16[32,2560]{1,0:T(8,128)(2,1)}, u32[]{:S(2)}) copy-start(bf16[32,2560]{1,0:T(8,128)(2,1)} %shard_map.104) | copy-start | bytes 491524
  5.0 13.7 %collective-permute-start.1 = (bf16[32,2560]{1,0:T(8,128)(2,1)}, bf16[32,2560]{1,0:T(8,128)(2,1)S(1)}, u32[]{:S(2)}, u32[]{:S(2)}) collective-permute-start(bf16[32,2560]{1,0:T(8,128)(2,1)} %shard_map.104), channel_id=1, source_target_pairs={{0,4},{1,5},{2,6},{3,7},{4,0},{5,1},{6,2},{7,3},{8,12},{9,13},{10,... | collective-permute-start | bytes 491528 | tf_op jit(solution)/shard_map/ppermute | solution.py:64
  9.2 9.6 %collective-permute-start.2 = (bf16[32,2560]{1,0:T(8,128)(2,1)}, bf16[32,2560]{1,0:T(8,128)(2,1)S(1)}, u32[]{:S(2)}, u32[]{:S(2)}) collective-permute-start(bf16[32,2560]{1,0:T(8,128)(2,1)} %shard_map.104), channel_id=1, source_target_pairs={{0,6},{1,7},{2,0},{3,1},{4,2},{5,3},{6,4},{7,5},{8,14},{9,15},{10,... | collective-permute-start | bytes 491528 | tf_op jit(solution)/shard_map/ppermute | solution.py:64
  10.5 11.3 %collective-permute-start = (bf16[32,2560]{1,0:T(8,128)(2,1)}, bf16[32,2560]{1,0:T(8,128)(2,1)S(1)}, u32[]{:S(2)}, u32[]{:S(2)}) collective-permute-start(bf16[32,2560]{1,0:T(8,128)(2,1)} %shard_map.104), channel_id=1, source_target_pairs={{0,2},{1,3},{2,4},{3,5},{4,6},{5,7},{6,0},{7,1},{8,10},{9,11},{10,... | collective-permute-start | bytes 491528 | tf_op jit(solution)/shard_map/ppermute | solution.py:64
  19.5 11.7 %collective-permute-start.5 = (bf16[64,2560]{1,0:T(8,128)(2,1)}, bf16[64,2560]{1,0:T(8,128)(2,1)}, u32[]{:S(2)}, u32[]{:S(2)}) collective-permute-start(bf16[64,2560]{1,0:T(8,128)(2,1)} %pad_maximum_fusion.6), channel_id=1, source_target_pairs={{0,16},{1,17},{2,18},{3,19},{4,20},{5,21},{6,22},{7,23},{8,24},{9,... | collective-permute-start | bytes 983048 | tf_op jit(solution)/shard_map/ppermute | solution.py:64
  22.6 8.9 %collective-permute-start.3 = (bf16[64,2560]{1,0:T(8,128)(2,1)}, bf16[64,2560]{1,0:T(8,128)(2,1)}, u32[]{:S(2)}, u32[]{:S(2)}) collective-permute-start(bf16[64,2560]{1,0:T(8,128)(2,1)} %pad_maximum_fusion.5), channel_id=1, source_target_pairs={{0,1},{1,0},{2,3},{3,2},{4,5},{5,4},{6,7},{7,6},{8,9},{9,8},{10,11... | collective-permute-start | bytes 983048 | tf_op jit(solution)/shard_map/ppermute | solution.py:64
  31.2 5.9 %copy-start.6 = (s32[32]{0:T(128)S(1)}, s32[32]{0:T(128)}, u32[]{:S(2)}) copy-start(s32[32]{0:T(128)} %param.13) | copy-start | bytes 388
  34.0 22.0 %collective-permute-start.18 = (f32[2,1,4,2,72,256]{5,4,3,2,1,0:T(8,128)S(1)}, f32[2,1,4,2,72,256]{5,4,3,2,1,0:T(8,128)}, u32[]{:S(2)}, u32[]{:S(2)}) collective-permute-start(f32[2,1,4,2,72,256]{5,4,3,2,1,0:T(8,128)S(1)} %constant_dynamic-slice_fusion.5), channel_id=1, source_target_pairs={{0,8},{1,9},{2,10},{3,11},{4,12},{5,13},{6,14},{7,15},{8,0},{9,1},... | collective-permute-start | bytes 3538952 | tf_op jit(solution)/shard_map/ppermute | solution.py:64
  34.1 17.4 %collective-permute-start.6 = (bf16[128,2560]{1,0:T(8,128)(2,1)}, bf16[128,2560]{1,0:T(8,128)(2,1)}, u32[]{:S(2)}, u32[]{:S(2)}) collective-permute-start(bf16[128,2560]{1,0:T(8,128)(2,1)} %get-tuple-element.43), channel_id=1, source_target_pairs={{0,1},{1,0},{2,3},{3,2},{4,5},{5,4},{6,7},{7,6},{8,9},{9,8},{10,11... | collective-permute-start | bytes 1966088 | tf_op jit(solution)/shard_map/ppermute | solution.py:64
  35.6 17.1 %collective-permute-start.4 = (bf16[128,2560]{1,0:T(8,128)(2,1)}, bf16[128,2560]{1,0:T(8,128)(2,1)}, u32[]{:S(2)}, u32[]{:S(2)}) collective-permute-start(bf16[128,2560]{1,0:T(8,128)(2,1)} %get-tuple-element.45), channel_id=1, source_target_pairs={{0,16},{1,17},{2,18},{3,19},{4,20},{5,21},{6,22},{7,23},{8,24},{9,... | collective-permute-start | bytes 1966088 | tf_op jit(solution)/shard_map/ppermute | solution.py:64
  40.6 23.4 %collective-permute-start.7 = (bf16[128,2560]{1,0:T(8,128)(2,1)}, bf16[128,2560]{1,0:T(8,128)(2,1)}, u32[]{:S(2)}, u32[]{:S(2)}) collective-permute-start(bf16[128,2560]{1,0:T(8,128)(2,1)} %get-tuple-element.44.refs_1_), channel_id=1, source_target_pairs={{0,8},{1,9},{2,10},{3,11},{4,12},{5,13},{6,14},{7,15},{8,0},{9,1},... | collective-permute-start | bytes 1966088 | tf_op jit(solution)/shard_map/ppermute | solution.py:64
  51.5 15.1 %collective-permute-start.11 = (bf16[128,2560]{1,0:T(8,128)(2,1)}, bf16[128,2560]{1,0:T(8,128)(2,1)}, u32[]{:S(2)}, u32[]{:S(2)}) collective-permute-start(bf16[128,2560]{1,0:T(8,128)(2,1)} %collective-permute-done.6.refs_5_), channel_id=1, source_target_pairs={{0,8},{1,9},{2,10},{3,11},{4,12},{5,13},{6,14},{7,15},{8,0},{9,1},... | collective-permute-start | bytes 1966088 | tf_op jit(solution)/shard_map/ppermute | solution.py:64
  52.7 13.9 %collective-permute-start.9 = (bf16[128,2560]{1,0:T(8,128)(2,1)}, bf16[128,2560]{1,0:T(8,128)(2,1)}, u32[]{:S(2)}, u32[]{:S(2)}) collective-permute-start(bf16[128,2560]{1,0:T(8,128)(2,1)} %collective-permute-done.4.refs_3_), channel_id=1, source_target_pairs={{0,8},{1,9},{2,10},{3,11},{4,12},{5,13},{6,14},{7,15},{8,0},{9,1},... | collective-permute-start | bytes 1966088 | tf_op jit(solution)/shard_map/ppermute | solution.py:64
  55.5 2.0 %collective-permute-start.10 = (bf16[64,2560]{1,0:T(8,128)(2,1)}, bf16[64,2560]{1,0:T(8,128)(2,1)S(1)}, u32[]{:S(2)}, u32[]{:S(2)}) collective-permute-start(bf16[64,2560]{1,0:T(8,128)(2,1)} %collective-permute-done.5.refs_4_), channel_id=1, source_target_pairs={{0,8},{1,9},{2,10},{3,11},{4,12},{5,13},{6,14},{7,15},{8,0},{9,1},... | collective-permute-start | bytes 983048 | tf_op jit(solution)/shard_map/ppermute | solution.py:64
  56.0 6.5 %collective-permute-start.8 = (bf16[64,2560]{1,0:T(8,128)(2,1)}, bf16[64,2560]{1,0:T(8,128)(2,1)S(1)}, u32[]{:S(2)}, u32[]{:S(2)}) collective-permute-start(bf16[64,2560]{1,0:T(8,128)(2,1)} %collective-permute-done.3.refs_2_), channel_id=1, source_target_pairs={{0,8},{1,9},{2,10},{3,11},{4,12},{5,13},{6,14},{7,15},{8,0},{9,1},... | collective-permute-start | bytes 983048 | tf_op jit(solution)/shard_map/ppermute | solution.py:64
  57.5 9.0 %copy-start.7 = (bf16[64,2560]{1,0:T(8,128)(2,1)}, bf16[64,2560]{1,0:T(8,128)(2,1)S(1)}, u32[]{:S(2)}) copy-start(bf16[64,2560]{1,0:T(8,128)(2,1)S(1)} %collective-permute-done.10.refs_9_) | copy-start | bytes 983044
  57.5 63.5 %collective-permute-start.19 = (f32[2,1,1,2,72,256]{5,4,3,2,1,0:T(8,128)S(1)}, f32[2,1,1,2,72,256]{5,4,3,2,1,0:T(8,128)S(1)}, u32[]{:S(2)}, u32[]{:S(2)}) collective-permute-start(f32[2,1,1,2,72,256]{5,4,3,2,1,0:T(8,128)S(1)} %get-tuple-element.40), channel_id=1, source_target_pairs={{0,2},{1,3},{2,4},{3,5},{4,6},{5,7},{6,0},{7,1},{8,10},{9,11},{10,... | collective-permute-start | bytes 884744 | tf_op jit(solution)/shard_map/ppermute | solution.py:64
  62.5 4.0 %copy-start.8 = (bf16[64,2560]{1,0:T(8,128)(2,1)}, bf16[64,2560]{1,0:T(8,128)(2,1)S(1)}, u32[]{:S(2)}) copy-start(bf16[64,2560]{1,0:T(8,128)(2,1)S(1)} %collective-permute-done.8.refs_7_) | copy-start | bytes 983044
  62.5 58.5 %collective-permute-start.20 = (f32[2,1,1,2,72,256]{5,4,3,2,1,0:T(8,128)S(1)}, f32[2,1,1,2,72,256]{5,4,3,2,1,0:T(8,128)S(1)}, u32[]{:S(2)}, u32[]{:S(2)}) collective-permute-start(f32[2,1,1,2,72,256]{5,4,3,2,1,0:T(8,128)S(1)} %get-tuple-element.42), channel_id=1, source_target_pairs={{0,4},{1,5},{2,6},{3,7},{4,0},{5,1},{6,2},{7,3},{8,12},{9,13},{10,... | collective-permute-start | bytes 884744 | tf_op jit(solution)/shard_map/ppermute | solution.py:64
  64.0 57.0 %collective-permute-start.21 = (f32[2,1,1,2,72,256]{5,4,3,2,1,0:T(8,128)S(1)}, f32[2,1,1,2,72,256]{5,4,3,2,1,0:T(8,128)S(1)}, u32[]{:S(2)}, u32[]{:S(2)}) collective-permute-start(f32[2,1,1,2,72,256]{5,4,3,2,1,0:T(8,128)S(1)} %get-tuple-element.41), channel_id=1, source_target_pairs={{0,6},{1,7},{2,0},{3,1},{4,2},{5,3},{6,4},{7,5},{8,14},{9,15},{10,... | collective-permute-start | bytes 884744 | tf_op jit(solution)/shard_map/ppermute | solution.py:64
  91.7 30.3 %collective-permute-start.12 = (f32[2,1,4,2,8,512]{5,4,3,2,1,0:T(8,128)}, f32[2,1,4,2,8,512]{5,4,3,2,1,0:T(8,128)}, u32[]{:S(2)}, u32[]{:S(2)}) collective-permute-start(f32[2,1,4,2,8,512]{5,4,3,2,1,0:T(8,128)} %constant_dynamic-slice_fusion.11), channel_id=1, source_target_pairs={{0,8},{1,9},{2,10},{3,11},{4,12},{5,13},{6,14},{7,15},{8,0},{9,1},... | collective-permute-start | bytes 786440 | tf_op jit(solution)/shard_map/ppermute | solution.py:64
  107.4 14.6 %copy-start.5 = (f32[256,512]{1,0:T(8,128)S(1)}, f32[256,512]{1,0:T(8,128)}, u32[]{:S(2)}) copy-start(f32[256,512]{1,0:T(8,128)} %get-tuple-element.21) | copy-start | bytes 1572868
  121.1 6.3 %collective-permute-start.22 = (f32[2,1,1,1,72,256]{5,4,3,2,1,0:T(8,128)S(1)}, f32[2,1,1,1,72,256]{5,4,3,2,1,0:T(8,128)S(1)}, u32[]{:S(2)}, u32[]{:S(2)}) collective-permute-start(f32[2,1,1,1,72,256]{5,4,3,2,1,0:T(8,128)S(1)} %constant_dynamic-slice_fusion.1), channel_id=1, source_target_pairs={{0,1},{1,0},{2,3},{3,2},{4,5},{5,4},{6,7},{7,6},{8,9},{9,8},{10,11... | collective-permute-start | bytes 442376 | tf_op jit(solution)/shard_map/ppermute | solution.py:64
  127.5 4.4 %collective-permute-start.23 = (f32[1,1,1,1,72,256]{5,4,3,2,1,0:T(8,128)S(1)}, f32[1,1,1,1,72,256]{5,4,3,2,1,0:T(8,128)S(1)}, u32[]{:S(2)}, u32[]{:S(2)}) collective-permute-start(f32[1,1,1,1,72,256]{5,4,3,2,1,0:T(8,128)S(1)} %constant_dynamic-slice_fusion), channel_id=1, source_target_pairs={{0,16},{1,17},{2,18},{3,19},{4,20},{5,21},{6,22},{7,23},{8,24},{9,... | collective-permute-start | bytes 221192 | tf_op jit(solution)/shard_map/ppermute | solution.py:64
  129.1 6.9 %collective-permute-start.13 = (f32[2,1,4,1,8,512]{5,4,3,2,1,0:T(8,128)S(1)}, f32[2,1,4,1,8,512]{5,4,3,2,1,0:T(8,128)S(1)}, u32[]{:S(2)}, u32[]{:S(2)}) collective-permute-start(f32[2,1,4,1,8,512]{5,4,3,2,1,0:T(8,128)S(1)} %constant_dynamic-slice_fusion.10), channel_id=1, source_target_pairs={{0,1},{1,0},{2,3},{3,2},{4,5},{5,4},{6,7},{7,6},{8,9},{9,8},{10,11... | collective-permute-start | bytes 393224 | tf_op jit(solution)/shard_map/ppermute | solution.py:64
  132.1 5.8 %collective-permute-start.24 = (bf16[1,1,1,1,64,256]{5,4,3,2,1,0:T(8,128)(2,1)S(1)}, bf16[1,1,1,1,64,256]{5,4,3,2,1,0:T(8,128)(2,1)S(1)}, u32[]{:S(2)}, u32[]{:S(2)}) collective-permute-start(bf16[1,1,1,1,64,256]{5,4,3,2,1,0:T(8,128)(2,1)S(1)} %get-tuple-element.39), channel_id=1, source_target_pairs={{0,2},{1,3},{2,4},{3,5},{4,6},{5,7},{6,0},{7,1},{8,10},{9,11},{10,... | collective-permute-start | bytes 98312 | tf_op jit(solution)/shard_map/ppermute | solution.py:64
  132.1 5.7 %collective-permute-start.25 = (bf16[1,1,1,1,64,256]{5,4,3,2,1,0:T(8,128)(2,1)S(1)}, bf16[1,1,1,1,64,256]{5,4,3,2,1,0:T(8,128)(2,1)S(1)}, u32[]{:S(2)}, u32[]{:S(2)}) collective-permute-start(bf16[1,1,1,1,64,256]{5,4,3,2,1,0:T(8,128)(2,1)S(1)} %get-tuple-element.39), channel_id=1, source_target_pairs={{0,4},{1,5},{2,6},{3,7},{4,0},{5,1},{6,2},{7,3},{8,12},{9,13},{10,... | collective-permute-start | bytes 98312 | tf_op jit(solution)/shard_map/ppermute | solution.py:64
  133.0 5.4 %collective-permute-start.26 = (bf16[1,1,1,1,64,256]{5,4,3,2,1,0:T(8,128)(2,1)S(1)}, bf16[1,1,1,1,64,256]{5,4,3,2,1,0:T(8,128)(2,1)S(1)}, u32[]{:S(2)}, u32[]{:S(2)}) collective-permute-start(bf16[1,1,1,1,64,256]{5,4,3,2,1,0:T(8,128)(2,1)S(1)} %get-tuple-element.39), channel_id=1, source_target_pairs={{0,6},{1,7},{2,0},{3,1},{4,2},{5,3},{6,4},{7,5},{8,14},{9,15},{10,... | collective-permute-start | bytes 98312 | tf_op jit(solution)/shard_map/ppermute | solution.py:64
  136.0 4.3 %collective-permute-start.14 = (f32[1,1,4,1,8,512]{5,4,3,2,1,0:T(8,128)S(1)}, f32[1,1,4,1,8,512]{5,4,3,2,1,0:T(8,128)S(1)}, u32[]{:S(2)}, u32[]{:S(2)}) collective-permute-start(f32[1,1,4,1,8,512]{5,4,3,2,1,0:T(8,128)S(1)} %constant_dynamic-slice_fusion.9), channel_id=1, source_target_pairs={{0,16},{1,17},{2,18},{3,19},{4,20},{5,21},{6,22},{7,23},{8,24},{9,... | collective-permute-start | bytes 196616 | tf_op jit(solution)/shard_map/ppermute | solution.py:64
  138.4 20.8 %collective-permute-start.27 = (bf16[1,1,4,1,64,256]{5,4,3,2,1,0:T(8,128)(2,1)S(1)}, bf16[1,1,4,1,64,256]{5,4,3,2,1,0:T(8,128)(2,1)S(1)}, u32[]{:S(2)}, u32[]{:S(2)}) collective-permute-start(bf16[1,1,4,1,64,256]{5,4,3,2,1,0:T(8,128)(2,1)S(1)} %constant_dynamic-update-slice_fusion.6), channel_id=1, source_target_pairs={{0,1},{1,0},{2,3},{3,2},{4,5},{5,4},{6,7},{7,6},{8,9},{9,8},{10,11... | collective-permute-start | bytes 393224 | tf_op jit(solution)/shard_map/ppermute | solution.py:64
  140.4 5.7 %collective-permute-start.15 = (f32[1,1,1,1,8,512]{5,4,3,2,1,0:T(8,128)S(1)}, f32[1,1,1,1,8,512]{5,4,3,2,1,0:T(8,128)S(1)}, u32[]{:S(2)}, u32[]{:S(2)}) collective-permute-start(f32[1,1,1,1,8,512]{5,4,3,2,1,0:T(8,128)S(1)} %get-tuple-element.46), channel_id=1, source_target_pairs={{0,2},{1,3},{2,4},{3,5},{4,6},{5,7},{6,0},{7,1},{8,10},{9,11},{10,... | collective-permute-start | bytes 49160 | tf_op jit(solution)/shard_map/ppermute | solution.py:64
  141.3 4.8 %collective-permute-start.16 = (f32[1,1,1,1,8,512]{5,4,3,2,1,0:T(8,128)S(1)}, f32[1,1,1,1,8,512]{5,4,3,2,1,0:T(8,128)S(1)}, u32[]{:S(2)}, u32[]{:S(2)}) collective-permute-start(f32[1,1,1,1,8,512]{5,4,3,2,1,0:T(8,128)S(1)} %get-tuple-element.48), channel_id=1, source_target_pairs={{0,4},{1,5},{2,6},{3,7},{4,0},{5,1},{6,2},{7,3},{8,12},{9,13},{10,... | collective-permute-start | bytes 49160 | tf_op jit(solution)/shard_map/ppermute | solution.py:64
  143.1 3.7 %collective-permute-start.17 = (f32[1,1,1,1,8,512]{5,4,3,2,1,0:T(8,128)S(1)}, f32[1,1,1,1,8,512]{5,4,3,2,1,0:T(8,128)S(1)}, u32[]{:S(2)}, u32[]{:S(2)}) collective-permute-start(f32[1,1,1,1,8,512]{5,4,3,2,1,0:T(8,128)S(1)} %get-tuple-element.47), channel_id=1, source_target_pairs={{0,6},{1,7},{2,0},{3,1},{4,2},{5,3},{6,4},{7,5},{8,14},{9,15},{10,... | collective-permute-start | bytes 49160 | tf_op jit(solution)/shard_map/ppermute | solution.py:64
  157.7 9.2 %copy-start.3 = (bf16[2048,256]{1,0:T(8,128)(2,1)S(1)}, bf16[2048,256]{1,0:T(8,128)(2,1)}, u32[]{:S(2)}) copy-start(bf16[2048,256]{1,0:T(8,128)(2,1)} %targets.1) | copy-start | bytes 3145732
  159.3 7.2 %collective-permute-start.28 = (bf16[1,1,4,2,64,256]{5,4,3,2,1,0:T(8,128)(2,1)S(1)}, bf16[1,1,4,2,64,256]{5,4,3,2,1,0:T(8,128)(2,1)S(1)}, u32[]{:S(2)}, u32[]{:S(2)}) collective-permute-start(bf16[1,1,4,2,64,256]{5,4,3,2,1,0:T(8,128)(2,1)S(1)} %constant_dynamic-update-slice_fusion.4), channel_id=1, source_target_pairs={{0,16},{1,17},{2,18},{3,19},{4,20},{5,21},{6,22},{7,23},{8,24},{9,... | collective-permute-start | bytes 786440 | tf_op jit(solution)/shard_map/ppermute | solution.py:64
  161.7 20.9 %all-to-all-start = ((bf16[32,16,512]{2,1,0:T(8,128)(2,1)}), bf16[32,16,512]{2,1,0:T(8,128)(2,1)S(1)}, u32[]{:S(2)}, u32[]{:S(2)}) async-start(bf16[32,16,512]{2,1,0:T(8,128)(2,1)} %broadcast_in_dim.62), calls=%async_computation | async-start | bytes 1048576 | tf_op jit(solution)/shard_map/all_to_all | solution.py:511
  166.5 3.7 %collective-permute-start.29 = (bf16[2,1,4,2,64,256]{5,4,3,2,1,0:T(8,128)(2,1)S(1)}, bf16[2,1,4,2,64,256]{5,4,3,2,1,0:T(8,128)(2,1)}, u32[]{:S(2)}, u32[]{:S(2)}) collective-permute-start(bf16[2,1,4,2,64,256]{5,4,3,2,1,0:T(8,128)(2,1)S(1)} %constant_dynamic-update-slice_fusion.2), channel_id=1, source_target_pairs={{0,8},{1,9},{2,10},{3,11},{4,12},{5,13},{6,14},{7,15},{8,0},{9,1},... | collective-permute-start | bytes 1572872 | tf_op jit(solution)/shard_map/ppermute | solution.py:64
  169.4 13.4 %copy-start = (bf16[512,2048]{1,0:T(8,128)(2,1)S(1)}, bf16[512,2048]{1,0:T(8,128)(2,1)}, u32[]{:S(2)}) copy-start(bf16[512,2048]{1,0:T(8,128)(2,1)} %get-tuple-element.34) | copy-start | bytes 6291460
  182.8 1.2 copy-start.4

commit v2 on v1

--- a/solution.py
+++ b/solution.py
@@ -10,6 +10,7 @@
 
 BLOCK = 512
 TILE = 128
+
 
 sharpness = 1.0
 ridge_shift = 0.01
@@ -66,34 +67,24 @@
     def spread(self, value, dim):
         return [self.shift(value, dim, s) for s in range(1, self.n[dim])]
 
-    def reduce_scatter(self, chunks, dims):
-        me, names = self.here(), list(self.n)
-        for dim in dims:
-            axis, n = names.index(dim), self.n[dim]
-
-            def pick(k):
-                return lax.dynamic_index_in_dim(chunks, k, names.index(dim), keepdims=True)
-
-            total = pick(me[dim])
-            for s in range(1, n):
-                total = total + self.shift(pick((me[dim] + s) % n), dim, s)
-            chunks = total
-            del axis
-        return chunks.reshape(chunks.shape[4:])
-
-    def gather(self, chunk, dims):
-        me, names = self.here(), list(self.n)
-        whole = chunk[None, None, None, None]
-        for dim in dims:
-            axis, n = names.index(dim), self.n[dim]
-            shape = list(whole.shape)
-            shape[axis] = n
-            out = jnp.zeros(shape, whole.dtype)
-            for s in range(n):
-                part = whole if s == 0 else self.shift(whole, dim, s)
-                out = lax.dynamic_update_slice_in_dim(out, part, (me[dim] - s) % n, axis)
-            whole = out
-        return whole
+    def take(self, chunks, dim, by=0):
+        at = (self.here()[dim] + by) % self.n[dim]
+        return lax.dynamic_index_in_dim(chunks, at, list(self.n).index(dim), keepdims=True)
+
+    def sends(self, chunks, dim):
+        return [self.take(chunks, dim, s) for s in range(1, self.n[dim])]
+
+    def reduce(self, chunks, dim, sends=None):
+        total = self.take(chunks, dim)
+        for s, part in enumerate(sends or self.sends(chunks, dim), 1):
+            total = total + self.shift(part, dim, s).astype(f32)
+        return total
+
+    def exchange(self, parts):
+        return lax.all_to_all(parts, AXES, 0, 0, tiled=True)
+
+    def everywhere(self, part):
+        return self.exchange(jnp.broadcast_to(part[None], (self.size,) + part.shape))
 
 
 ALIGN = 16
@@ -427,55 +418,9 @@
     held, nt, width = factor.shape[1], targets.shape[1], points.shape[1]
 
     own = own_rows(points, factor, pivot_slots)
-    blocks = [own] + grid.spread(own, "z")
-    zs = [(0, 0, s, 0) for s in range(n["z"])]
-    half = (n["z"] + 1) // 2
-
-    def moved(origin, dim):
-        at = "yczx".index(dim)
-        return [
-            tuple(v + s if k == at else v for k, v in enumerate(o))
-            for s in range(1, n[dim])
-            for o in origin
-        ]
-
-    pieces, origins = [jnp.concatenate(blocks, 0)], list(zs)
-    for part, origin, dims in (
-        (blocks[:half], zs[:half], "xy"),
-        (blocks[half:], zs[half:], "yx"),
-    ):
-        if not part:
-            continue
-        held_here, held_origin = jnp.concatenate(part, 0), origin
-        for dim in dims:
-            if n[dim] == 1:
-                continue
-            got = grid.spread(held_here, dim)
-            arrived = jnp.concatenate(got, 0) if len(got) > 1 else got[0]
-            new_origin = moved(held_origin, dim)
-            pieces.append(arrived)
-            origins += new_origin
-            held_here = jnp.concatenate([held_here, arrived], 0)
-            held_origin = held_origin + new_origin
-    zdone = pieces[0]
-    mine = list(pieces)
-    for s in range(1, n["c"]):
-        pieces += [grid.shift(p, "c", s) for p in mine]
-        origins += [(o[0], o[1] + s, o[2], o[3]) for o in origins[: len(origins)]]
-
-    shifts = np.array(origins)
-    dev = jnp.zeros((len(origins),), jnp.int32)
-    for k, dim in enumerate("yczx"):
-        dev = dev * n[dim] + (me[dim] - shifts[:, k]) % n[dim]
-    ends = jnp.cumsum(pivot_counts)
-    onehot = dev[:, None] == jnp.arange(devices, dtype=jnp.int32)[None, :]
-    count = jnp.sum(jnp.where(onehot, pivot_counts[None, :], 0), axis=1)
-    start = jnp.sum(jnp.where(onehot, (ends - pivot_counts)[None, :], 0), axis=1)
-    slot = jnp.arange(cap, dtype=jnp.int32)[None, :]
-    place = jnp.where(slot < count[:, None], start[:, None] + slot, -1).reshape(1, -1)
-
-    cross = dot(factor, targets, 0, 0)
-    squares = jnp.sum(jnp.square(factor.astype(f32)), axis=0)
+    own, late_factor = lax.optimization_barrier((own, factor))
+    cross = dot(late_factor, targets, 0, 0)
+    squares = jnp.sum(jnp.square(late_factor.astype(f32)), axis=0)
     m = held // devices
     extra = 8 * -(-m // (8 * nt))
     chunks = jnp.concatenate(
@@ -487,16 +432,69 @@
         ],
         axis=1,
     )
-    chunks, zdone = lax.optimization_barrier((chunks, zdone))
-    chunk = grid.reduce_scatter(chunks.reshape(grid.shape + chunks.shape[1:]), "czxy")
-    norm = chunk[m:].reshape(-1)[:m]
-    coef = (chunk[:m] / (norm + damping)[:, None]).astype(bf16)
-    coef_held = grid.gather(coef, "zxyc").reshape(held, nt)
-
+    chunks = grid.reduce(chunks.reshape(grid.shape + chunks.shape[1:]), "c")
+    sends = [part.astype(bf16) for part in grid.sends(chunks, "z")]
+
+    arrived = grid.spread(own, "z")
+    along_z = jnp.concatenate([own] + arrived, 0)
+    along_z, sends = lax.optimization_barrier((along_z, sends))
+    zs = [(0, 0, s, 0) for s in range(n["z"])]
+
+    def moved(origin, dim, s):
+        at = "yczx".index(dim)
+        return [tuple(v + s if k == at else v for k, v in enumerate(o)) for o in origin]
+
+    pieces, origins = [along_z], list(zs)
+    by_x, by_y = grid.spread(along_z, "x"), grid.spread(along_z, "y")
+    pieces += by_x + by_y
+    for s in range(1, n["x"]):
+        origins += moved(zs, "x", s)
+    for s in range(1, n["y"]):
+        origins += moved(zs, "y", s)
+    chunks = grid.reduce(chunks, "z", sends)
+    half = (n["z"] + 1) // 2
+    for s, block in enumerate(by_x, 1):
+        pieces += grid.spread(block[: half * cap], "y")
+        for r in range(1, n["y"]):
+            origins += moved(moved(zs[:half], "x", s), "y", r)
+    for r, block in enumerate(by_y, 1):
+        if half < n["z"]:
+            pieces += grid.spread(block[half * cap :], "x")
+            for s in range(1, n["x"]):
+                origins += moved(moved(zs[half:], "x", s), "y", r)
+    mine, mine_origins = list(pieces), list(origins)
+    for s in range(1, n["c"]):
+        pieces += [grid.shift(p, "c", s) for p in mine]
+        origins += moved(mine_origins, "c", s)
+
+    shifts = np.array(origins)
+    dev = jnp.zeros((len(origins),), jnp.int32)
+    for k, dim in enumerate("yczx"):
+        dev = dev * n[dim] + (me[dim] - shifts[:, k]) % n[dim]
+    ends = jnp.cumsum(pivot_counts)
+    onehot = dev[:, None] == jnp.arange(devices, dtype=jnp.int32)[None, :]
+    count = jnp.sum(jnp.where(onehot, pivot_counts[None, :], 0), axis=1)
+    start = jnp.sum(jnp.where(onehot, (ends - pivot_counts)[None, :], 0), axis=1)
+    slot = jnp.arange(cap, dtype=jnp.int32)[None, :]
+    place = jnp.where(slot < count[:, None], start[:, None] + slot, -1).reshape(1, -1)
+
+    for dim in "xy":
+        sends = [part.astype(bf16) for part in grid.sends(chunks, dim)]
+        chunks = grid.reduce(chunks, dim, sends)
+    chunks = chunks.reshape(m + extra, nt)
+    norm = chunks[m:].reshape(-1)[:m]
+    coef = (chunks[:m] / (norm + damping)[:, None]).astype(bf16)
+    coef = jnp.broadcast_to(coef[None], (devices,) + coef.shape)
+
+    place, coef = lax.optimization_barrier((place, coef))
     ps, pf, ridged = prepare(place, pieces, width)
     high, low, z = downdate(ps, pf, points, factor, targets)
     t = nt // devices
-    z_own = grid.reduce_scatter(z.reshape(grid.shape + (t, BLOCK)), "cxyz")
+    coef_held = grid.exchange(coef)
+    z, coef_held = lax.optimization_barrier((z, coef_held))
+    coef_held = coef_held.reshape(held, nt)
+    z_parts = grid.exchange(z.reshape(devices, t, BLOCK))
+    z_own = jnp.sum(z_parts, axis=0)
 
     inverse = jnp.zeros((BLOCK, BLOCK), f32)
     middle = BLOCK // TILE // 2
@@ -508,21 +506,23 @@
     nl2 = (norm_own - nh.astype(f32) - nl.astype(f32)).astype(bf16)
     late = jnp.concatenate([cross_own.astype(bf16), nh, nl, nl2], axis=0)
     late = jnp.pad(late, ((0, -late.shape[0] % 16), (0, 0)))
-    every = lax.all_to_all(
-        jnp.broadcast_to(late[None], (devices,) + late.shape), AXES, 0, 0, tiled=True
-    ).astype(f32)
+    every = grid.everywhere(late).astype(f32)
     norm_new = jnp.sum(every[:, t : t + 3], axis=(0, 1))
     coef_new = (every[:, :t].reshape(nt, BLOCK) / (norm_new + damping)[None, :]).astype(bf16)
 
-    fitted = jnp.dot(factor, coef_held, preferred_element_type=f32)
+    fitted = dot(factor, coef_held)
     fitted = fitted + dot(new_columns, coef_new, 0, 1)
     return new_columns, targets.astype(f32) - fitted
+
+
+def step(grid, *args):
+    return on_device(grid, *args)
 
 
 def solution(mesh):
     spec = P(AXES, None)
     return jax.shard_map(
-        functools.partial(on_device, Grid(mesh)),
+        functools.partial(step, Grid(mesh)),
         mesh=mesh,
         in_specs=(spec, spec, spec, spec, P()),
         out_specs=(P(None, AXES), spec),

time: 193 us -> 179 us (0.927)
  starting transfers between devices: 43.5 us -> 35.7 us
  other arithmetic: 20.7 us -> 13.6 us
  waiting for transfers between devices: 33.2 us -> 39.1 us
  local copies, waits for them, and re-layouts: 13.2 us -> 9.56 us
    ppermute x30 -> x18, starting transfers between devices: 38.9 us -> 22.5 us  [shift(): return lax.ppermute(value, AXES, list(zip(self.ids.ravel(), to.ravel())))]
    all_to_all x1 -> x3, starting transfers between devices: 4.64 us -> 13.2 us  [exchange(): return lax.all_to_all(parts, AXES, 0, 0, tiled=True)]
    dot_general x1 -> x0, matrix products: 6.11 us -> none  [on_device(): fitted = jnp.dot(factor, coef_held, preferred_element_type=f32)]
    ppermute x30 -> x18, waiting for transfers between devices: 22.7 us -> 28.6 us  [shift(): return lax.ppermute(value, AXES, list(zip(self.ids.ravel(), to.ravel())))]
    dot_general x2 -> x3, matrix products: 7.88 us -> 13 us  [dot(): lax.dot_general(a, b, (((da,), (db,)), ((), ())), precision=lax.Precision...]
    dynamic_update_slice x9 -> x0, local copies, waits for them, and re-layouts: 2.81 us -> none  [gather(): out = lax.dynamic_update_slice_in_dim(out, part, (me[dim] - s) % n, axis)]
    add x8 -> x5, other arithmetic: 2.55 us -> 0.27 us  [the longest x4 0.26 us: reduce(): total = total + self.shift(part, dim, s).astype(f32)]
    dynamic_slice x8 -> x0, local copies, waits for them, and re-layouts: 1.95 us -> none  [pick(): return lax.dynamic_index_in_dim(chunks, k, names.index(dim), keepdims=True)]
  transfers between devices with their start and end apart: 31 -> 21, of which waited for: 14 -> 9; matrix products, arithmetic and copies ran while one was open for 19% -> 9% of each run, Pallas kernels for 32% -> 29%
where the time goes in v2:
time: 179 us; the launch traced here: 178 us
  Pallas kernels  65.9 us (37%)
  waiting for transfers between devices  39.1 us (22%)
  starting transfers between devices  35.7 us (20%)
  other arithmetic  13.6 us (8%)
  matrix products  13 us (7%)
  local copies, waits for them, and re-layouts  9.56 us (5%)
    ppermute x18, waiting for transfers between devices, shift(): return lax.ppermute(value, AXES, list(zip(self.ids.ravel(), to.ravel())))  28.6 us
    pallas_call x2, Pallas kernels, factor_step(): pl.pallas_call(functools.partial(factor_kernel, first, last), out_shape=(...  27.9 us
    ppermute x18, starting transfers between devices, shift(): return lax.ppermute(value, AXES, list(zip(self.ids.ravel(), to.ravel())))  22.5 us
    pallas_call x1, Pallas kernels, downdate(): pl.pallas_call(downdate_kernel, grid=(pts // blk,), out_shape=(jax.ShapeD...  14.8 us
    all_to_all x3, starting transfers between devices, exchange(): return lax.all_to_all(parts, AXES, 0, 0, tiled=True)  13.2 us
    dot_general x3, matrix products, dot(): lax.dot_general(a, b, (((da,), (db,)), ((), ())), precision=lax.Precision...  13 us
    all_to_all x3, waiting for transfers between devices, exchange(): return lax.all_to_all(parts, AXES, 0, 0, tiled=True)  10.5 us
    pallas_call x1, Pallas kernels, make_columns(): pl.pallas_call(columns_kernel, grid=(pts // blk,), out_shape=(jax.ShapeDt...  10.2 us
  transfers between devices with their start and end apart: 21, of which 9 were waited for; matrix products, arithmetic and copies ran while one was open for 9% of the time, Pallas kernels for 29%

profile of v2, /device:TPU:0, one launch (start us, length us, event | category | flops | bytes accessed | tf_op | source)
XLA Modules:
  0.0 177.9 jit_solution(7660259983261009056)
XLA Ops:
  0.7 4.4 %shard_map.104 = bf16[32,2560]{1,0:T(8,128)(2,1)} custom-call(s32[1,32]{1,0:T(1,128)} %slots.1, bf16[2048,512]{1,0:T(8,128)(2,1)} %points.3, bf16[2048,2048]{1,0:T(8,128)(2,1)} %factor.3), custom_call_target="tpu_custom_call" | custom-call | flops 100000000 | bytes 3000000 | tf_op jit(solution)/shard_map/pallas_call | solution.py:128
  5.1 5.3 %multiply_reduce_fusion = f32[2048]{0:T(1024)S(1)} fusion(bf16[2048,2048]{1,0:T(8,128)(2,1)} %factor.3), kind=kLoop, calls=%fused_computation | loop fusion | flops 12580864 | bytes 8396800 | tf_op jit(solution)/shard_map/reduce_sum | solution.py:423
  10.4 0.5 copy-done
  10.8 2.6 %fusion.29 = f32[2048,256]{1,0:T(8,128)S(1)} fusion(bf16[2048,2048]{1,0:T(8,128)(2,1)S(1)} %copy-done, bf16[2048,256]{1,0:T(8,128)(2,1)S(1)} %copy-done.1), kind=kOutput, calls=%fused_computation.70 | convolution fusion | flops 2147483648 | bytes 11534336 | tf_op jit(solution)/shard_map/dot_general | solution.py:28
  13.5 0.1 reshape.134
  13.6 0.1 copy.34
  13.7 1.1 fusion.1
  14.8 0.5 collective-permute-start
  15.3 2.6 %collective-permute-start.1 = (bf16[32,2560]{1,0:T(8,128)(2,1)}, bf16[32,2560]{1,0:T(8,128)(2,1)}, u32[]{:S(2)}, u32[]{:S(2)}) collective-permute-start(bf16[32,2560]{1,0:T(8,128)(2,1)} %shard_map.104), channel_id=1, source_target_pairs={{0,2},{1,3},{2,4},{3,5},{4,6},{5,7},{6,0},{7,1},{8,10},{9,11},{10,... | collective-permute-start | bytes 491528 | tf_op jit(solution)/shard_map/ppermute | solution.py:65
  17.9 2.6 %collective-permute-start.2 = (bf16[32,2560]{1,0:T(8,128)(2,1)}, bf16[32,2560]{1,0:T(8,128)(2,1)}, u32[]{:S(2)}, u32[]{:S(2)}) collective-permute-start(bf16[32,2560]{1,0:T(8,128)(2,1)} %shard_map.104), channel_id=1, source_target_pairs={{0,4},{1,5},{2,6},{3,7},{4,0},{5,1},{6,2},{7,3},{8,12},{9,13},{10,... | collective-permute-start | bytes 491528 | tf_op jit(solution)/shard_map/ppermute | solution.py:65
  20.5 1.4 collective-permute-start.3
  21.8 0.7 copy.27
  22.5 0.8 reduce-window.9
  23.3 0.7 reduce
  23.9 0.7 sub.60
  24.6 0.8 collective-permute-done.1
  25.4 6.8 %collective-permute-done.2 = bf16[32,2560]{1,0:T(8,128)(2,1)} collective-permute-done((bf16[32,2560]{1,0:T(8,128)(2,1)}, bf16[32,2560]{1,0:T(8,128)(2,1)}, u32[]{:S(2)}, u32[]{:S(2)}) %collective-permute-start.2) | collective-permute-done | bytes 163872 | tf_op jit(solution)/shard_map/ppermute | solution.py:65
  32.2 2.0 %pad_maximum_fusion.refs_1_ = bf16[128,2560]{1,0:T(8,128)(2,1)} fusion(bf16[32,2560]{1,0:T(8,128)(2,1)} %collective-permute-done.3, bf16[32,2560]{1,0:T(8,128)(2,1)} %collective-permute-done.2, bf16[32,2560]{1,0:T(8,128)(2,1)} %collective-permute-done.1, bf16[32,2560]{1,0:T(8,128)(2,1)} %shard_map.104), kind=kLoop, calls=%fused_computation.11 | loop fusion | flops 2621440 | bytes 1310720 | tf_op jit(solution)/shard_map/concatenate | solution.py:439
  34.3 0.2 fusion.3
  34.5 4.1 %collective-permute-start.4 = (bf16[2,1,1,2,72,256]{5,4,3,2,1,0:T(8,128)(2,1)S(1)}, bf16[2,1,1,2,72,256]{5,4,3,2,1,0:T(8,128)(2,1)S(1)}, u32[]{:S(2)}, u32[]{:S(2)}) collective-permute-start(bf16[2,1,1,2,72,256]{5,4,3,2,1,0:T(8,128)(2,1)S(1)} %get-tuple-element.26), channel_id=1, source_target_pairs={{0,2},{1,3},{2,4},{3,5},{4,6},{5,7},{6,0},{7,1},{8,10},{9,11},{10,... | collective-permute-start | bytes 442376 | tf_op jit(solution)/shard_map/ppermute | solution.py:65
  38.6 1.6 collective-permute-start.5
  40.2 0.8 collective-permute-start.6
  41.1 1.5 collective-permute-start.9
  42.6 1.5 collective-permute-start.10
  44.1 0.3 collective-permute-done.4
  44.4 5.3 %collective-permute-done.5 = bf16[2,1,1,2,72,256]{5,4,3,2,1,0:T(8,128)(2,1)S(1)} collective-permute-done((bf16[2,1,1,2,72,256]{5,4,3,2,1,0:T(8,128)(2,1)S(1)}, bf16[2,1,1,2,72,256]{5,4,3,2,1,0:T(8,128)(2,1)S(1)}, u32[]{:S(2)}, u32[]{:S(2)}) %collective-permute-start.5) | collective-permute-done | bytes 147488 | tf_op jit(solution)/shard_map/ppermute | solution.py:65
  49.8 1.6 collective-permute-start.7
  51.4 0.2 select_reduce_fusion.1
  51.5 7.5 %collective-permute-done.7 = bf16[2,1,1,1,72,256]{5,4,3,2,1,0:T(8,128)(2,1)S(1)} collective-permute-done((bf16[2,1,1,1,72,256]{5,4,3,2,1,0:T(8,128)(2,1)S(1)}, bf16[2,1,1,1,72,256]{5,4,3,2,1,0:T(8,128)(2,1)S(1)}, u32[]{:S(2)}, u32[]{:S(2)}) %collective-permute-start.7) | collective-permute-done | bytes 73760 | tf_op jit(solution)/shard_map/ppermute | solution.py:65
  59.1 1.6 collective-permute-start.8
  60.6 0.1 add_select_fusion
  60.7 0.7 select_n.156.refs_0_
  61.4 0.6 collective-permute-start.11
  62.1 1.5 collective-permute-start.12
  63.6 0.1 collective-permute-start.14
  63.7 0.5 collective-permute-start.15
  64.2 7.5 %collective-permute-done.11.refs_4_ = bf16[64,2560]{1,0:T(8,128)(2,1)} collective-permute-done((bf16[64,2560]{1,0:T(8,128)(2,1)S(1)}, bf16[64,2560]{1,0:T(8,128)(2,1)}, u32[]{:S(2)}, u32[]{:S(2)}) %collective-permute-start.11) | collective-permute-done | bytes 327712 | tf_op jit(solution)/shard_map/ppermute | solution.py:65
  71.7 0.3 collective-permute-done.12.refs_5_
  72.1 0.2 collective-permute-start.17
  72.2 0.1 fusion.9
  72.3 1.1 broadcast_in_dim.50
  73.4 4.1 %all-to-all-start = ((bf16[32,64,256]{2,1,0:T(8,128)(2,1)}), bf16[32,64,256]{2,1,0:T(8,128)(2,1)}, u32[]{:S(2)}, u32[]{:S(2)}) async-start(bf16[32,64,256]{2,1,0:T(8,128)(2,1)} %broadcast_in_dim.50), calls=%async_computation | async-start | bytes 2097152 | tf_op jit(solution)/shard_map/all_to_all | solution.py:84
  77.7 0.8 copy-done.11
  78.4 0.2 copy-done.12
  78.7 0.9 copy-done.13
  79.5 8.5 %shard_map.105 = (bf16[512,512]{1,0:T(8,128)(2,1)}, bf16[512,2048]{1,0:T(8,128)(2,1)}, f32[512,512]{1,0:T(8,128)}) custom-call(s32[1,1024]{1,0:T(1,128)} %select_n.156.refs_0_, bf16[128,2560]{1,0:T(8,128)(2,1)} %pad_maximum_fusion.refs_1_, bf16[128,2560]{1,0:T(8,128)(2,1)} %copy-done.3, bf16[128,2560]{1,0:T(8,128)(2,1)} %copy-done.4, ...), custom_call_target="tpu_custom_call" | custom-call | flops 6000000000 | bytes 10000000 | tf_op jit(solution)/shard_map/pallas_call | solution.py:175
  88.0 14.8 %shard_map.108 = (bf16[512,2048]{1,0:T(8,128)(2,1)}, bf16[512,2048]{1,0:T(8,128)(2,1)}, f32[256,512]{1,0:T(8,128)}) custom-call(bf16[512,512]{1,0:T(8,128)(2,1)} %get-tuple-element.35.ps, bf16[512,2048]{1,0:T(8,128)(2,1)} %get-tuple-element.36.pf, bf16[2048,512]{1,0:T(8,128)(2,1)} %points.3, bf16[2048,2048]{1,0:T(8,128)(2,1)} %factor.3, ...), custom_call_target="tpu_custom_call" | custom-call | flops 6000000000 | bytes 16000000 | tf_op jit(solution)/shard_map/pallas_call | solution.py:219
  102.9 1.1 broadcast_in_dim.51.r_in
  104.0 14.6 %shard_map.106 = (f32[512,512]{1,0:T(8,128)}, f32[512,512]{1,0:T(8,128)}) custom-call(f32[512,512]{1,0:T(8,128)} %get-tuple-element.31.a_in, f32[512,512]{1,0:T(8,128)} %broadcast_in_dim.51.r_in), custom_call_target="tpu_custom_call", output_to_operand_aliasing={{0}: (0, {}), {1}: (1, {})} | custom-call | flops 12000000000 | bytes 4000000 | tf_op jit(solution)/shard_map/pallas_call | solution.py:343
  118.5 5.8 %all-to-all-start.1 = ((f32[32,8,512]{2,1,0:T(8,128)}), f32[32,8,512]{2,1,0:T(8,128)S(1)}, u32[]{:S(2)}, u32[]{:S(2)}) async-start(f32[32,8,512]{2,1,0:T(8,128)} %bitcast.3), calls=%async_computation.1 | async-start | bytes 1048576 | tf_op jit(solution)/shard_map/all_to_all | solution.py:84
  124.4 13.4 %shard_map.107 = (f32[512,512]{1,0:T(8,128)}, f32[512,512]{1,0:T(8,128)}) custom-call(f32[512,512]{1,0:T(8,128)} %get-tuple-element.32.a_in, f32[512,512]{1,0:T(8,128)} %get-tuple-element.33.r_in), custom_call_target="tpu_custom_call", output_to_operand_aliasing={{0}: (0, {}), {1}: (1, {})} | custom-call | flops 12000000000 | bytes 4000000 | tf_op jit(solution)/shard_map/pallas_call | solution.py:343
  137.7 2.7 %all-to-all-done.1 = f32[32,8,512]{2,1,0:T(8,128)S(1)} async-done(((f32[32,8,512]{2,1,0:T(8,128)}), f32[32,8,512]{2,1,0:T(8,128)S(1)}, u32[]{:S(2)}, u32[]{:S(2)}) %all-to-all-start.1) | async-done | bytes 524320 | tf_op jit(solution)/shard_map/all_to_all | solution.py:84
  140.4 0.6 reduce_sum.48.z
  141.0 10.2 %shard_map.109 = (bf16[512,2048]{1,0:T(8,128)(2,1)}, f32[8,512]{1,0:T(8,128)}, f32[1,512]{1,0:T(1,128)}) custom-call(f32[512,512]{1,0:T(8,128)} %get-tuple-element.34.inv, f32[8,512]{1,0:T(8,128)} %reduce_sum.48.z, bf16[512,2048]{1,0:T(8,128)(2,1)} %get-tuple-element.40.high, bf16[512,2048]{1,0:T(8,128)(2,1)} %get-tuple-element.41.low), custom_call_target="tpu_custom_call" | custom-call | flops 4000000000 | bytes 8000000 | tf_op jit(solution)/shard_map/pallas_call | solution.py:385
  151.2 0.8 convert_element_type.85
  152.1 0.7 fusion.28
  152.8 0.9 broadcast_in_dim.52
  153.7 3.2 %all-to-all-start.2 = ((bf16[32,16,512]{2,1,0:T(8,128)(2,1)}), bf16[32,16,512]{2,1,0:T(8,128)(2,1)S(1)}, u32[]{:S(2)}, u32[]{:S(2)}) async-start(bf16[32,16,512]{2,1,0:T(8,128)(2,1)} %broadcast_in_dim.52), calls=%async_computation.2 | async-start | bytes 1048576 | tf_op jit(solution)/shard_map/all_to_all | solution.py:84
  156.9 0.6 copy.28
  157.6 7.4 %convolution_bitcast_fusion = f32[2048,256]{0,1:T(8,128)} fusion(bf16[2048,256]{1,0:T(8,128)(2,1)} %bitcast.4, bf16[2048,2048]{1,0:T(8,128)(2,1)} %factor.3), kind=kOutput, calls=%fused_computation.5 | convolution fusion | flops 2147483648 | bytes 11534336 | tf_op jit(solution)/shard_map/dot_general | solution.py:28
  165.0 7.9 %all-to-all-done.2 = bf16[32,16,512]{2,1,0:T(8,128)(2,1)S(1)} async-done(((bf16[32,16,512]{2,1,0:T(8,128)(2,1)}), bf16[32,16,512]{2,1,0:T(8,128)(2,1)S(1)}, u32[]{:S(2)}, u32[]{:S(2)}) %all-to-all-start.2) | async-done | bytes 524320 | tf_op jit(solution)/shard_map/all_to_all | solution.py:84
  172.9 0.1 convert_element_type.91
  173.1 3.0 %fusion = f32[2048,256]{0,1:T(8,128)S(1)} fusion(f32[2048,256]{0,1:T(8,128)} %convolution_bitcast_fusion, bf16[512,2048]{1,0:T(8,128)(2,1)} %get-tuple-element.52, bf16[2048,256]{0,1:T(8,128)(2,1)S(1)} %copy.28, f32[32,16,512]{2,1,0:T(8,128)S(1)} %convert_element_type.91, f32[512]{0:T(512)S(1)} %broadcast_add_fusion), kind=kOutput, calls=%fused_computation.4 | convolution fusion | flops 538705920 | bytes 7866368 | tf_op jit(solution)/shard_map/dot_general | solution.py:28
  176.0 1.8 %copy.31 = f32[2048,256]{1,0:T(8,128)} copy(f32[2048,256]{0,1:T(8,128)S(1)} %fusion) | data formatting | bytes 4194304
  (54 shorter events, 0.5 us)
Async XLA Ops:
  0.7 9.7 %copy-start.1 = (bf16[2048,256]{1,0:T(8,128)(2,1)S(1)}, bf16[2048,256]{1,0:T(8,128)(2,1)}, u32[]{:S(2)}) copy-start(bf16[2048,256]{1,0:T(8,128)(2,1)} %targets.1) | copy-start | bytes 3145732
  5.1 5.8 %copy-start = (bf16[2048,2048]{1,0:T(8,128)(2,1)S(1)}, bf16[2048,2048]{1,0:T(8,128)(2,1)}, u32[]{:S(2)}) copy-start(bf16[2048,2048]{1,0:T(8,128)(2,1)} %factor.3) | copy-start | bytes 25165828
  13.6 8.2 %copy-start.5 = (s32[32]{0:T(128)S(1)}, s32[32]{0:T(128)}, u32[]{:S(2)}) copy-start(s32[32]{0:T(128)} %param.13) | copy-start | bytes 388
  14.8 19.4 %collective-permute-start = (f32[2,1,4,2,72,256]{5,4,3,2,1,0:T(8,128)}, f32[2,1,4,2,72,256]{5,4,3,2,1,0:T(8,128)S(1)}, u32[]{:S(2)}, u32[]{:S(2)}) collective-permute-start(f32[2,1,4,2,72,256]{5,4,3,2,1,0:T(8,128)} %fusion.1), channel_id=1, source_target_pairs={{0,8},{1,9},{2,10},{3,11},{4,12},{5,13},{6,14},{7,15},{8,0},{9,1},... | collective-permute-start | bytes 3538952 | tf_op jit(solution)/shard_map/ppermute | solution.py:65
  15.3 10.1 %collective-permute-start.1 = (bf16[32,2560]{1,0:T(8,128)(2,1)}, bf16[32,2560]{1,0:T(8,128)(2,1)}, u32[]{:S(2)}, u32[]{:S(2)}) collective-permute-start(bf16[32,2560]{1,0:T(8,128)(2,1)} %shard_map.104), channel_id=1, source_target_pairs={{0,2},{1,3},{2,4},{3,5},{4,6},{5,7},{6,0},{7,1},{8,10},{9,11},{10,... | collective-permute-start | bytes 491528 | tf_op jit(solution)/shard_map/ppermute | solution.py:65
  17.9 14.3 %collective-permute-start.2 = (bf16[32,2560]{1,0:T(8,128)(2,1)}, bf16[32,2560]{1,0:T(8,128)(2,1)}, u32[]{:S(2)}, u32[]{:S(2)}) collective-permute-start(bf16[32,2560]{1,0:T(8,128)(2,1)} %shard_map.104), channel_id=1, source_target_pairs={{0,4},{1,5},{2,6},{3,7},{4,0},{5,1},{6,2},{7,3},{8,12},{9,13},{10,... | collective-permute-start | bytes 491528 | tf_op jit(solution)/shard_map/ppermute | solution.py:65
  20.5 11.7 %collective-permute-start.3 = (bf16[32,2560]{1,0:T(8,128)(2,1)}, bf16[32,2560]{1,0:T(8,128)(2,1)}, u32[]{:S(2)}, u32[]{:S(2)}) collective-permute-start(bf16[32,2560]{1,0:T(8,128)(2,1)} %shard_map.104), channel_id=1, source_target_pairs={{0,6},{1,7},{2,0},{3,1},{4,2},{5,3},{6,4},{7,5},{8,14},{9,15},{10,... | collective-permute-start | bytes 491528 | tf_op jit(solution)/shard_map/ppermute | solution.py:65
  34.2 6.8 %copy-start.7 = (s32[32]{0:T(128)S(1)}, s32[32]{0:T(128)}, u32[]{:S(2)}) copy-start(s32[32]{0:T(128)} %constant.195) | copy-start | bytes 388
  34.2 6.8 %copy-start.8 = (s32[32]{0:T(128)S(1)}, s32[32]{0:T(128)}, u32[]{:S(2)}) copy-start(s32[32]{0:T(128)} %constant.196) | copy-start | bytes 388
  34.2 6.8 %copy-start.9 = (s32[32]{0:T(128)S(1)}, s32[32]{0:T(128)}, u32[]{:S(2)}) copy-start(s32[32]{0:T(128)} %constant.197) | copy-start | bytes 388
  34.2 6.8 %copy-start.10 = (s32[32]{0:T(128)S(1)}, s32[32]{0:T(128)}, u32[]{:S(2)}) copy-start(s32[32]{0:T(128)} %constant.198) | copy-start | bytes 388
  34.3 17.1 %copy-start.6 = (s32[32]{0:T(128)S(1)}, s32[32]{0:T(128)}, u32[]{:S(2)}) copy-start(s32[32]{0:T(128)} %param.13) | copy-start | bytes 388
  34.5 9.9 %collective-permute-start.4 = (bf16[2,1,1,2,72,256]{5,4,3,2,1,0:T(8,128)(2,1)S(1)}, bf16[2,1,1,2,72,256]{5,4,3,2,1,0:T(8,128)(2,1)S(1)}, u32[]{:S(2)}, u32[]{:S(2)}) collective-permute-start(bf16[2,1,1,2,72,256]{5,4,3,2,1,0:T(8,128)(2,1)S(1)} %get-tuple-element.26), channel_id=1, source_target_pairs={{0,2},{1,3},{2,4},{3,5},{4,6},{5,7},{6,0},{7,1},{8,10},{9,11},{10,... | collective-permute-start | bytes 442376 | tf_op jit(solution)/shard_map/ppermute | solution.py:65
  38.6 11.1 %collective-permute-start.5 = (bf16[2,1,1,2,72,256]{5,4,3,2,1,0:T(8,128)(2,1)S(1)}, bf16[2,1,1,2,72,256]{5,4,3,2,1,0:T(8,128)(2,1)S(1)}, u32[]{:S(2)}, u32[]{:S(2)}) collective-permute-start(bf16[2,1,1,2,72,256]{5,4,3,2,1,0:T(8,128)(2,1)S(1)} %get-tuple-element.27), channel_id=1, source_target_pairs={{0,4},{1,5},{2,6},{3,7},{4,0},{5,1},{6,2},{7,3},{8,12},{9,13},{10,... | collective-permute-start | bytes 442376 | tf_op jit(solution)/shard_map/ppermute | solution.py:65
  40.2 9.5 %collective-permute-start.6 = (bf16[2,1,1,2,72,256]{5,4,3,2,1,0:T(8,128)(2,1)S(1)}, bf16[2,1,1,2,72,256]{5,4,3,2,1,0:T(8,128)(2,1)S(1)}, u32[]{:S(2)}, u32[]{:S(2)}) collective-permute-start(bf16[2,1,1,2,72,256]{5,4,3,2,1,0:T(8,128)(2,1)S(1)} %get-tuple-element.28), channel_id=1, source_target_pairs={{0,6},{1,7},{2,0},{3,1},{4,2},{5,3},{6,4},{7,5},{8,14},{9,15},{10,... | collective-permute-start | bytes 442376 | tf_op jit(solution)/shard_map/ppermute | solution.py:65
  41.1 20.3 %collective-permute-start.9 = (bf16[128,2560]{1,0:T(8,128)(2,1)}, bf16[128,2560]{1,0:T(8,128)(2,1)S(1)}, u32[]{:S(2)}, u32[]{:S(2)}) collective-permute-start(bf16[128,2560]{1,0:T(8,128)(2,1)} %pad_maximum_fusion.refs_1_), channel_id=1, source_target_pairs={{0,1},{1,0},{2,3},{3,2},{4,5},{5,4},{6,7},{7,6},{8,9},{9,8},{10,11... | collective-permute-start | bytes 1966088 | tf_op jit(solution)/shard_map/ppermute | solution.py:65
  42.6 19.4 %collective-permute-start.10 = (bf16[128,2560]{1,0:T(8,128)(2,1)}, bf16[128,2560]{1,0:T(8,128)(2,1)S(1)}, u32[]{:S(2)}, u32[]{:S(2)}) collective-permute-start(bf16[128,2560]{1,0:T(8,128)(2,1)} %pad_maximum_fusion.refs_1_), channel_id=1, source_target_pairs={{0,16},{1,17},{2,18},{3,19},{4,20},{5,21},{6,22},{7,23},{8,24},{9,... | collective-permute-start | bytes 1966088 | tf_op jit(solution)/shard_map/ppermute | solution.py:65
  49.8 9.2 %collective-permute-start.7 = (bf16[2,1,1,1,72,256]{5,4,3,2,1,0:T(8,128)(2,1)S(1)}, bf16[2,1,1,1,72,256]{5,4,3,2,1,0:T(8,128)(2,1)S(1)}, u32[]{:S(2)}, u32[]{:S(2)}) collective-permute-start(bf16[2,1,1,1,72,256]{5,4,3,2,1,0:T(8,128)(2,1)S(1)} %dynamic-slice_convert_fusion.3), channel_id=1, source_target_pairs={{0,1},{1,0},{2,3},{3,2},{4,5},{5,4},{6,7},{7,6},{8,9},{9,8},{10,11... | collective-permute-start | bytes 221192 | tf_op jit(solution)/shard_map/ppermute | solution.py:65
  59.1 4.5 %collective-permute-start.8 = (bf16[1,1,1,1,72,256]{5,4,3,2,1,0:T(8,128)(2,1)S(1)}, bf16[1,1,1,1,72,256]{5,4,3,2,1,0:T(8,128)(2,1)S(1)}, u32[]{:S(2)}, u32[]{:S(2)}) collective-permute-start(bf16[1,1,1,1,72,256]{5,4,3,2,1,0:T(8,128)(2,1)S(1)} %dynamic-slice_convert_fusion.4), channel_id=1, source_target_pairs={{0,16},{1,17},{2,18},{3,19},{4,20},{5,21},{6,22},{7,23},{8,24},{9,... | collective-permute-start | bytes 110600 | tf_op jit(solution)/shard_map/ppermute | solution.py:65
  61.4 16.2 %collective-permute-start.13 = (bf16[128,2560]{1,0:T(8,128)(2,1)}, bf16[128,2560]{1,0:T(8,128)(2,1)S(1)}, u32[]{:S(2)}, u32[]{:S(2)}) collective-permute-start(bf16[128,2560]{1,0:T(8,128)(2,1)} %pad_maximum_fusion.refs_1_), channel_id=1, source_target_pairs={{0,8},{1,9},{2,10},{3,11},{4,12},{5,13},{6,14},{7,15},{8,0},{9,1},... | collective-permute-start | bytes 1966088 | tf_op jit(solution)/shard_map/ppermute | solution.py:65
  61.4 12.0 %copy-start.3 = (bf16[128,2560]{1,0:T(8,128)(2,1)}, bf16[128,2560]{1,0:T(8,128)(2,1)S(1)}, u32[]{:S(2)}) copy-start(bf16[128,2560]{1,0:T(8,128)(2,1)S(1)} %collective-permute-done.9.refs_2_) | copy-start | bytes 1966084
  61.4 10.3 %collective-permute-start.11 = (bf16[64,2560]{1,0:T(8,128)(2,1)S(1)}, bf16[64,2560]{1,0:T(8,128)(2,1)}, u32[]{:S(2)}, u32[]{:S(2)}) collective-permute-start(bf16[64,2560]{1,0:T(8,128)(2,1)S(1)} %slice.36), channel_id=1, source_target_pairs={{0,16},{1,17},{2,18},{3,19},{4,20},{5,21},{6,22},{7,23},{8,24},{9,... | collective-permute-start | bytes 983048 | tf_op jit(solution)/shard_map/ppermute | solution.py:65
  62.0 15.6 %copy-start.4 = (bf16[128,2560]{1,0:T(8,128)(2,1)}, bf16[128,2560]{1,0:T(8,128)(2,1)S(1)}, u32[]{:S(2)}) copy-start(bf16[128,2560]{1,0:T(8,128)(2,1)S(1)} %collective-permute-done.10.refs_3_) | copy-start | bytes 1966084
  62.1 10.0 %collective-permute-start.12 = (bf16[64,2560]{1,0:T(8,128)(2,1)S(1)}, bf16[64,2560]{1,0:T(8,128)(2,1)}, u32[]{:S(2)}, u32[]{:S(2)}) collective-permute-start(bf16[64,2560]{1,0:T(8,128)(2,1)S(1)} %slice.37), channel_id=1, source_target_pairs={{0,1},{1,0},{2,3},{3,2},{4,5},{5,4},{6,7},{7,6},{8,9},{9,8},{10,11... | collective-permute-start | bytes 983048 | tf_op jit(solution)/shard_map/ppermute | solution.py:65
  63.6 14.0 %collective-permute-start.14 = (bf16[128,2560]{1,0:T(8,128)(2,1)S(1)}, bf16[128,2560]{1,0:T(8,128)(2,1)S(1)}, u32[]{:S(2)}, u32[]{:S(2)}) collective-permute-start(bf16[128,2560]{1,0:T(8,128)(2,1)S(1)} %collective-permute-done.9.refs_2_), channel_id=1, source_target_pairs={{0,8},{1,9},{2,10},{3,11},{4,12},{5,13},{6,14},{7,15},{8,0},{9,1},... | collective-permute-start | bytes 1966088 | tf_op jit(solution)/shard_map/ppermute | solution.py:65
  63.7 14.0 %collective-permute-start.15 = (bf16[128,2560]{1,0:T(8,128)(2,1)S(1)}, bf16[128,2560]{1,0:T(8,128)(2,1)S(1)}, u32[]{:S(2)}, u32[]{:S(2)}) collective-permute-start(bf16[128,2560]{1,0:T(8,128)(2,1)S(1)} %collective-permute-done.10.refs_3_), channel_id=1, source_target_pairs={{0,8},{1,9},{2,10},{3,11},{4,12},{5,13},{6,14},{7,15},{8,0},{9,1},... | collective-permute-start | bytes 1966088 | tf_op jit(solution)/shard_map/ppermute | solution.py:65
  71.7 5.9 %collective-permute-start.16 = (bf16[64,2560]{1,0:T(8,128)(2,1)}, bf16[64,2560]{1,0:T(8,128)(2,1)}, u32[]{:S(2)}, u32[]{:S(2)}) collective-permute-start(bf16[64,2560]{1,0:T(8,128)(2,1)} %collective-permute-done.11.refs_4_), channel_id=1, source_target_pairs={{0,8},{1,9},{2,10},{3,11},{4,12},{5,13},{6,14},{7,15},{8,0},{9,1},... | collective-permute-start | bytes 983048 | tf_op jit(solution)/shard_map/ppermute | solution.py:65
  72.1 5.5 %collective-permute-start.17 = (bf16[64,2560]{1,0:T(8,128)(2,1)}, bf16[64,2560]{1,0:T(8,128)(2,1)}, u32[]{:S(2)}, u32[]{:S(2)}) collective-permute-start(bf16[64,2560]{1,0:T(8,128)(2,1)} %collective-permute-done.12.refs_5_), channel_id=1, source_target_pairs={{0,8},{1,9},{2,10},{3,11},{4,12},{5,13},{6,14},{7,15},{8,0},{9,1},... | collective-permute-start | bytes 983048 | tf_op jit(solution)/shard_map/ppermute | solution.py:65
  73.4 45.1 %all-to-all-start = ((bf16[32,64,256]{2,1,0:T(8,128)(2,1)}), bf16[32,64,256]{2,1,0:T(8,128)(2,1)}, u32[]{:S(2)}, u32[]{:S(2)}) async-start(bf16[32,64,256]{2,1,0:T(8,128)(2,1)} %broadcast_in_dim.50), calls=%async_computation | async-start | bytes 2097152 | tf_op jit(solution)/shard_map/all_to_all | solution.py:84
  77.6 0.9 copy-start.11
  77.6 1.0 copy-start.12
  78.7 0.9 copy-start.13
  118.5 21.8 %all-to-all-start.1 = ((f32[32,8,512]{2,1,0:T(8,128)}), f32[32,8,512]{2,1,0:T(8,128)S(1)}, u32[]{:S(2)}, u32[]{:S(2)}) async-start(f32[32,8,512]{2,1,0:T(8,128)} %bitcast.3), calls=%async_computation.1 | async-start | bytes 1048576 | tf_op jit(solution)/shard_map/all_to_all | solution.py:84
  151.2 5.7 %copy-start.2 = (bf16[2048,256]{1,0:T(8,128)(2,1)S(1)}, bf16[2048,256]{1,0:T(8,128)(2,1)}, u32[]{:S(2)}) copy-start(bf16[2048,256]{1,0:T(8,128)(2,1)} %targets.1) | copy-start | bytes 3145732
  153.7 19.2 %all-to-all-start.2 = ((bf16[32,16,512]{2,1,0:T(8,128)(2,1)}), bf16[32,16,512]{2,1,0:T(8,128)(2,1)S(1)}, u32[]{:S(2)}, u32[]{:S(2)}) async-start(bf16[32,16,512]{2,1,0:T(8,128)(2,1)} %broadcast_in_dim.52), calls=%async_computation.2 | async-start | bytes 1048576 | tf_op jit(solution)/shard_map/all_to_all | solution.py:84

commit v3 on v2

--- a/solution.py
+++ b/solution.py
@@ -142,7 +142,7 @@
 
 def prepare_kernel(count, width, *refs):
     place, pieces = refs[0], refs[1 : 1 + count]
-    scaled_ref, factor_ref, ridged_ref, rows, sems = refs[1 + count :]
+    turned_ref, ridged_ref, rows, sems = refs[1 + count :]
     copies, at = [], 0
     for k, piece in enumerate(pieces):
         n = piece.shape[0]
@@ -154,16 +154,17 @@
     pick = (slot == place[...]).astype(f32).astype(bf16)
     for copy in copies:
         copy.wait()
-    step = width
-    for lo in range(0, rows.shape[1], step):
-        part = dot(pick, rows[:, lo : lo + step]).astype(bf16)
+    inter = cosine = None
+    for lo in range(0, rows.shape[1], width):
+        part = dot(pick, rows[:, lo : lo + width]).astype(bf16)
+        turned = part.T
+        turned_ref[lo : lo + width, :] = turned
+        product = dot(part, turned)
         if lo == 0:
-            scaled_ref[...] = part
+            cosine = product / width
         else:
-            factor_ref[:, lo - width : lo - width + step] = part
-    inter = dot(factor_ref[...], factor_ref[...], 1, 1)
+            inter = product if inter is None else inter + product
     shift = ridge_shift + jnp.max(jnp.sum(jnp.abs(inter), axis=1, keepdims=True))
-    cosine = dot(scaled_ref[...], scaled_ref[...], 1, 1) / width
     r = lax.broadcasted_iota(jnp.int32, (BLOCK, BLOCK), 0)
     c = lax.broadcasted_iota(jnp.int32, (BLOCK, BLOCK), 1)
     ridged_ref[...] = jnp.exp(sharpness * (cosine - 1.0)) - inter + jnp.where(r == c, shift, 0.0)
@@ -175,12 +176,11 @@
     return pl.pallas_call(
         functools.partial(prepare_kernel, len(pieces), width),
         out_shape=(
-            jax.ShapeDtypeStruct((BLOCK, width), bf16),
-            jax.ShapeDtypeStruct((BLOCK, wide - width), bf16),
+            jax.ShapeDtypeStruct((wide, BLOCK), bf16),
             jax.ShapeDtypeStruct((BLOCK, BLOCK), f32),
         ),
         in_specs=[VMEM] + [ANY] * len(pieces),
-        out_specs=(VMEM,) * 3,
+        out_specs=(VMEM,) * 2,
         scratch_shapes=[
             pltpu.VMEM((total, wide), bf16),
             pltpu.SemaphoreType.DMA((len(pieces),)),
@@ -191,56 +191,52 @@
     )(place, *pieces)
 
 
-def downdate_kernel(ps, pf, points, factor, targets, high_ref, low_ref, z_ref, acc):
+def downdate_kernel(turned, points, factor, targets, high_ref, low_ref, z_ref):
     step = pl.program_id(0)
-    cosine = dot(ps[...], normalize(points[...]), 1, 1) / ps.shape[1]
-    down = jnp.exp(sharpness * (cosine - 1.0)) - dot(pf[...], factor[...], 1, 1)
+    width = points.shape[1]
+    cosine = dot(normalize(points[...]), turned[:width, :]) / width
+    down = jnp.exp(sharpness * (cosine - 1.0)) - dot(factor[...], turned[width:, :])
     high, low = split(down)
     high_ref[...] = high
     low_ref[...] = low
-    part = dot(high, targets[...]) + dot(low, targets[...])
+    t = targets[...].T
+    part = dot(jnp.concatenate([t, t], 1), jnp.concatenate([high, low], 0))
 
     @pl.when(step == 0)
     def _():
-        acc[...] = part
+        z_ref[...] = part
 
     @pl.when(step > 0)
     def _():
-        acc[...] += part
-
-    @pl.when(step == pl.num_programs(0) - 1)
-    def _():
-        z_ref[...] = acc[...].T
-
-
-def downdate(ps, pf, points, factor, targets):
+        z_ref[...] += part
+
+
+def downdate(turned, points, factor, targets):
     pts, width, held, nt = points.shape[0], points.shape[1], factor.shape[1], targets.shape[1]
-    blk = 256
+    blk = 512
     return pl.pallas_call(
         downdate_kernel,
         grid=(pts // blk,),
         out_shape=(
-            jax.ShapeDtypeStruct((BLOCK, pts), bf16),
-            jax.ShapeDtypeStruct((BLOCK, pts), bf16),
+            jax.ShapeDtypeStruct((pts, BLOCK), bf16),
+            jax.ShapeDtypeStruct((pts, BLOCK), bf16),
             jax.ShapeDtypeStruct((nt, BLOCK), f32),
         ),
         in_specs=[
-            pl.BlockSpec((BLOCK, width), lambda i: (0, 0)),
-            pl.BlockSpec((BLOCK, held), lambda i: (0, 0)),
+            pl.BlockSpec((width + held, BLOCK), lambda i: (0, 0)),
             pl.BlockSpec((blk, width), lambda i: (i, 0)),
             pl.BlockSpec((blk, held), lambda i: (i, 0)),
             pl.BlockSpec((blk, nt), lambda i: (i, 0)),
         ],
         out_specs=(
-            pl.BlockSpec((BLOCK, blk), lambda i: (0, i)),
-            pl.BlockSpec((BLOCK, blk), lambda i: (0, i)),
+            pl.BlockSpec((blk, BLOCK), lambda i: (i, 0)),
+            pl.BlockSpec((blk, BLOCK), lambda i: (i, 0)),
             pl.BlockSpec((nt, BLOCK), lambda i: (0, 0)),
         ),
-        scratch_shapes=[pltpu.VMEM((BLOCK, nt), f32)],
         cost_estimate=pl.CostEstimate(
             flops=6 * 10**9, bytes_accessed=16 * 10**6, transcendentals=BLOCK * pts
         ),
-    )(ps, pf, points, factor, targets)
+    )(turned, points, factor, targets)
 
 
 def across(v):
@@ -353,63 +349,61 @@
     )(a, r)
 
 
-def columns_kernel(inv, z, high, low, new_ref, cross_ref, norm_ref, acc, ih, il):
+def columns_kernel(inv, high, low, new_ref, turned_ref, norm_ref, acc, left, right):
     step = pl.program_id(0)
+    half = BLOCK // 2
 
     @pl.when(step == 0)
     def _():
-        ih[...], il[...] = split(inv[...])
-        cross_ref[...] = dot(z[...], inv[...], 1, 1, exact=True)
-
-    h = high[...]
-    new = (dot(ih[...], h) + (dot(ih[...], low[...]) + dot(il[...], h))).astype(bf16)
-    new_ref[...] = new
-    wide = new.astype(f32)
-    part = wide * wide
-
-    @pl.when(step == 0)
-    def _():
-        acc[...] = part
-
-    @pl.when(step > 0)
-    def _():
-        acc[...] += part
+        ih, il = split(inv[...].T)
+        left[...] = jnp.concatenate([ih[:half, :half], ih[:half, :half], il[:half, :half]], 0)
+        right[...] = jnp.concatenate([ih[:, half:], ih[:, half:], il[:, half:]], 0)
+        acc[...] = jnp.zeros_like(acc)
+
+    h, l = high[...], low[...]
+    for lo, weights in ((0, left), (half, right)):
+        k = lo + half
+        rows = jnp.concatenate([h[:, :k], l[:, :k], h[:, :k]], 1)
+        new = dot(rows, weights[...]).astype(bf16)
+        turned_ref[:, lo:k] = new
+        new_ref[lo:k, :] = new.T
+        wide = new.astype(f32)
+        acc[:, lo:k] += jnp.sum((wide * wide).reshape(-1, 8, half), axis=0)
 
     @pl.when(step == pl.num_programs(0) - 1)
     def _():
-        norm_ref[...] = jnp.sum(acc[...].T, axis=0, keepdims=True)
-
-
-def make_columns(inv, z, high, low):
-    pts, blk = high.shape[1], 256
+        norm_ref[...] = jnp.sum(acc[...], axis=0, keepdims=True)
+
+
+def make_columns(inv, high, low):
+    pts, blk = high.shape[0], 512
     return pl.pallas_call(
         columns_kernel,
         grid=(pts // blk,),
         out_shape=(
             jax.ShapeDtypeStruct((BLOCK, pts), bf16),
-            jax.ShapeDtypeStruct(z.shape, f32),
+            jax.ShapeDtypeStruct((pts, BLOCK), bf16),
             jax.ShapeDtypeStruct((1, BLOCK), f32),
         ),
         in_specs=[
             pl.BlockSpec((BLOCK, BLOCK), lambda i: (0, 0)),
-            pl.BlockSpec(z.shape, lambda i: (0, 0)),
-            pl.BlockSpec((BLOCK, blk), lambda i: (0, i)),
-            pl.BlockSpec((BLOCK, blk), lambda i: (0, i)),
+            pl.BlockSpec((blk, BLOCK), lambda i: (i, 0)),
+            pl.BlockSpec((blk, BLOCK), lambda i: (i, 0)),
         ],
         out_specs=(
             pl.BlockSpec((BLOCK, blk), lambda i: (0, i)),
-            pl.BlockSpec(z.shape, lambda i: (0, 0)),
+            pl.BlockSpec((blk, BLOCK), lambda i: (i, 0)),
             pl.BlockSpec((1, BLOCK), lambda i: (0, 0)),
         ),
         scratch_shapes=[
-            pltpu.VMEM((BLOCK, blk), f32),
-            pltpu.VMEM((BLOCK, BLOCK), bf16),
-            pltpu.VMEM((BLOCK, BLOCK), bf16),
+            pltpu.VMEM((8, BLOCK), f32),
+            pltpu.VMEM((3 * BLOCK // 2, BLOCK // 2), bf16),
+            pltpu.VMEM((3 * BLOCK, BLOCK // 2), bf16),
         ],
         cost_estimate=pl.CostEstimate(
             flops=4 * 10**9, bytes_accessed=8 * 10**6, transcendentals=0
         ),
-    )(inv, z, high, low)
+    )(inv, high, low)
 
 
 def on_device(grid, points, factor, targets, pivot_slots, pivot_counts):
@@ -433,11 +427,9 @@
         axis=1,
     )
     chunks = grid.reduce(chunks.reshape(grid.shape + chunks.shape[1:]), "c")
-    sends = [part.astype(bf16) for part in grid.sends(chunks, "z")]
 
     arrived = grid.spread(own, "z")
     along_z = jnp.concatenate([own] + arrived, 0)
-    along_z, sends = lax.optimization_barrier((along_z, sends))
     zs = [(0, 0, s, 0) for s in range(n["z"])]
 
     def moved(origin, dim, s):
@@ -451,7 +443,9 @@
         origins += moved(zs, "x", s)
     for s in range(1, n["y"]):
         origins += moved(zs, "y", s)
-    chunks = grid.reduce(chunks, "z", sends)
+    for dim in "zxy":
+        sends = [part.astype(bf16) for part in grid.sends(chunks, dim)]
+        chunks = grid.reduce(chunks, dim, sends)
     half = (n["z"] + 1) // 2
     for s, block in enumerate(by_x, 1):
         pieces += grid.spread(block[: half * cap], "y")
@@ -478,21 +472,18 @@
     slot = jnp.arange(cap, dtype=jnp.int32)[None, :]
     place = jnp.where(slot < count[:, None], start[:, None] + slot, -1).reshape(1, -1)
 
-    for dim in "xy":
-        sends = [part.astype(bf16) for part in grid.sends(chunks, dim)]
-        chunks = grid.reduce(chunks, dim, sends)
     chunks = chunks.reshape(m + extra, nt)
     norm = chunks[m:].reshape(-1)[:m]
     coef = (chunks[:m] / (norm + damping)[:, None]).astype(bf16)
     coef = jnp.broadcast_to(coef[None], (devices,) + coef.shape)
 
-    place, coef = lax.optimization_barrier((place, coef))
-    ps, pf, ridged = prepare(place, pieces, width)
-    high, low, z = downdate(ps, pf, points, factor, targets)
-    t = nt // devices
     coef_held = grid.exchange(coef)
+
+    turned, ridged = prepare(place, pieces, width)
+    high, low, z = downdate(turned, points, factor, targets)
     z, coef_held = lax.optimization_barrier((z, coef_held))
     coef_held = coef_held.reshape(held, nt)
+    t = nt // devices
     z_parts = grid.exchange(z.reshape(devices, t, BLOCK))
     z_own = jnp.sum(z_parts, axis=0)
 
@@ -501,7 +492,8 @@
     ridged, inverse = factor_step(ridged, inverse, 0, middle)
     ridged, inverse = factor_step(ridged, inverse, middle, BLOCK // TILE)
 
-    new_columns, cross_own, norm_own = make_columns(inverse, z_own, high, low)
+    new_columns, new_turned, norm_own = make_columns(inverse, high, low)
+    cross_own = dot(z_own, inverse, 1, 1, exact=True)
     nh, nl = split(norm_own)
     nl2 = (norm_own - nh.astype(f32) - nl.astype(f32)).astype(bf16)
     late = jnp.concatenate([cross_own.astype(bf16), nh, nl, nl2], axis=0)
@@ -511,8 +503,7 @@
     coef_new = (every[:, :t].reshape(nt, BLOCK) / (norm_new + damping)[None, :]).astype(bf16)
 
     fitted = dot(factor, coef_held)
-    fitted = fitted + dot(new_columns, coef_new, 0, 1)
-    return new_columns, targets.astype(f32) - fitted
+    return new_columns, (targets.astype(f32) - fitted) - dot(new_turned, coef_new, 1, 1)
 
 
 def step(grid, *args):

time: 179 us -> 162 us (0.905)
  waiting for transfers between devices: 39.1 us -> 23.9 us
  local copies, waits for them, and re-layouts: 9.56 us -> 16 us
  Pallas kernels: 65.9 us -> 61.7 us
  other arithmetic: 13.6 us -> 10.2 us
    ppermute x18, waiting for transfers between devices: 28.6 us -> 16.7 us  [shift(): return lax.ppermute(value, AXES, list(zip(self.ids.ravel(), to.ravel())))]
    unnamed x33 -> x42, local copies, waits for them, and re-layouts: 4.92 us -> 9.68 us
    ppermute x18, starting transfers between devices: 22.5 us -> 18.4 us  [shift(): return lax.ppermute(value, AXES, list(zip(self.ids.ravel(), to.ravel())))]
    all_to_all x3, waiting for transfers between devices: 10.5 us -> 7.17 us  [exchange(): return lax.all_to_all(parts, AXES, 0, 0, tiled=True)]
    pallas_call x1, Pallas kernels: 10.2 us -> 7.16 us  [make_columns(): pl.pallas_call(columns_kernel, grid=(pts // blk,), out_shape=(jax.ShapeDt...]
    all_to_all x3, starting transfers between devices: 13.2 us -> 16 us  [exchange(): return lax.all_to_all(parts, AXES, 0, 0, tiled=True)]
    pallas_call x1, Pallas kernels: 14.8 us -> 12.7 us  [downdate(): pl.pallas_call(downdate_kernel, grid=(pts // blk,), out_shape=(jax.ShapeD...]
    concatenate x1 -> x0, other arithmetic: 2.04 us -> none  [on_device(): along_z = jnp.concatenate([own] + arrived, 0)]
  transfers between devices with their start and end apart: 21 -> 21, of which waited for: 9 -> 6; matrix products, arithmetic and copies ran while one was open for 9% -> 20% of each run, Pallas kernels for 29% -> 36%
where the time goes in v3:
time: 162 us; the launch traced here: 161 us
  Pallas kernels  61.7 us (38%)
  starting transfers between devices  34.3 us (21%)
  waiting for transfers between devices  23.9 us (15%)
  local copies, waits for them, and re-layouts  16 us (10%)
  matrix products  13.9 us (9%)
  other arithmetic  10.2 us (6%)
    pallas_call x2, Pallas kernels, factor_step(): pl.pallas_call(functools.partial(factor_kernel, first, last), out_shape=(...  28 us
    ppermute x18, starting transfers between devices, shift(): return lax.ppermute(value, AXES, list(zip(self.ids.ravel(), to.ravel())))  18.4 us
    ppermute x18, waiting for transfers between devices, shift(): return lax.ppermute(value, AXES, list(zip(self.ids.ravel(), to.ravel())))  16.7 us
    all_to_all x3, starting transfers between devices, exchange(): return lax.all_to_all(parts, AXES, 0, 0, tiled=True)  16 us
    dot_general x4, matrix products, dot(): lax.dot_general(a, b, (((da,), (db,)), ((), ())), precision=lax.Precision...  13.9 us
    pallas_call x1, Pallas kernels, downdate(): pl.pallas_call(downdate_kernel, grid=(pts // blk,), out_shape=(jax.ShapeD...  12.7 us
    unnamed x42, local copies, waits for them, and re-layouts  9.68 us
    pallas_call x1, Pallas kernels, prepare(): pl.pallas_call(functools.partial(prepare_kernel, len(pieces), width), out...  9.54 us
  transfers between devices with their start and end apart: 21, of which 6 were waited for; matrix products, arithmetic and copies ran while one was open for 20% of the time, Pallas kernels for 36%

profile of v3, /device:TPU:0, one launch (start us, length us, event | category | flops | bytes accessed | tf_op | source)
XLA Modules:
  0.0 161.0 jit_solution(18405816453053307347)
XLA Ops:
  0.6 0.0 copy-start.2
  0.6 4.4 %shard_map.104 = bf16[32,2560]{1,0:T(8,128)(2,1)} custom-call(s32[1,32]{1,0:T(1,128)} %slots.1, bf16[2048,512]{1,0:T(8,128)(2,1)} %points.3, bf16[2048,2048]{1,0:T(8,128)(2,1)} %factor.3), custom_call_target="tpu_custom_call" | custom-call | flops 100000000 | bytes 3000000 | tf_op jit(solution)/shard_map/pallas_call | solution.py:128
  5.0 3.1 %collective-permute-start = (bf16[32,2560]{1,0:T(8,128)(2,1)}, bf16[32,2560]{1,0:T(8,128)(2,1)}, u32[]{:S(2)}, u32[]{:S(2)}) collective-permute-start(bf16[32,2560]{1,0:T(8,128)(2,1)} %shard_map.104), channel_id=1, source_target_pairs={{0,2},{1,3},{2,4},{3,5},{4,6},{5,7},{6,0},{7,1},{8,10},{9,11},{10,... | collective-permute-start | bytes 491528 | tf_op jit(solution)/shard_map/ppermute | solution.py:65
  8.1 2.6 %collective-permute-start.1 = (bf16[32,2560]{1,0:T(8,128)(2,1)}, bf16[32,2560]{1,0:T(8,128)(2,1)}, u32[]{:S(2)}, u32[]{:S(2)}) collective-permute-start(bf16[32,2560]{1,0:T(8,128)(2,1)} %shard_map.104), channel_id=1, source_target_pairs={{0,4},{1,5},{2,6},{3,7},{4,0},{5,1},{6,2},{7,3},{8,12},{9,13},{10,... | collective-permute-start | bytes 491528 | tf_op jit(solution)/shard_map/ppermute | solution.py:65
  10.7 1.3 collective-permute-start.2
  12.1 5.3 %multiply_reduce_fusion = f32[2048]{0:T(1024)S(1)} fusion(bf16[2048,2048]{1,0:T(8,128)(2,1)} %factor.3), kind=kLoop, calls=%fused_computation | loop fusion | flops 12580864 | bytes 8396800 | tf_op jit(solution)/shard_map/reduce_sum | solution.py:417
  17.4 0.5 copy-done
  17.8 2.6 %fusion.29 = f32[2048,256]{1,0:T(8,128)S(1)} fusion(bf16[2048,2048]{1,0:T(8,128)(2,1)S(1)} %copy-done, bf16[2048,256]{1,0:T(8,128)(2,1)S(1)} %copy-done.2), kind=kOutput, calls=%fused_computation.74 | convolution fusion | flops 2147483648 | bytes 11534336 | tf_op jit(solution)/shard_map/dot_general | solution.py:28
  20.5 0.1 reshape.134
  20.6 0.1 copy.34
  20.7 1.1 fusion.1
  21.8 1.6 constant_dynamic-update-slice_fusion.3
  23.4 0.7 copy.27
  24.1 0.8 reduce-window.9
  24.9 0.7 reduce
  25.6 0.7 sub.63
  26.2 1.6 constant_dynamic-update-slice_fusion.2
  27.8 1.6 constant_dynamic-update-slice_fusion.1
  29.4 1.6 constant_dynamic-update-slice_fusion.refs_1_
  31.0 1.6 collective-permute-start.3
  32.6 1.5 collective-permute-start.4
  34.1 0.2 fusion.3
  34.3 0.1 dynamic-slice_convert_fusion.2
  34.4 0.7 collective-permute-start.13
  35.1 0.3 collective-permute-start.14
  35.4 2.8 %collective-permute-start.15 = (bf16[2,1,1,2,72,256]{5,4,3,2,1,0:T(8,128)(2,1)S(1)}, bf16[2,1,1,2,72,256]{5,4,3,2,1,0:T(8,128)(2,1)S(1)}, u32[]{:S(2)}, u32[]{:S(2)}) collective-permute-start(bf16[2,1,1,2,72,256]{5,4,3,2,1,0:T(8,128)(2,1)S(1)} %get-tuple-element.43), channel_id=1, source_target_pairs={{0,6},{1,7},{2,0},{3,1},{4,2},{5,3},{6,4},{7,5},{8,14},{9,15},{10,... | collective-permute-start | bytes 442376 | tf_op jit(solution)/shard_map/ppermute | solution.py:65
  38.3 4.8 %collective-permute-done.13 = bf16[2,1,1,2,72,256]{5,4,3,2,1,0:T(8,128)(2,1)S(1)} collective-permute-done((bf16[2,1,1,2,72,256]{5,4,3,2,1,0:T(8,128)(2,1)S(1)}, bf16[2,1,1,2,72,256]{5,4,3,2,1,0:T(8,128)(2,1)S(1)}, u32[]{:S(2)}, u32[]{:S(2)}) %collective-permute-start.13) | collective-permute-done | bytes 147488 | tf_op jit(solution)/shard_map/ppermute | solution.py:65
  43.0 5.3 %collective-permute-done.14 = bf16[2,1,1,2,72,256]{5,4,3,2,1,0:T(8,128)(2,1)S(1)} collective-permute-done((bf16[2,1,1,2,72,256]{5,4,3,2,1,0:T(8,128)(2,1)S(1)}, bf16[2,1,1,2,72,256]{5,4,3,2,1,0:T(8,128)(2,1)S(1)}, u32[]{:S(2)}, u32[]{:S(2)}) %collective-permute-start.14) | collective-permute-done | bytes 147488 | tf_op jit(solution)/shard_map/ppermute | solution.py:65
  48.4 0.1 convert_add_fusion
  48.5 0.6 collective-permute-start.16
  49.1 0.2 select_reduce_fusion.1
  49.3 0.7 collective-permute-start.5
  50.1 1.9 %collective-permute-start.6 = (bf16[64,2560]{1,0:T(8,128)(2,1)S(1)}, bf16[64,2560]{1,0:T(8,128)(2,1)}, u32[]{:S(2)}, u32[]{:S(2)}) collective-permute-start(bf16[64,2560]{1,0:T(8,128)(2,1)S(1)} %slice.34), channel_id=1, source_target_pairs={{0,1},{1,0},{2,3},{3,2},{4,5},{5,4},{6,7},{7,6},{8,9},{9,8},{10,11... | collective-permute-start | bytes 983048 | tf_op jit(solution)/shard_map/ppermute | solution.py:65
  52.0 1.7 %collective-permute-done.16 = bf16[2,1,1,1,72,256]{5,4,3,2,1,0:T(8,128)(2,1)S(1)} collective-permute-done((bf16[2,1,1,1,72,256]{5,4,3,2,1,0:T(8,128)(2,1)S(1)}, bf16[2,1,1,1,72,256]{5,4,3,2,1,0:T(8,128)(2,1)S(1)}, u32[]{:S(2)}, u32[]{:S(2)}) %collective-permute-start.16) | collective-permute-done | bytes 73760 | tf_op jit(solution)/shard_map/ppermute | solution.py:65
  53.8 0.1 collective-permute-start.17
  53.8 0.1 add_select_fusion
  53.9 0.7 select_n.156.refs_0_
  54.6 0.5 collective-permute-start.8
  55.1 3.2 %collective-permute-done.5.refs_4_ = bf16[64,2560]{1,0:T(8,128)(2,1)} collective-permute-done((bf16[64,2560]{1,0:T(8,128)(2,1)S(1)}, bf16[64,2560]{1,0:T(8,128)(2,1)}, u32[]{:S(2)}, u32[]{:S(2)}) %collective-permute-start.5) | collective-permute-done | bytes 327712 | tf_op jit(solution)/shard_map/ppermute | solution.py:65
  58.3 1.7 %collective-permute-done.6.refs_5_ = bf16[64,2560]{1,0:T(8,128)(2,1)} collective-permute-done((bf16[64,2560]{1,0:T(8,128)(2,1)S(1)}, bf16[64,2560]{1,0:T(8,128)(2,1)}, u32[]{:S(2)}, u32[]{:S(2)}) %collective-permute-start.6) | collective-permute-done | bytes 327712 | tf_op jit(solution)/shard_map/ppermute | solution.py:65
  60.0 0.5 collective-permute-start.11
  60.6 0.1 fusion.9
  60.7 1.1 broadcast_in_dim.51
  61.8 4.2 %all-to-all-start = ((bf16[32,64,256]{2,1,0:T(8,128)(2,1)}), bf16[32,64,256]{2,1,0:T(8,128)(2,1)S(1)}, u32[]{:S(2)}, u32[]{:S(2)}) async-start(bf16[32,64,256]{2,1,0:T(8,128)(2,1)} %broadcast_in_dim.51), calls=%async_computation | async-start | bytes 2097152 | tf_op jit(solution)/shard_map/all_to_all | solution.py:84
  66.1 0.8 copy-done.15
  66.9 0.2 copy-done.16
  67.1 9.5 %shard_map.105 = (bf16[2560,512]{1,0:T(8,128)(2,1)}, f32[512,512]{1,0:T(8,128)}) custom-call(s32[1,1024]{1,0:T(1,128)} %select_n.156.refs_0_, bf16[128,2560]{1,0:T(8,128)(2,1)} %constant_dynamic-update-slice_fusion.refs_1_, bf16[128,2560]{1,0:T(8,128)(2,1)} %copy-done.6, bf16[128,2560]{1,0:T(8,128)(2,1)} %copy-done.7, ...), custom_call_target="tpu_custom_call" | custom-call | flops 6000000000 | bytes 10000000 | tf_op jit(solution)/shard_map/pallas_call | solution.py:176
  76.6 12.7 %shard_map.108 = (bf16[2048,512]{1,0:T(8,128)(2,1)}, bf16[2048,512]{1,0:T(8,128)(2,1)}, f32[256,512]{1,0:T(8,128)}) custom-call(bf16[2560,512]{1,0:T(8,128)(2,1)} %get-tuple-element.22.turned, bf16[2048,512]{1,0:T(8,128)(2,1)} %points.3, bf16[2048,2048]{1,0:T(8,128)(2,1)} %factor.3, bf16[2048,256]{1,0:T(8,128)(2,1)} %targets.1), custom_call_target="tpu_custom_call" | custom-call | flops 6000000000 | bytes 16000000 | tf_op jit(solution)/shard_map/pallas_call | solution.py:217
  89.3 1.1 broadcast_in_dim.50.r_in
  90.4 14.6 %shard_map.106 = (f32[512,512]{1,0:T(8,128)}, f32[512,512]{1,0:T(8,128)}) custom-call(f32[512,512]{1,0:T(8,128)} %get-tuple-element.18.a_in, f32[512,512]{1,0:T(8,128)} %broadcast_in_dim.50.r_in), custom_call_target="tpu_custom_call", output_to_operand_aliasing={{0}: (0, {}), {1}: (1, {})} | custom-call | flops 12000000000 | bytes 4000000 | tf_op jit(solution)/shard_map/pallas_call | solution.py:339
  105.1 5.9 %all-to-all-start.1 = ((f32[32,8,512]{2,1,0:T(8,128)}), f32[32,8,512]{2,1,0:T(8,128)S(1)}, u32[]{:S(2)}, u32[]{:S(2)}) async-start(f32[32,8,512]{2,1,0:T(8,128)} %bitcast.5), calls=%async_computation.1 | async-start | bytes 1048576 | tf_op jit(solution)/shard_map/all_to_all | solution.py:84
  111.0 13.4 %shard_map.107 = (f32[512,512]{1,0:T(8,128)}, f32[512,512]{1,0:T(8,128)}) custom-call(f32[512,512]{1,0:T(8,128)} %get-tuple-element.19.a_in, f32[512,512]{1,0:T(8,128)} %get-tuple-element.20.r_in), custom_call_target="tpu_custom_call", output_to_operand_aliasing={{0}: (0, {}), {1}: (1, {})} | custom-call | flops 12000000000 | bytes 4000000 | tf_op jit(solution)/shard_map/pallas_call | solution.py:339
  124.4 7.2 %shard_map.109 = (bf16[512,2048]{1,0:T(8,128)(2,1)}, bf16[2048,512]{1,0:T(8,128)(2,1)}, f32[1,512]{1,0:T(1,128)}) custom-call(f32[512,512]{1,0:T(8,128)} %get-tuple-element.21.inv, bf16[2048,512]{1,0:T(8,128)(2,1)} %get-tuple-element.23.high, bf16[2048,512]{1,0:T(8,128)(2,1)} %get-tuple-element.24.low), custom_call_target="tpu_custom_call" | custom-call | flops 4000000000 | bytes 8000000 | tf_op jit(solution)/shard_map/pallas_call | solution.py:380
  131.5 0.8 fusion.28
  132.4 1.0 convolution_convert_fusion
  133.4 0.9 broadcast_in_dim.52
  134.2 5.9 %all-to-all-start.2 = ((bf16[32,16,512]{2,1,0:T(8,128)(2,1)}), bf16[32,16,512]{2,1,0:T(8,128)(2,1)S(1)}, u32[]{:S(2)}, u32[]{:S(2)}) async-start(bf16[32,16,512]{2,1,0:T(8,128)(2,1)} %broadcast_in_dim.52), calls=%async_computation.2 | async-start | bytes 1048576 | tf_op jit(solution)/shard_map/all_to_all | solution.py:84
  140.1 1.4 copy.28
  141.6 7.3 %fusion = f32[2048,256]{0,1:T(8,128)} fusion(bf16[2048,256]{1,0:T(8,128)(2,1)S(1)} %bitcast.38, bf16[2048,2048]{1,0:T(8,128)(2,1)} %factor.3, bf16[2048,256]{0,1:T(8,128)(2,1)} %copy.28), kind=kOutput, calls=%fused_computation.5 | convolution fusion | flops 2148532224 | bytes 12582912 | tf_op jit(solution)/shard_map/dot_general | solution.py:28
  148.9 7.2 %all-to-all-done.2 = bf16[32,16,512]{2,1,0:T(8,128)(2,1)S(1)} async-done(((bf16[32,16,512]{2,1,0:T(8,128)(2,1)}), bf16[32,16,512]{2,1,0:T(8,128)(2,1)S(1)}, u32[]{:S(2)}, u32[]{:S(2)}) %all-to-all-start.2) | async-done | bytes 524320 | tf_op jit(solution)/shard_map/all_to_all | solution.py:84
  156.1 0.1 convert_element_type.91
  156.2 0.1 slice_reduce_fusion
  156.2 3.0 %convolution_subtract_fusion = f32[2048,256]{0,1:T(8,128)S(1)} fusion(f32[2048,256]{0,1:T(8,128)} %fusion, bf16[2048,512]{1,0:T(8,128)(2,1)} %get-tuple-element.29, f32[32,16,512]{2,1,0:T(8,128)S(1)} %convert_element_type.91, f32[512]{0:T(512)S(1)} %broadcast_add_fusion), kind=kOutput, calls=%fused_computation.3 | convolution fusion | flops 537657344 | bytes 6817792 | tf_op jit(solution)/shard_map/dot_general | solution.py:28
  159.2 1.8 %copy.31 = f32[2048,256]{1,0:T(8,128)} copy(f32[2048,256]{0,1:T(8,128)S(1)} %convolution_subtract_fusion) | data formatting | bytes 4194304
  (63 shorter events, 0.4 us)
Async XLA Ops:
  0.6 16.7 %copy-start.2 = (bf16[2048,256]{1,0:T(8,128)(2,1)S(1)}, bf16[2048,256]{1,0:T(8,128)(2,1)}, u32[]{:S(2)}) copy-start(bf16[2048,256]{1,0:T(8,128)(2,1)} %targets.1) | copy-start | bytes 3145732
  5.0 21.2 %collective-permute-start = (bf16[32,2560]{1,0:T(8,128)(2,1)}, bf16[32,2560]{1,0:T(8,128)(2,1)}, u32[]{:S(2)}, u32[]{:S(2)}) collective-permute-start(bf16[32,2560]{1,0:T(8,128)(2,1)} %shard_map.104), channel_id=1, source_target_pairs={{0,2},{1,3},{2,4},{3,5},{4,6},{5,7},{6,0},{7,1},{8,10},{9,11},{10,... | collective-permute-start | bytes 491528 | tf_op jit(solution)/shard_map/ppermute | solution.py:65
  8.1 19.7 %collective-permute-start.1 = (bf16[32,2560]{1,0:T(8,128)(2,1)}, bf16[32,2560]{1,0:T(8,128)(2,1)}, u32[]{:S(2)}, u32[]{:S(2)}) collective-permute-start(bf16[32,2560]{1,0:T(8,128)(2,1)} %shard_map.104), channel_id=1, source_target_pairs={{0,4},{1,5},{2,6},{3,7},{4,0},{5,1},{6,2},{7,3},{8,12},{9,13},{10,... | collective-permute-start | bytes 491528 | tf_op jit(solution)/shard_map/ppermute | solution.py:65
  10.7 18.7 %collective-permute-start.2 = (bf16[32,2560]{1,0:T(8,128)(2,1)}, bf16[32,2560]{1,0:T(8,128)(2,1)}, u32[]{:S(2)}, u32[]{:S(2)}) collective-permute-start(bf16[32,2560]{1,0:T(8,128)(2,1)} %shard_map.104), channel_id=1, source_target_pairs={{0,6},{1,7},{2,0},{3,1},{4,2},{5,3},{6,4},{7,5},{8,14},{9,15},{10,... | collective-permute-start | bytes 491528 | tf_op jit(solution)/shard_map/ppermute | solution.py:65
  12.1 5.8 %copy-start = (bf16[2048,2048]{1,0:T(8,128)(2,1)S(1)}, bf16[2048,2048]{1,0:T(8,128)(2,1)}, u32[]{:S(2)}) copy-start(bf16[2048,2048]{1,0:T(8,128)(2,1)} %factor.3) | copy-start | bytes 25165828
  20.7 2.8 %copy-start.9 = (s32[32]{0:T(128)S(1)}, s32[32]{0:T(128)}, u32[]{:S(2)}) copy-start(s32[32]{0:T(128)} %param.13) | copy-start | bytes 388
  21.8 12.3 %collective-permute-start.12 = (f32[2,1,4,2,72,256]{5,4,3,2,1,0:T(8,128)}, f32[2,1,4,2,72,256]{5,4,3,2,1,0:T(8,128)S(1)}, u32[]{:S(2)}, u32[]{:S(2)}) collective-permute-start(f32[2,1,4,2,72,256]{5,4,3,2,1,0:T(8,128)} %fusion.1), channel_id=1, source_target_pairs={{0,8},{1,9},{2,10},{3,11},{4,12},{5,13},{6,14},{7,15},{8,0},{9,1},... | collective-permute-start | bytes 3538952 | tf_op jit(solution)/shard_map/ppermute | solution.py:65
  31.0 7.2 %copy-start.11 = (s32[32]{0:T(128)S(1)}, s32[32]{0:T(128)}, u32[]{:S(2)}) copy-start(s32[32]{0:T(128)} %constant.195) | copy-start | bytes 388
  31.0 7.2 %copy-start.12 = (s32[32]{0:T(128)S(1)}, s32[32]{0:T(128)}, u32[]{:S(2)}) copy-start(s32[32]{0:T(128)} %constant.196) | copy-start | bytes 388
  31.0 7.2 %copy-start.13 = (s32[32]{0:T(128)S(1)}, s32[32]{0:T(128)}, u32[]{:S(2)}) copy-start(s32[32]{0:T(128)} %constant.197) | copy-start | bytes 388
  31.0 7.2 %copy-start.14 = (s32[32]{0:T(128)S(1)}, s32[32]{0:T(128)}, u32[]{:S(2)}) copy-start(s32[32]{0:T(128)} %constant.198) | copy-start | bytes 388
  31.0 18.1 %copy-start.10 = (s32[32]{0:T(128)S(1)}, s32[32]{0:T(128)}, u32[]{:S(2)}) copy-start(s32[32]{0:T(128)} %param.13) | copy-start | bytes 388
  31.0 18.2 %collective-permute-start.3 = (bf16[128,2560]{1,0:T(8,128)(2,1)}, bf16[128,2560]{1,0:T(8,128)(2,1)S(1)}, u32[]{:S(2)}, u32[]{:S(2)}) collective-permute-start(bf16[128,2560]{1,0:T(8,128)(2,1)} %constant_dynamic-update-slice_fusion.refs_1_), channel_id=1, source_target_pairs={{0,1},{1,0},{2,3},{3,2},{4,5},{5,4},{6,7},{7,6},{8,9},{9,8},{10,11... | collective-permute-start | bytes 1966088 | tf_op jit(solution)/shard_map/ppermute | solution.py:65
  32.6 17.5 %collective-permute-start.4 = (bf16[128,2560]{1,0:T(8,128)(2,1)}, bf16[128,2560]{1,0:T(8,128)(2,1)S(1)}, u32[]{:S(2)}, u32[]{:S(2)}) collective-permute-start(bf16[128,2560]{1,0:T(8,128)(2,1)} %constant_dynamic-update-slice_fusion.refs_1_), channel_id=1, source_target_pairs={{0,16},{1,17},{2,18},{3,19},{4,20},{5,21},{6,22},{7,23},{8,24},{9,... | collective-permute-start | bytes 1966088 | tf_op jit(solution)/shard_map/ppermute | solution.py:65
  34.3 20.3 %copy-start.8 = (bf16[128,2560]{1,0:T(8,128)(2,1)S(1)}, bf16[128,2560]{1,0:T(8,128)(2,1)}, u32[]{:S(2)}) copy-start(bf16[128,2560]{1,0:T(8,128)(2,1)} %constant_dynamic-update-slice_fusion.refs_1_) | copy-start | bytes 1966084
  34.4 8.7 %collective-permute-start.13 = (bf16[2,1,1,2,72,256]{5,4,3,2,1,0:T(8,128)(2,1)S(1)}, bf16[2,1,1,2,72,256]{5,4,3,2,1,0:T(8,128)(2,1)S(1)}, u32[]{:S(2)}, u32[]{:S(2)}) collective-permute-start(bf16[2,1,1,2,72,256]{5,4,3,2,1,0:T(8,128)(2,1)S(1)} %get-tuple-element.42), channel_id=1, source_target_pairs={{0,2},{1,3},{2,4},{3,5},{4,6},{5,7},{6,0},{7,1},{8,10},{9,11},{10,... | collective-permute-start | bytes 442376 | tf_op jit(solution)/shard_map/ppermute | solution.py:65
  35.1 13.3 %collective-permute-start.14 = (bf16[2,1,1,2,72,256]{5,4,3,2,1,0:T(8,128)(2,1)S(1)}, bf16[2,1,1,2,72,256]{5,4,3,2,1,0:T(8,128)(2,1)S(1)}, u32[]{:S(2)}, u32[]{:S(2)}) collective-permute-start(bf16[2,1,1,2,72,256]{5,4,3,2,1,0:T(8,128)(2,1)S(1)} %get-tuple-element.44), channel_id=1, source_target_pairs={{0,4},{1,5},{2,6},{3,7},{4,0},{5,1},{6,2},{7,3},{8,12},{9,13},{10,... | collective-permute-start | bytes 442376 | tf_op jit(solution)/shard_map/ppermute | solution.py:65
  35.4 12.9 %collective-permute-start.15 = (bf16[2,1,1,2,72,256]{5,4,3,2,1,0:T(8,128)(2,1)S(1)}, bf16[2,1,1,2,72,256]{5,4,3,2,1,0:T(8,128)(2,1)S(1)}, u32[]{:S(2)}, u32[]{:S(2)}) collective-permute-start(bf16[2,1,1,2,72,256]{5,4,3,2,1,0:T(8,128)(2,1)S(1)} %get-tuple-element.43), channel_id=1, source_target_pairs={{0,6},{1,7},{2,0},{3,1},{4,2},{5,3},{6,4},{7,5},{8,14},{9,15},{10,... | collective-permute-start | bytes 442376 | tf_op jit(solution)/shard_map/ppermute | solution.py:65
  48.5 5.2 %collective-permute-start.16 = (bf16[2,1,1,1,72,256]{5,4,3,2,1,0:T(8,128)(2,1)S(1)}, bf16[2,1,1,1,72,256]{5,4,3,2,1,0:T(8,128)(2,1)S(1)}, u32[]{:S(2)}, u32[]{:S(2)}) collective-permute-start(bf16[2,1,1,1,72,256]{5,4,3,2,1,0:T(8,128)(2,1)S(1)} %dynamic-slice_convert_fusion.3), channel_id=1, source_target_pairs={{0,1},{1,0},{2,3},{3,2},{4,5},{5,4},{6,7},{7,6},{8,9},{9,8},{10,11... | collective-permute-start | bytes 221192 | tf_op jit(solution)/shard_map/ppermute | solution.py:65
  49.3 4.4 %copy-start.6 = (bf16[128,2560]{1,0:T(8,128)(2,1)}, bf16[128,2560]{1,0:T(8,128)(2,1)S(1)}, u32[]{:S(2)}) copy-start(bf16[128,2560]{1,0:T(8,128)(2,1)S(1)} %collective-permute-done.3.refs_2_) | copy-start | bytes 1966084
  49.3 9.0 %collective-permute-start.5 = (bf16[64,2560]{1,0:T(8,128)(2,1)S(1)}, bf16[64,2560]{1,0:T(8,128)(2,1)}, u32[]{:S(2)}, u32[]{:S(2)}) collective-permute-start(bf16[64,2560]{1,0:T(8,128)(2,1)S(1)} %slice.33), channel_id=1, source_target_pairs={{0,16},{1,17},{2,18},{3,19},{4,20},{5,21},{6,22},{7,23},{8,24},{9,... | collective-permute-start | bytes 983048 | tf_op jit(solution)/shard_map/ppermute | solution.py:65
  50.1 3.7 %copy-start.7 = (bf16[128,2560]{1,0:T(8,128)(2,1)}, bf16[128,2560]{1,0:T(8,128)(2,1)S(1)}, u32[]{:S(2)}) copy-start(bf16[128,2560]{1,0:T(8,128)(2,1)S(1)} %collective-permute-done.4.refs_3_) | copy-start | bytes 1966084
  50.1 9.9 %collective-permute-start.6 = (bf16[64,2560]{1,0:T(8,128)(2,1)S(1)}, bf16[64,2560]{1,0:T(8,128)(2,1)}, u32[]{:S(2)}, u32[]{:S(2)}) collective-permute-start(bf16[64,2560]{1,0:T(8,128)(2,1)S(1)} %slice.34), channel_id=1, source_target_pairs={{0,1},{1,0},{2,3},{3,2},{4,5},{5,4},{6,7},{7,6},{8,9},{9,8},{10,11... | collective-permute-start | bytes 983048 | tf_op jit(solution)/shard_map/ppermute | solution.py:65
  53.8 6.3 %collective-permute-start.17 = (bf16[1,1,1,1,72,256]{5,4,3,2,1,0:T(8,128)(2,1)S(1)}, bf16[1,1,1,1,72,256]{5,4,3,2,1,0:T(8,128)(2,1)S(1)}, u32[]{:S(2)}, u32[]{:S(2)}) collective-permute-start(bf16[1,1,1,1,72,256]{5,4,3,2,1,0:T(8,128)(2,1)S(1)} %dynamic-slice_convert_fusion.4), channel_id=1, source_target_pairs={{0,16},{1,17},{2,18},{3,19},{4,20},{5,21},{6,22},{7,23},{8,24},{9,... | collective-permute-start | bytes 110600 | tf_op jit(solution)/shard_map/ppermute | solution.py:65
  54.6 11.4 %collective-permute-start.7 = (bf16[128,2560]{1,0:T(8,128)(2,1)S(1)}, bf16[128,2560]{1,0:T(8,128)(2,1)S(1)}, u32[]{:S(2)}, u32[]{:S(2)}) collective-permute-start(bf16[128,2560]{1,0:T(8,128)(2,1)S(1)} %copy-done.8), channel_id=1, source_target_pairs={{0,8},{1,9},{2,10},{3,11},{4,12},{5,13},{6,14},{7,15},{8,0},{9,1},... | collective-permute-start | bytes 1966088 | tf_op jit(solution)/shard_map/ppermute | solution.py:65
  54.6 11.5 %collective-permute-start.8 = (bf16[128,2560]{1,0:T(8,128)(2,1)}, bf16[128,2560]{1,0:T(8,128)(2,1)S(1)}, u32[]{:S(2)}, u32[]{:S(2)}) collective-permute-start(bf16[128,2560]{1,0:T(8,128)(2,1)} %copy-done.6), channel_id=1, source_target_pairs={{0,8},{1,9},{2,10},{3,11},{4,12},{5,13},{6,14},{7,15},{8,0},{9,1},... | collective-permute-start | bytes 1966088 | tf_op jit(solution)/shard_map/ppermute | solution.py:65
  58.3 7.8 %collective-permute-start.9 = (bf16[128,2560]{1,0:T(8,128)(2,1)}, bf16[128,2560]{1,0:T(8,128)(2,1)}, u32[]{:S(2)}, u32[]{:S(2)}) collective-permute-start(bf16[128,2560]{1,0:T(8,128)(2,1)} %copy-done.7), channel_id=1, source_target_pairs={{0,8},{1,9},{2,10},{3,11},{4,12},{5,13},{6,14},{7,15},{8,0},{9,1},... | collective-permute-start | bytes 1966088 | tf_op jit(solution)/shard_map/ppermute | solution.py:65
  60.0 6.0 %collective-permute-start.10 = (bf16[64,2560]{1,0:T(8,128)(2,1)}, bf16[64,2560]{1,0:T(8,128)(2,1)}, u32[]{:S(2)}, u32[]{:S(2)}) collective-permute-start(bf16[64,2560]{1,0:T(8,128)(2,1)} %collective-permute-done.5.refs_4_), channel_id=1, source_target_pairs={{0,8},{1,9},{2,10},{3,11},{4,12},{5,13},{6,14},{7,15},{8,0},{9,1},... | collective-permute-start | bytes 983048 | tf_op jit(solution)/shard_map/ppermute | solution.py:65
  60.0 6.0 %collective-permute-start.11 = (bf16[64,2560]{1,0:T(8,128)(2,1)}, bf16[64,2560]{1,0:T(8,128)(2,1)}, u32[]{:S(2)}, u32[]{:S(2)}) collective-permute-start(bf16[64,2560]{1,0:T(8,128)(2,1)} %collective-permute-done.6.refs_5_), channel_id=1, source_target_pairs={{0,8},{1,9},{2,10},{3,11},{4,12},{5,13},{6,14},{7,15},{8,0},{9,1},... | collective-permute-start | bytes 983048 | tf_op jit(solution)/shard_map/ppermute | solution.py:65
  61.8 43.2 %all-to-all-start = ((bf16[32,64,256]{2,1,0:T(8,128)(2,1)}), bf16[32,64,256]{2,1,0:T(8,128)(2,1)S(1)}, u32[]{:S(2)}, u32[]{:S(2)}) async-start(bf16[32,64,256]{2,1,0:T(8,128)(2,1)} %broadcast_in_dim.51), calls=%async_computation | async-start | bytes 2097152 | tf_op jit(solution)/shard_map/all_to_all | solution.py:84
  66.0 0.8 copy-start.15
  66.1 1.0 copy-start.16
  105.1 19.3 %copy-start.4 = (bf16[32,64,256]{2,1,0:T(8,128)(2,1)}, bf16[32,64,256]{2,1,0:T(8,128)(2,1)S(1)}, u32[]{:S(2)}) copy-start(bf16[32,64,256]{2,1,0:T(8,128)(2,1)S(1)} %all-to-all-done) | copy-start | bytes 3145732
  105.1 27.2 %all-to-all-start.1 = ((f32[32,8,512]{2,1,0:T(8,128)}), f32[32,8,512]{2,1,0:T(8,128)S(1)}, u32[]{:S(2)}, u32[]{:S(2)}) async-start(f32[32,8,512]{2,1,0:T(8,128)} %bitcast.5), calls=%async_computation.1 | async-start | bytes 1048576 | tf_op jit(solution)/shard_map/all_to_all | solution.py:84
  124.4 8.0 %copy-start.1 = (f32[512,512]{1,0:T(8,128)S(1)}, f32[512,512]{1,0:T(8,128)}, u32[]{:S(2)}) copy-start(f32[512,512]{1,0:T(8,128)} %get-tuple-element.21.inv) | copy-start | bytes 3145732
  131.5 8.6 %copy-start.3 = (bf16[2048,256]{1,0:T(8,128)(2,1)S(1)}, bf16[2048,256]{1,0:T(8,128)(2,1)}, u32[]{:S(2)}) copy-start(bf16[2048,256]{1,0:T(8,128)(2,1)} %targets.1) | copy-start | bytes 3145732
  133.3 8.2 %copy-start.5 = (bf16[32,64,256]{2,1,0:T(8,128)(2,1)S(1)}, bf16[32,64,256]{2,1,0:T(8,128)(2,1)}, u32[]{:S(2)}) copy-start(bf16[32,64,256]{2,1,0:T(8,128)(2,1)} %copy-done.4) | copy-start | bytes 3145732
  134.2 21.8 %all-to-all-start.2 = ((bf16[32,16,512]{2,1,0:T(8,128)(2,1)}), bf16[32,16,512]{2,1,0:T(8,128)(2,1)S(1)}, u32[]{:S(2)}, u32[]{:S(2)}) async-start(bf16[32,16,512]{2,1,0:T(8,128)(2,1)} %broadcast_in_dim.52), calls=%async_computation.2 | async-start | bytes 1048576 | tf_op jit(solution)/shard_map/all_to_all | solution.py:84

commit v4 on v3

--- a/solution.py
+++ b/solution.py
@@ -142,7 +142,7 @@
 
 def prepare_kernel(count, width, *refs):
     place, pieces = refs[0], refs[1 : 1 + count]
-    turned_ref, ridged_ref, rows, sems = refs[1 + count :]
+    turned_ref, ridged_ref, rows, straight, sems = refs[1 + count :]
     copies, at = [], 0
     for k, piece in enumerate(pieces):
         n = piece.shape[0]
@@ -154,16 +154,12 @@
     pick = (slot == place[...]).astype(f32).astype(bf16)
     for copy in copies:
         copy.wait()
-    inter = cosine = None
     for lo in range(0, rows.shape[1], width):
         part = dot(pick, rows[:, lo : lo + width]).astype(bf16)
-        turned = part.T
-        turned_ref[lo : lo + width, :] = turned
-        product = dot(part, turned)
-        if lo == 0:
-            cosine = product / width
-        else:
-            inter = product if inter is None else inter + product
+        straight[:, lo : lo + width] = part
+        turned_ref[lo : lo + width, :] = part.T
+    inter = dot(straight[:, width:], turned_ref[width:, :])
+    cosine = dot(straight[:, :width], turned_ref[:width, :]) / width
     shift = ridge_shift + jnp.max(jnp.sum(jnp.abs(inter), axis=1, keepdims=True))
     r = lax.broadcasted_iota(jnp.int32, (BLOCK, BLOCK), 0)
     c = lax.broadcasted_iota(jnp.int32, (BLOCK, BLOCK), 1)
@@ -183,6 +179,7 @@
         out_specs=(VMEM,) * 2,
         scratch_shapes=[
             pltpu.VMEM((total, wide), bf16),
+            pltpu.VMEM((BLOCK, wide), bf16),
             pltpu.SemaphoreType.DMA((len(pieces),)),
         ],
         cost_estimate=pl.CostEstimate(
@@ -406,6 +403,29 @@
     )(inv, high, low)
 
 
+def finish_kernel(base, turned, coef, out):
+    out[...] = base[...] - dot(turned[...], coef[...], 1, 1)
+
+
+def finish(base, turned, coef):
+    pts, nt = base.shape
+    blk = pts // 2
+    return pl.pallas_call(
+        finish_kernel,
+        grid=(pts // blk,),
+        out_shape=jax.ShapeDtypeStruct((pts, nt), f32),
+        in_specs=[
+            pl.BlockSpec((blk, nt), lambda i: (i, 0)),
+            pl.BlockSpec((blk, BLOCK), lambda i: (i, 0)),
+            pl.BlockSpec((nt, BLOCK), lambda i: (0, 0)),
+        ],
+        out_specs=pl.BlockSpec((blk, nt), lambda i: (i, 0)),
+        cost_estimate=pl.CostEstimate(
+            flops=10**9, bytes_accessed=8 * 10**6, transcendentals=0
+        ),
+    )(base, turned, coef)
+
+
 def on_device(grid, points, factor, targets, pivot_slots, pivot_counts):
     n, me = grid.n, grid.here()
     cap, devices = pivot_slots.shape[1], grid.size
@@ -428,38 +448,41 @@
     )
     chunks = grid.reduce(chunks.reshape(grid.shape + chunks.shape[1:]), "c")
 
-    arrived = grid.spread(own, "z")
-    along_z = jnp.concatenate([own] + arrived, 0)
-    zs = [(0, 0, s, 0) for s in range(n["z"])]
-
     def moved(origin, dim, s):
         at = "yczx".index(dim)
         return [tuple(v + s if k == at else v for k, v in enumerate(o)) for o in origin]
 
-    pieces, origins = [along_z], list(zs)
-    by_x, by_y = grid.spread(along_z, "x"), grid.spread(along_z, "y")
-    pieces += by_x + by_y
-    for s in range(1, n["x"]):
-        origins += moved(zs, "x", s)
-    for s in range(1, n["y"]):
-        origins += moved(zs, "y", s)
+    blocks = [own] + grid.spread(own, "z")
+    unit = max(1, ALIGN // cap)
+    along_z = []
+    for k in range(0, n["z"], unit):
+        part = blocks[k : k + unit]
+        along_z.append(
+            (
+                part[0] if len(part) == 1 else jnp.concatenate(part, 0),
+                [(0, 0, s, 0) for s in range(k, k + len(part))],
+            )
+        )
+
+    def forward(units, dim):
+        return [
+            (grid.shift(part, dim, s), moved(origin, dim, s))
+            for part, origin in units
+            for s in range(1, n[dim])
+        ]
+
+    half = (len(along_z) + 1) // 2
+    found = list(along_z)
+    for k, one in enumerate(along_z):
+        by_x, by_y = forward([one], "x"), forward([one], "y")
+        both = forward(by_x, "y") if k < half else forward(by_y, "x")
+        found += by_x + by_y + both
+    found += forward(found, "c")
+    pieces = [part for part, _ in found]
+    origins = [o for _, origin in found for o in origin]
     for dim in "zxy":
         sends = [part.astype(bf16) for part in grid.sends(chunks, dim)]
         chunks = grid.reduce(chunks, dim, sends)
-    half = (n["z"] + 1) // 2
-    for s, block in enumerate(by_x, 1):
-        pieces += grid.spread(block[: half * cap], "y")
-        for r in range(1, n["y"]):
-            origins += moved(moved(zs[:half], "x", s), "y", r)
-    for r, block in enumerate(by_y, 1):
-        if half < n["z"]:
-            pieces += grid.spread(block[half * cap :], "x")
-            for s in range(1, n["x"]):
-                origins += moved(moved(zs[half:], "x", s), "y", r)
-    mine, mine_origins = list(pieces), list(origins)
-    for s in range(1, n["c"]):
-        pieces += [grid.shift(p, "c", s) for p in mine]
-        origins += moved(mine_origins, "c", s)
 
     shifts = np.array(origins)
     dev = jnp.zeros((len(origins),), jnp.int32)
@@ -502,8 +525,8 @@
     norm_new = jnp.sum(every[:, t : t + 3], axis=(0, 1))
     coef_new = (every[:, :t].reshape(nt, BLOCK) / (norm_new + damping)[None, :]).astype(bf16)
 
-    fitted = dot(factor, coef_held)
-    return new_columns, (targets.astype(f32) - fitted) - dot(new_turned, coef_new, 1, 1)
+    base = targets.astype(f32) - dot(factor, coef_held)
+    return new_columns, finish(base, new_turned, coef_new)
 
 
 def step(grid, *args):

time: 162 us -> 188 us (1.16)
  waiting for transfers between devices: 23.9 us -> 43.9 us
  starting transfers between devices: 34.3 us -> 49.3 us
  local copies, waits for them, and re-layouts: 16 us -> 5.71 us
  Pallas kernels: 61.7 us -> 65.2 us
  matrix products: 13.9 us -> 10.9 us
    ppermute x18 -> x37, waiting for transfers between devices: 16.7 us -> 35 us  [shift(): return lax.ppermute(value, AXES, list(zip(self.ids.ravel(), to.ravel())))]
    ppermute x18 -> x37, starting transfers between devices: 18.4 us -> 29.6 us  [shift(): return lax.ppermute(value, AXES, list(zip(self.ids.ravel(), to.ravel())))]
    unnamed x42 -> x65, local copies, waits for them, and re-layouts: 9.68 us -> 1.04 us
    pallas_call x0 -> x1, Pallas kernels: none -> 3.7 us  [finish(): pl.pallas_call(finish_kernel, grid=(pts // blk,), out_shape=jax.ShapeDtyp...]
    all_to_all x3, starting transfers between devices: 16 us -> 19.6 us  [exchange(): return lax.all_to_all(parts, AXES, 0, 0, tiled=True)]
    dot_general x4 -> x3, matrix products: 13.9 us -> 10.9 us  [dot(): lax.dot_general(a, b, (((da,), (db,)), ((), ())), precision=lax.Precision...]
  transfers between devices with their start and end apart: 21 -> 40, of which waited for: 6 -> 13; matrix products, arithmetic and copies ran while one was open for 20% -> 8% of each run, Pallas kernels for 36% -> 31%
where the time goes in v4:
time: 188 us; the launch traced here: 187 us
  Pallas kernels  65.2 us (35%)
  starting transfers between devices  49.3 us (26%)
  waiting for transfers between devices  43.9 us (23%)
  other arithmetic  10.9 us (6%)
  matrix products  10.9 us (6%)
  local copies, waits for them, and re-layouts  5.71 us (3%)
    ppermute x37, waiting for transfers between devices, shift(): return lax.ppermute(value, AXES, list(zip(self.ids.ravel(), to.ravel())))  35 us
    ppermute x37, starting transfers between devices, shift(): return lax.ppermute(value, AXES, list(zip(self.ids.ravel(), to.ravel())))  29.6 us
    pallas_call x2, Pallas kernels, factor_step(): pl.pallas_call(functools.partial(factor_kernel, first, last), out_shape=(...  28 us
    all_to_all x3, starting transfers between devices, exchange(): return lax.all_to_all(parts, AXES, 0, 0, tiled=True)  19.6 us
    pallas_call x1, Pallas kernels, downdate(): pl.pallas_call(downdate_kernel, grid=(pts // blk,), out_shape=(jax.ShapeD...  12.7 us
    dot_general x3, matrix products, dot(): lax.dot_general(a, b, (((da,), (db,)), ((), ())), precision=lax.Precision...  10.9 us
    pallas_call x1, Pallas kernels, prepare(): pl.pallas_call(functools.partial(prepare_kernel, len(pieces), width), out...  9.26 us
    all_to_all x3, waiting for transfers between devices, exchange(): return lax.all_to_all(parts, AXES, 0, 0, tiled=True)  8.9 us
  transfers between devices with their start and end apart: 40, of which 13 were waited for; matrix products, arithmetic and copies ran while one was open for 8% of the time, Pallas kernels for 31%

profile of v4, /device:TPU:0, one launch (start us, length us, event | category | flops | bytes accessed | tf_op | source)
XLA Modules:
  0.0 187.1 jit_solution(17323936869101577771)
XLA Ops:
  0.7 4.4 %shard_map.104.refs_1_ = bf16[32,2560]{1,0:T(8,128)(2,1)} custom-call(s32[1,32]{1,0:T(1,128)} %slots.1, bf16[2048,512]{1,0:T(8,128)(2,1)} %points.3, bf16[2048,2048]{1,0:T(8,128)(2,1)} %factor.3), custom_call_target="tpu_custom_call" | custom-call | flops 100000000 | bytes 3000000 | tf_op jit(solution)/shard_map/pallas_call | solution.py:128
  5.1 5.3 %multiply_reduce_fusion = f32[2048]{0:T(1024)S(1)} fusion(bf16[2048,2048]{1,0:T(8,128)(2,1)} %factor.3), kind=kLoop, calls=%fused_computation | loop fusion | flops 12580864 | bytes 8396800 | tf_op jit(solution)/shard_map/reduce_sum | solution.py:437
  10.4 0.5 copy-done
  10.8 2.6 %fusion.27 = f32[2048,256]{1,0:T(8,128)S(1)} fusion(bf16[2048,2048]{1,0:T(8,128)(2,1)S(1)} %copy-done, bf16[2048,256]{1,0:T(8,128)(2,1)S(1)} %copy-done.9), kind=kOutput, calls=%fused_computation.68 | convolution fusion | flops 2147483648 | bytes 11534336 | tf_op jit(solution)/shard_map/dot_general | solution.py:28
  13.7 1.1 fusion.1
  14.8 0.5 collective-permute-start.31
  15.3 2.6 %collective-permute-start = (bf16[32,2560]{1,0:T(8,128)(2,1)}, bf16[32,2560]{1,0:T(8,128)(2,1)}, u32[]{:S(2)}, u32[]{:S(2)}) collective-permute-start(bf16[32,2560]{1,0:T(8,128)(2,1)} %shard_map.104.refs_1_), channel_id=1, source_target_pairs={{0,2},{1,3},{2,4},{3,5},{4,6},{5,7},{6,0},{7,1},{8,10},{9,11},{10,... | collective-permute-start | bytes 491528 | tf_op jit(solution)/shard_map/ppermute | solution.py:65
  17.9 2.6 %collective-permute-start.1 = (bf16[32,2560]{1,0:T(8,128)(2,1)}, bf16[32,2560]{1,0:T(8,128)(2,1)}, u32[]{:S(2)}, u32[]{:S(2)}) collective-permute-start(bf16[32,2560]{1,0:T(8,128)(2,1)} %shard_map.104.refs_1_), channel_id=1, source_target_pairs={{0,4},{1,5},{2,6},{3,7},{4,0},{5,1},{6,2},{7,3},{8,12},{9,13},{10,... | collective-permute-start | bytes 491528 | tf_op jit(solution)/shard_map/ppermute | solution.py:65
  20.5 0.7 copy.19
  21.2 0.8 reduce-window.9
  21.9 0.6 reduce
  22.6 0.7 sub.60
  23.6 1.9 %collective-permute-start.33 = (bf16[2,1,1,2,72,256]{5,4,3,2,1,0:T(8,128)(2,1)S(1)}, bf16[2,1,1,2,72,256]{5,4,3,2,1,0:T(8,128)(2,1)S(1)}, u32[]{:S(2)}, u32[]{:S(2)}) collective-permute-start(bf16[2,1,1,2,72,256]{5,4,3,2,1,0:T(8,128)(2,1)S(1)} %get-tuple-element.36), channel_id=1, source_target_pairs={{0,4},{1,5},{2,6},{3,7},{4,0},{5,1},{6,2},{7,3},{8,12},{9,13},{10,... | collective-permute-start | bytes 442376 | tf_op jit(solution)/shard_map/ppermute | solution.py:65
  25.5 1.9 %collective-permute-start.34 = (bf16[2,1,1,2,72,256]{5,4,3,2,1,0:T(8,128)(2,1)S(1)}, bf16[2,1,1,2,72,256]{5,4,3,2,1,0:T(8,128)(2,1)S(1)}, u32[]{:S(2)}, u32[]{:S(2)}) collective-permute-start(bf16[2,1,1,2,72,256]{5,4,3,2,1,0:T(8,128)(2,1)S(1)} %get-tuple-element.35), channel_id=1, source_target_pairs={{0,6},{1,7},{2,0},{3,1},{4,2},{5,3},{6,4},{7,5},{8,14},{9,15},{10,... | collective-permute-start | bytes 442376 | tf_op jit(solution)/shard_map/ppermute | solution.py:65
  27.4 4.8 %collective-permute-done.32 = bf16[2,1,1,2,72,256]{5,4,3,2,1,0:T(8,128)(2,1)S(1)} collective-permute-done((bf16[2,1,1,2,72,256]{5,4,3,2,1,0:T(8,128)(2,1)S(1)}, bf16[2,1,1,2,72,256]{5,4,3,2,1,0:T(8,128)(2,1)S(1)}, u32[]{:S(2)}, u32[]{:S(2)}) %collective-permute-start.32) | collective-permute-done | bytes 147488 | tf_op jit(solution)/shard_map/ppermute | solution.py:65
  32.2 1.0 collective-permute-start.2
  33.2 8.4 %collective-permute-done.33 = bf16[2,1,1,2,72,256]{5,4,3,2,1,0:T(8,128)(2,1)S(1)} collective-permute-done((bf16[2,1,1,2,72,256]{5,4,3,2,1,0:T(8,128)(2,1)S(1)}, bf16[2,1,1,2,72,256]{5,4,3,2,1,0:T(8,128)(2,1)S(1)}, u32[]{:S(2)}, u32[]{:S(2)}) %collective-permute-start.33) | collective-permute-done | bytes 147488 | tf_op jit(solution)/shard_map/ppermute | solution.py:65
  41.6 1.5 collective-permute-start.3
  43.2 0.6 collective-permute-start.35
  44.0 1.6 collective-permute-start.4
  45.6 3.7 %collective-permute-done.35 = bf16[2,1,1,1,72,256]{5,4,3,2,1,0:T(8,128)(2,1)S(1)} collective-permute-done((bf16[2,1,1,1,72,256]{5,4,3,2,1,0:T(8,128)(2,1)S(1)}, bf16[2,1,1,1,72,256]{5,4,3,2,1,0:T(8,128)(2,1)S(1)}, u32[]{:S(2)}, u32[]{:S(2)}) %collective-permute-start.35) | collective-permute-done | bytes 73760 | tf_op jit(solution)/shard_map/ppermute | solution.py:65
  49.3 1.5 collective-permute-start.6
  50.8 1.6 collective-permute-start.7
  52.4 0.5 collective-permute-start.10
  52.9 0.5 collective-permute-start.9
  53.5 1.5 collective-permute-start.13
  55.0 0.7 collective-permute-done.6.refs_8_
  55.6 1.5 collective-permute-start.36
  57.2 0.7 select_n.156.refs_0_
  57.9 3.8 %collective-permute-done.10.refs_12_ = bf16[32,2560]{1,0:T(8,128)(2,1)S(1)} collective-permute-done((bf16[32,2560]{1,0:T(8,128)(2,1)}, bf16[32,2560]{1,0:T(8,128)(2,1)S(1)}, u32[]{:S(2)}, u32[]{:S(2)}) %collective-permute-start.10) | collective-permute-done | bytes 163872 | tf_op jit(solution)/shard_map/ppermute | solution.py:65
  61.7 0.5 collective-permute-start.12
  62.2 1.2 collective-permute-done.13.refs_15_
  63.5 0.5 collective-permute-start.17
  64.1 1.5 collective-permute-start.5
  65.6 1.4 collective-permute-done.12.refs_14_
  67.0 3.6 %collective-permute-done.5.refs_7_ = bf16[32,2560]{1,0:T(8,128)(2,1)S(1)} collective-permute-done((bf16[32,2560]{1,0:T(8,128)(2,1)S(1)}, bf16[32,2560]{1,0:T(8,128)(2,1)S(1)}, u32[]{:S(2)}, u32[]{:S(2)}) %collective-permute-start.5) | collective-permute-done | bytes 163872 | tf_op jit(solution)/shard_map/ppermute | solution.py:65
  70.6 1.6 collective-permute-start.8
  72.2 0.5 collective-permute-start.11
  72.7 1.5 collective-permute-start.14
  74.4 0.5 collective-permute-start.26
  74.8 2.5 %collective-permute-done.8.refs_10_ = bf16[32,2560]{1,0:T(8,128)(2,1)} collective-permute-done((bf16[32,2560]{1,0:T(8,128)(2,1)S(1)}, bf16[32,2560]{1,0:T(8,128)(2,1)}, u32[]{:S(2)}, u32[]{:S(2)}) %collective-permute-start.8) | collective-permute-done | bytes 163872 | tf_op jit(solution)/shard_map/ppermute | solution.py:65
  77.3 2.1 %collective-permute-done.11.refs_13_ = bf16[32,2560]{1,0:T(8,128)(2,1)} collective-permute-done((bf16[32,2560]{1,0:T(8,128)(2,1)S(1)}, bf16[32,2560]{1,0:T(8,128)(2,1)}, u32[]{:S(2)}, u32[]{:S(2)}) %collective-permute-start.11) | collective-permute-done | bytes 163872 | tf_op jit(solution)/shard_map/ppermute | solution.py:65
  79.4 2.7 %collective-permute-done.14.refs_16_ = bf16[32,2560]{1,0:T(8,128)(2,1)} collective-permute-done((bf16[32,2560]{1,0:T(8,128)(2,1)S(1)}, bf16[32,2560]{1,0:T(8,128)(2,1)}, u32[]{:S(2)}, u32[]{:S(2)}) %collective-permute-start.14) | collective-permute-done | bytes 163872 | tf_op jit(solution)/shard_map/ppermute | solution.py:65
  82.1 0.6 collective-permute-start.28
  82.8 0.4 collective-permute-start.24
  83.5 0.3 collective-permute-start.30
  83.8 0.3 copy-done.30
  84.2 1.1 broadcast_in_dim.51
  85.4 8.1 %all-to-all-start = ((bf16[32,64,256]{2,1,0:T(8,128)(2,1)}), bf16[32,64,256]{2,1,0:T(8,128)(2,1)S(1)}, u32[]{:S(2)}, u32[]{:S(2)}) async-start(bf16[32,64,256]{2,1,0:T(8,128)(2,1)} %broadcast_in_dim.51), calls=%async_computation | async-start | bytes 2097152 | tf_op jit(solution)/shard_map/all_to_all | solution.py:84
  93.7 9.3 %shard_map.105 = (bf16[2560,512]{1,0:T(8,128)(2,1)}, f32[512,512]{1,0:T(8,128)}) custom-call(s32[1,1024]{1,0:T(1,128)} %select_n.156.refs_0_, bf16[32,2560]{1,0:T(8,128)(2,1)} %shard_map.104.refs_1_, bf16[32,2560]{1,0:T(8,128)(2,1)} %collective-permute-done.refs_2_, bf16[32,2560]{1,0:T(8,128)(2,1)} %collective-permute-done.1.refs_3_, ...), custom_call_target="tpu_custom_call" | custom-call | flops 6000000000 | bytes 10000000 | tf_op jit(solution)/shard_map/pallas_call | solution.py:172
  103.0 12.7 %shard_map.108 = (bf16[2048,512]{1,0:T(8,128)(2,1)}, bf16[2048,512]{1,0:T(8,128)(2,1)}, f32[256,512]{1,0:T(8,128)}) custom-call(bf16[2560,512]{1,0:T(8,128)(2,1)} %get-tuple-element.22.turned, bf16[2048,512]{1,0:T(8,128)(2,1)} %points.3, bf16[2048,2048]{1,0:T(8,128)(2,1)} %factor.3, bf16[2048,256]{1,0:T(8,128)(2,1)} %targets.1), custom_call_target="tpu_custom_call" | custom-call | flops 6000000000 | bytes 16000000 | tf_op jit(solution)/shard_map/pallas_call | solution.py:214
  115.6 1.1 broadcast_in_dim.50.r_in
  116.8 14.6 %shard_map.106 = (f32[512,512]{1,0:T(8,128)}, f32[512,512]{1,0:T(8,128)}) custom-call(f32[512,512]{1,0:T(8,128)} %get-tuple-element.18.a_in, f32[512,512]{1,0:T(8,128)} %broadcast_in_dim.50.r_in), custom_call_target="tpu_custom_call", output_to_operand_aliasing={{0}: (0, {}), {1}: (1, {})} | custom-call | flops 12000000000 | bytes 4000000 | tf_op jit(solution)/shard_map/pallas_call | solution.py:336
  131.4 5.9 %all-to-all-start.1 = ((f32[32,8,512]{2,1,0:T(8,128)}), f32[32,8,512]{2,1,0:T(8,128)S(1)}, u32[]{:S(2)}, u32[]{:S(2)}) async-start(f32[32,8,512]{2,1,0:T(8,128)} %bitcast.5), calls=%async_computation.1 | async-start | bytes 1048576 | tf_op jit(solution)/shard_map/all_to_all | solution.py:84
  137.3 13.4 %shard_map.107 = (f32[512,512]{1,0:T(8,128)}, f32[512,512]{1,0:T(8,128)}) custom-call(f32[512,512]{1,0:T(8,128)} %get-tuple-element.19.a_in, f32[512,512]{1,0:T(8,128)} %get-tuple-element.20.r_in), custom_call_target="tpu_custom_call", output_to_operand_aliasing={{0}: (0, {}), {1}: (1, {})} | custom-call | flops 12000000000 | bytes 4000000 | tf_op jit(solution)/shard_map/pallas_call | solution.py:336
  150.6 7.2 %shard_map.109 = (bf16[512,2048]{1,0:T(8,128)(2,1)}, bf16[2048,512]{1,0:T(8,128)(2,1)}, f32[1,512]{1,0:T(1,128)}) custom-call(f32[512,512]{1,0:T(8,128)} %get-tuple-element.21.inv, bf16[2048,512]{1,0:T(8,128)(2,1)} %get-tuple-element.23.high, bf16[2048,512]{1,0:T(8,128)(2,1)} %get-tuple-element.24.low), custom_call_target="tpu_custom_call" | custom-call | flops 4000000000 | bytes 8000000 | tf_op jit(solution)/shard_map/pallas_call | solution.py:377
  157.9 0.7 fusion.26
  158.7 1.0 convolution_convert_fusion
  159.7 0.9 broadcast_in_dim.52
  160.5 5.6 %all-to-all-start.2 = ((bf16[32,16,512]{2,1,0:T(8,128)(2,1)}), bf16[32,16,512]{2,1,0:T(8,128)(2,1)S(1)}, u32[]{:S(2)}, u32[]{:S(2)}) async-start(bf16[32,16,512]{2,1,0:T(8,128)(2,1)} %broadcast_in_dim.52), calls=%async_computation.2 | async-start | bytes 1048576 | tf_op jit(solution)/shard_map/all_to_all | solution.py:84
  166.2 7.3 %fusion.base = f32[2048,256]{1,0:T(8,128)} fusion(bf16[2048,2048]{1,0:T(8,128)(2,1)} %factor.3, bf16[2048,256]{1,0:T(8,128)(2,1)S(1)} %bitcast.36, bf16[2048,256]{1,0:T(8,128)(2,1)} %targets.1), kind=kOutput, calls=%fused_computation.4 | convolution fusion | flops 2148532224 | bytes 12582912 | tf_op jit(solution)/shard_map/dot_general | solution.py:28
  173.5 8.9 %all-to-all-done.2 = bf16[32,16,512]{2,1,0:T(8,128)(2,1)S(1)} async-done(((bf16[32,16,512]{2,1,0:T(8,128)(2,1)}), bf16[32,16,512]{2,1,0:T(8,128)(2,1)S(1)}, u32[]{:S(2)}, u32[]{:S(2)}) %all-to-all-start.2) | async-done | bytes 524320 | tf_op jit(solution)/shard_map/all_to_all | solution.py:84
  182.6 0.8 fusion.5.coef
  183.4 3.7 %shard_map.110 = f32[2048,256]{1,0:T(8,128)} custom-call(f32[2048,256]{1,0:T(8,128)} %fusion.base, bf16[2048,512]{1,0:T(8,128)(2,1)} %get-tuple-element.29.turned, bf16[256,512]{1,0:T(8,128)(2,1)} %fusion.5.coef), custom_call_target="tpu_custom_call" | custom-call | flops 1000000000 | bytes 8000000 | tf_op jit(solution)/shard_map/pallas_call | solution.py:413
  (122 shorter events, 2.0 us)
Async XLA Ops:
  0.7 9.7 %copy-start.9 = (bf16[2048,256]{1,0:T(8,128)(2,1)S(1)}, bf16[2048,256]{1,0:T(8,128)(2,1)}, u32[]{:S(2)}) copy-start(bf16[2048,256]{1,0:T(8,128)(2,1)} %targets.1) | copy-start | bytes 3145732
  5.1 5.8 %copy-start = (bf16[2048,2048]{1,0:T(8,128)(2,1)S(1)}, bf16[2048,2048]{1,0:T(8,128)(2,1)}, u32[]{:S(2)}) copy-start(bf16[2048,2048]{1,0:T(8,128)(2,1)} %factor.3) | copy-start | bytes 25165828
  13.6 6.9 %copy-start.3 = (s32[32]{0:T(128)S(1)}, s32[32]{0:T(128)}, u32[]{:S(2)}) copy-start(s32[32]{0:T(128)} %param.13) | copy-start | bytes 388
  14.8 8.4 %collective-permute-start.31 = (f32[2,1,4,2,72,256]{5,4,3,2,1,0:T(8,128)}, f32[2,1,4,2,72,256]{5,4,3,2,1,0:T(8,128)S(1)}, u32[]{:S(2)}, u32[]{:S(2)}) collective-permute-start(f32[2,1,4,2,72,256]{5,4,3,2,1,0:T(8,128)} %fusion.1), channel_id=1, source_target_pairs={{0,8},{1,9},{2,10},{3,11},{4,12},{5,13},{6,14},{7,15},{8,0},{9,1},... | collective-permute-start | bytes 3538952 | tf_op jit(solution)/shard_map/ppermute | solution.py:65
  15.3 28.7 %collective-permute-start = (bf16[32,2560]{1,0:T(8,128)(2,1)}, bf16[32,2560]{1,0:T(8,128)(2,1)}, u32[]{:S(2)}, u32[]{:S(2)}) collective-permute-start(bf16[32,2560]{1,0:T(8,128)(2,1)} %shard_map.104.refs_1_), channel_id=1, source_target_pairs={{0,2},{1,3},{2,4},{3,5},{4,6},{5,7},{6,0},{7,1},{8,10},{9,11},{10,... | collective-permute-start | bytes 491528 | tf_op jit(solution)/shard_map/ppermute | solution.py:65
  17.9 27.7 %collective-permute-start.1 = (bf16[32,2560]{1,0:T(8,128)(2,1)}, bf16[32,2560]{1,0:T(8,128)(2,1)}, u32[]{:S(2)}, u32[]{:S(2)}) collective-permute-start(bf16[32,2560]{1,0:T(8,128)(2,1)} %shard_map.104.refs_1_), channel_id=1, source_target_pairs={{0,4},{1,5},{2,6},{3,7},{4,0},{5,1},{6,2},{7,3},{8,12},{9,13},{10,... | collective-permute-start | bytes 491528 | tf_op jit(solution)/shard_map/ppermute | solution.py:65
  23.2 4.2 %copy-start.7 = (s32[32]{0:T(128)S(1)}, s32[32]{0:T(128)}, u32[]{:S(2)}) copy-start(s32[32]{0:T(128)} %constant.197) | copy-start | bytes 388
  23.2 4.2 %copy-start.8 = (s32[32]{0:T(128)S(1)}, s32[32]{0:T(128)}, u32[]{:S(2)}) copy-start(s32[32]{0:T(128)} %constant.198) | copy-start | bytes 388
  23.2 8.9 %copy-start.2 = (bf16[32,2560]{1,0:T(8,128)(2,1)S(1)}, bf16[32,2560]{1,0:T(8,128)(2,1)}, u32[]{:S(2)}) copy-start(bf16[32,2560]{1,0:T(8,128)(2,1)} %shard_map.104.refs_1_) | copy-start | bytes 491524
  23.2 20.5 %copy-start.4 = (s32[32]{0:T(128)S(1)}, s32[32]{0:T(128)}, u32[]{:S(2)}) copy-start(s32[32]{0:T(128)} %param.13) | copy-start | bytes 388
  23.5 8.7 %collective-permute-start.32 = (bf16[2,1,1,2,72,256]{5,4,3,2,1,0:T(8,128)(2,1)S(1)}, bf16[2,1,1,2,72,256]{5,4,3,2,1,0:T(8,128)(2,1)S(1)}, u32[]{:S(2)}, u32[]{:S(2)}) collective-permute-start(bf16[2,1,1,2,72,256]{5,4,3,2,1,0:T(8,128)(2,1)S(1)} %get-tuple-element.34), channel_id=1, source_target_pairs={{0,2},{1,3},{2,4},{3,5},{4,6},{5,7},{6,0},{7,1},{8,10},{9,11},{10,... | collective-permute-start | bytes 442376 | tf_op jit(solution)/shard_map/ppermute | solution.py:65
  23.6 18.0 %collective-permute-start.33 = (bf16[2,1,1,2,72,256]{5,4,3,2,1,0:T(8,128)(2,1)S(1)}, bf16[2,1,1,2,72,256]{5,4,3,2,1,0:T(8,128)(2,1)S(1)}, u32[]{:S(2)}, u32[]{:S(2)}) collective-permute-start(bf16[2,1,1,2,72,256]{5,4,3,2,1,0:T(8,128)(2,1)S(1)} %get-tuple-element.36), channel_id=1, source_target_pairs={{0,4},{1,5},{2,6},{3,7},{4,0},{5,1},{6,2},{7,3},{8,12},{9,13},{10,... | collective-permute-start | bytes 442376 | tf_op jit(solution)/shard_map/ppermute | solution.py:65
  25.5 17.6 %collective-permute-start.34 = (bf16[2,1,1,2,72,256]{5,4,3,2,1,0:T(8,128)(2,1)S(1)}, bf16[2,1,1,2,72,256]{5,4,3,2,1,0:T(8,128)(2,1)S(1)}, u32[]{:S(2)}, u32[]{:S(2)}) collective-permute-start(bf16[2,1,1,2,72,256]{5,4,3,2,1,0:T(8,128)(2,1)S(1)} %get-tuple-element.35), channel_id=1, source_target_pairs={{0,6},{1,7},{2,0},{3,1},{4,2},{5,3},{6,4},{7,5},{8,14},{9,15},{10,... | collective-permute-start | bytes 442376 | tf_op jit(solution)/shard_map/ppermute | solution.py:65
  32.2 18.6 %collective-permute-start.2 = (bf16[32,2560]{1,0:T(8,128)(2,1)S(1)}, bf16[32,2560]{1,0:T(8,128)(2,1)S(1)}, u32[]{:S(2)}, u32[]{:S(2)}) collective-permute-start(bf16[32,2560]{1,0:T(8,128)(2,1)S(1)} %copy-done.2), channel_id=1, source_target_pairs={{0,6},{1,7},{2,0},{3,1},{4,2},{5,3},{6,4},{7,5},{8,14},{9,15},{10,... | collective-permute-start | bytes 491528 | tf_op jit(solution)/shard_map/ppermute | solution.py:65
  41.6 10.8 %collective-permute-start.3 = (bf16[32,2560]{1,0:T(8,128)(2,1)S(1)}, bf16[32,2560]{1,0:T(8,128)(2,1)S(1)}, u32[]{:S(2)}, u32[]{:S(2)}) collective-permute-start(bf16[32,2560]{1,0:T(8,128)(2,1)S(1)} %copy-done.2), channel_id=1, source_target_pairs={{0,1},{1,0},{2,3},{3,2},{4,5},{5,4},{6,7},{7,6},{8,9},{9,8},{10,11... | collective-permute-start | bytes 491528 | tf_op jit(solution)/shard_map/ppermute | solution.py:65
  43.2 6.1 %collective-permute-start.35 = (bf16[2,1,1,1,72,256]{5,4,3,2,1,0:T(8,128)(2,1)S(1)}, bf16[2,1,1,1,72,256]{5,4,3,2,1,0:T(8,128)(2,1)S(1)}, u32[]{:S(2)}, u32[]{:S(2)}) collective-permute-start(bf16[2,1,1,1,72,256]{5,4,3,2,1,0:T(8,128)(2,1)S(1)} %dynamic-slice_convert_fusion.3), channel_id=1, source_target_pairs={{0,1},{1,0},{2,3},{3,2},{4,5},{5,4},{6,7},{7,6},{8,9},{9,8},{10,11... | collective-permute-start | bytes 221192 | tf_op jit(solution)/shard_map/ppermute | solution.py:65
  44.0 8.9 %collective-permute-start.4 = (bf16[32,2560]{1,0:T(8,128)(2,1)S(1)}, bf16[32,2560]{1,0:T(8,128)(2,1)S(1)}, u32[]{:S(2)}, u32[]{:S(2)}) collective-permute-start(bf16[32,2560]{1,0:T(8,128)(2,1)S(1)} %copy-done.2), channel_id=1, source_target_pairs={{0,16},{1,17},{2,18},{3,19},{4,20},{5,21},{6,22},{7,23},{8,24},{9,... | collective-permute-start | bytes 491528 | tf_op jit(solution)/shard_map/ppermute | solution.py:65
  45.6 7.9 %collective-permute-start.15 = (bf16[32,2560]{1,0:T(8,128)(2,1)S(1)}, bf16[32,2560]{1,0:T(8,128)(2,1)S(1)}, u32[]{:S(2)}, u32[]{:S(2)}) collective-permute-start(bf16[32,2560]{1,0:T(8,128)(2,1)S(1)} %copy-done.2), channel_id=1, source_target_pairs={{0,8},{1,9},{2,10},{3,11},{4,12},{5,13},{6,14},{7,15},{8,0},{9,1},... | collective-permute-start | bytes 491528 | tf_op jit(solution)/shard_map/ppermute | solution.py:65
  49.3 6.4 %collective-permute-start.6 = (bf16[32,2560]{1,0:T(8,128)(2,1)}, bf16[32,2560]{1,0:T(8,128)(2,1)S(1)}, u32[]{:S(2)}, u32[]{:S(2)}) collective-permute-start(bf16[32,2560]{1,0:T(8,128)(2,1)} %collective-permute-done.refs_2_), channel_id=1, source_target_pairs={{0,1},{1,0},{2,3},{3,2},{4,5},{5,4},{6,7},{7,6},{8,9},{9,8},{10,11... | collective-permute-start | bytes 491528 | tf_op jit(solution)/shard_map/ppermute | solution.py:65
  50.8 42.8 %copy-start.10 = (bf16[32,2560]{1,0:T(8,128)(2,1)}, bf16[32,2560]{1,0:T(8,128)(2,1)S(1)}, u32[]{:S(2)}) copy-start(bf16[32,2560]{1,0:T(8,128)(2,1)S(1)} %collective-permute-done.2.refs_4_) | copy-start | bytes 491524
  50.8 12.6 %collective-permute-start.7 = (bf16[32,2560]{1,0:T(8,128)(2,1)}, bf16[32,2560]{1,0:T(8,128)(2,1)S(1)}, u32[]{:S(2)}, u32[]{:S(2)}) collective-permute-start(bf16[32,2560]{1,0:T(8,128)(2,1)} %collective-permute-done.refs_2_), channel_id=1, source_target_pairs={{0,16},{1,17},{2,18},{3,19},{4,20},{5,21},{6,22},{7,23},{8,24},{9,... | collective-permute-start | bytes 491528 | tf_op jit(solution)/shard_map/ppermute | solution.py:65
  52.4 41.2 %copy-start.11 = (bf16[32,2560]{1,0:T(8,128)(2,1)}, bf16[32,2560]{1,0:T(8,128)(2,1)S(1)}, u32[]{:S(2)}) copy-start(bf16[32,2560]{1,0:T(8,128)(2,1)S(1)} %collective-permute-done.3.refs_5_) | copy-start | bytes 491524
  52.4 9.3 %collective-permute-start.10 = (bf16[32,2560]{1,0:T(8,128)(2,1)}, bf16[32,2560]{1,0:T(8,128)(2,1)S(1)}, u32[]{:S(2)}, u32[]{:S(2)}) collective-permute-start(bf16[32,2560]{1,0:T(8,128)(2,1)} %collective-permute-done.1.refs_3_), channel_id=1, source_target_pairs={{0,16},{1,17},{2,18},{3,19},{4,20},{5,21},{6,22},{7,23},{8,24},{9,... | collective-permute-start | bytes 491528 | tf_op jit(solution)/shard_map/ppermute | solution.py:65
  52.9 40.7 %copy-start.12 = (bf16[32,2560]{1,0:T(8,128)(2,1)}, bf16[32,2560]{1,0:T(8,128)(2,1)S(1)}, u32[]{:S(2)}) copy-start(bf16[32,2560]{1,0:T(8,128)(2,1)S(1)} %collective-permute-done.4.refs_6_) | copy-start | bytes 491524
  52.9 11.1 %collective-permute-start.9 = (bf16[32,2560]{1,0:T(8,128)(2,1)}, bf16[32,2560]{1,0:T(8,128)(2,1)S(1)}, u32[]{:S(2)}, u32[]{:S(2)}) collective-permute-start(bf16[32,2560]{1,0:T(8,128)(2,1)} %collective-permute-done.1.refs_3_), channel_id=1, source_target_pairs={{0,1},{1,0},{2,3},{3,2},{4,5},{5,4},{6,7},{7,6},{8,9},{9,8},{10,11... | collective-permute-start | bytes 491528 | tf_op jit(solution)/shard_map/ppermute | solution.py:65
  53.5 40.1 %copy-start.13 = (bf16[32,2560]{1,0:T(8,128)(2,1)}, bf16[32,2560]{1,0:T(8,128)(2,1)S(1)}, u32[]{:S(2)}) copy-start(bf16[32,2560]{1,0:T(8,128)(2,1)S(1)} %collective-permute-done.15.refs_17_) | copy-start | bytes 491524
  53.5 10.0 %collective-permute-start.13 = (bf16[32,2560]{1,0:T(8,128)(2,1)S(1)}, bf16[32,2560]{1,0:T(8,128)(2,1)S(1)}, u32[]{:S(2)}, u32[]{:S(2)}) collective-permute-start(bf16[32,2560]{1,0:T(8,128)(2,1)S(1)} %collective-permute-done.2.refs_4_), channel_id=1, source_target_pairs={{0,16},{1,17},{2,18},{3,19},{4,20},{5,21},{6,22},{7,23},{8,24},{9,... | collective-permute-start | bytes 491528 | tf_op jit(solution)/shard_map/ppermute | solution.py:65
  55.6 38.0 %copy-start.14 = (bf16[32,2560]{1,0:T(8,128)(2,1)}, bf16[32,2560]{1,0:T(8,128)(2,1)S(1)}, u32[]{:S(2)}) copy-start(bf16[32,2560]{1,0:T(8,128)(2,1)S(1)} %collective-permute-done.6.refs_8_) | copy-start | bytes 491524
  55.6 8.4 %collective-permute-start.36 = (bf16[1,1,1,1,72,256]{5,4,3,2,1,0:T(8,128)(2,1)S(1)}, bf16[1,1,1,1,72,256]{5,4,3,2,1,0:T(8,128)(2,1)S(1)}, u32[]{:S(2)}, u32[]{:S(2)}) collective-permute-start(bf16[1,1,1,1,72,256]{5,4,3,2,1,0:T(8,128)(2,1)S(1)} %dynamic-slice_convert_fusion.4), channel_id=1, source_target_pairs={{0,16},{1,17},{2,18},{3,19},{4,20},{5,21},{6,22},{7,23},{8,24},{9,... | collective-permute-start | bytes 110600 | tf_op jit(solution)/shard_map/ppermute | solution.py:65
  61.7 31.9 %copy-start.16 = (bf16[32,2560]{1,0:T(8,128)(2,1)}, bf16[32,2560]{1,0:T(8,128)(2,1)S(1)}, u32[]{:S(2)}) copy-start(bf16[32,2560]{1,0:T(8,128)(2,1)S(1)} %collective-permute-done.10.refs_12_) | copy-start | bytes 491524
  61.7 5.3 %collective-permute-start.12 = (bf16[32,2560]{1,0:T(8,128)(2,1)S(1)}, bf16[32,2560]{1,0:T(8,128)(2,1)S(1)}, u32[]{:S(2)}, u32[]{:S(2)}) collective-permute-start(bf16[32,2560]{1,0:T(8,128)(2,1)S(1)} %collective-permute-done.2.refs_4_), channel_id=1, source_target_pairs={{0,1},{1,0},{2,3},{3,2},{4,5},{5,4},{6,7},{7,6},{8,9},{9,8},{10,11... | collective-permute-start | bytes 491528 | tf_op jit(solution)/shard_map/ppermute | solution.py:65
  63.4 30.2 %copy-start.18 = (bf16[32,2560]{1,0:T(8,128)(2,1)}, bf16[32,2560]{1,0:T(8,128)(2,1)S(1)}, u32[]{:S(2)}) copy-start(bf16[32,2560]{1,0:T(8,128)(2,1)S(1)} %collective-permute-done.13.refs_15_) | copy-start | bytes 491524
  63.5 7.2 %collective-permute-start.16 = (bf16[32,2560]{1,0:T(8,128)(2,1)}, bf16[32,2560]{1,0:T(8,128)(2,1)S(1)}, u32[]{:S(2)}, u32[]{:S(2)}) collective-permute-start(bf16[32,2560]{1,0:T(8,128)(2,1)} %collective-permute-done.refs_2_), channel_id=1, source_target_pairs={{0,8},{1,9},{2,10},{3,11},{4,12},{5,13},{6,14},{7,15},{8,0},{9,1},... | collective-permute-start | bytes 491528 | tf_op jit(solution)/shard_map/ppermute | solution.py:65
  63.5 30.2 %copy-start.15 = (bf16[32,2560]{1,0:T(8,128)(2,1)}, bf16[32,2560]{1,0:T(8,128)(2,1)S(1)}, u32[]{:S(2)}) copy-start(bf16[32,2560]{1,0:T(8,128)(2,1)S(1)} %collective-permute-done.7.refs_9_) | copy-start | bytes 491524
  63.5 8.7 %collective-permute-start.17 = (bf16[32,2560]{1,0:T(8,128)(2,1)}, bf16[32,2560]{1,0:T(8,128)(2,1)S(1)}, u32[]{:S(2)}, u32[]{:S(2)}) collective-permute-start(bf16[32,2560]{1,0:T(8,128)(2,1)} %collective-permute-done.1.refs_3_), channel_id=1, source_target_pairs={{0,8},{1,9},{2,10},{3,11},{4,12},{5,13},{6,14},{7,15},{8,0},{9,1},... | collective-permute-start | bytes 491528 | tf_op jit(solution)/shard_map/ppermute | solution.py:65
  64.0 29.7 %copy-start.17 = (bf16[32,2560]{1,0:T(8,128)(2,1)}, bf16[32,2560]{1,0:T(8,128)(2,1)S(1)}, u32[]{:S(2)}) copy-start(bf16[32,2560]{1,0:T(8,128)(2,1)S(1)} %collective-permute-done.9.refs_11_) | copy-start | bytes 491524
  64.0 8.8 %collective-permute-start.18 = (bf16[32,2560]{1,0:T(8,128)(2,1)S(1)}, bf16[32,2560]{1,0:T(8,128)(2,1)S(1)}, u32[]{:S(2)}, u32[]{:S(2)}) collective-permute-start(bf16[32,2560]{1,0:T(8,128)(2,1)S(1)} %collective-permute-done.2.refs_4_), channel_id=1, source_target_pairs={{0,8},{1,9},{2,10},{3,11},{4,12},{5,13},{6,14},{7,15},{8,0},{9,1},... | collective-permute-start | bytes 491528 | tf_op jit(solution)/shard_map/ppermute | solution.py:65
  64.1 6.5 %collective-permute-start.5 = (bf16[32,2560]{1,0:T(8,128)(2,1)S(1)}, bf16[32,2560]{1,0:T(8,128)(2,1)S(1)}, u32[]{:S(2)}, u32[]{:S(2)}) collective-permute-start(bf16[32,2560]{1,0:T(8,128)(2,1)S(1)} %collective-permute-done.3.refs_5_), channel_id=1, source_target_pairs={{0,16},{1,17},{2,18},{3,19},{4,20},{5,21},{6,22},{7,23},{8,24},{9,... | collective-permute-start | bytes 491528 | tf_op jit(solution)/shard_map/ppermute | solution.py:65
  67.0 26.7 %copy-start.19 = (bf16[32,2560]{1,0:T(8,128)(2,1)}, bf16[32,2560]{1,0:T(8,128)(2,1)S(1)}, u32[]{:S(2)}) copy-start(bf16[32,2560]{1,0:T(8,128)(2,1)S(1)} %collective-permute-done.12.refs_14_) | copy-start | bytes 491524
  67.0 7.3 %collective-permute-start.19 = (bf16[32,2560]{1,0:T(8,128)(2,1)S(1)}, bf16[32,2560]{1,0:T(8,128)(2,1)S(1)}, u32[]{:S(2)}, u32[]{:S(2)}) collective-permute-start(bf16[32,2560]{1,0:T(8,128)(2,1)S(1)} %collective-permute-done.3.refs_5_), channel_id=1, source_target_pairs={{0,8},{1,9},{2,10},{3,11},{4,12},{5,13},{6,14},{7,15},{8,0},{9,1},... | collective-permute-start | bytes 491528 | tf_op jit(solution)/shard_map/ppermute | solution.py:65
  70.6 23.1 %copy-start.23 = (bf16[32,2560]{1,0:T(8,128)(2,1)}, bf16[32,2560]{1,0:T(8,128)(2,1)S(1)}, u32[]{:S(2)}) copy-start(bf16[32,2560]{1,0:T(8,128)(2,1)S(1)} %collective-permute-done.5.refs_7_) | copy-start | bytes 491524
  70.6 3.7 %collective-permute-start.20 = (bf16[32,2560]{1,0:T(8,128)(2,1)S(1)}, bf16[32,2560]{1,0:T(8,128)(2,1)S(1)}, u32[]{:S(2)}, u32[]{:S(2)}) collective-permute-start(bf16[32,2560]{1,0:T(8,128)(2,1)S(1)} %collective-permute-done.4.refs_6_), channel_id=1, source_target_pairs={{0,8},{1,9},{2,10},{3,11},{4,12},{5,13},{6,14},{7,15},{8,0},{9,1},... | collective-permute-start | bytes 491528 | tf_op jit(solution)/shard_map/ppermute | solution.py:65
  70.6 23.1 %copy-start.20 = (bf16[32,2560]{1,0:T(8,128)(2,1)}, bf16[32,2560]{1,0:T(8,128)(2,1)S(1)}, u32[]{:S(2)}) copy-start(bf16[32,2560]{1,0:T(8,128)(2,1)S(1)} %collective-permute-done.16.refs_18_) | copy-start | bytes 491524
  70.6 6.7 %collective-permute-start.8 = (bf16[32,2560]{1,0:T(8,128)(2,1)S(1)}, bf16[32,2560]{1,0:T(8,128)(2,1)}, u32[]{:S(2)}, u32[]{:S(2)}) collective-permute-start(bf16[32,2560]{1,0:T(8,128)(2,1)S(1)} %collective-permute-done.6.refs_8_), channel_id=1, source_target_pairs={{0,16},{1,17},{2,18},{3,19},{4,20},{5,21},{6,22},{7,23},{8,24},{9,... | collective-permute-start | bytes 491528 | tf_op jit(solution)/shard_map/ppermute | solution.py:65
  72.2 21.5 %copy-start.21 = (bf16[32,2560]{1,0:T(8,128)(2,1)}, bf16[32,2560]{1,0:T(8,128)(2,1)S(1)}, u32[]{:S(2)}) copy-start(bf16[32,2560]{1,0:T(8,128)(2,1)S(1)} %collective-permute-done.17.refs_19_) | copy-start | bytes 491524
  72.2 7.2 %collective-permute-start.11 = (bf16[32,2560]{1,0:T(8,128)(2,1)S(1)}, bf16[32,2560]{1,0:T(8,128)(2,1)}, u32[]{:S(2)}, u32[]{:S(2)}) collective-permute-start(bf16[32,2560]{1,0:T(8,128)(2,1)S(1)} %collective-permute-done.10.refs_12_), channel_id=1, source_target_pairs={{0,1},{1,0},{2,3},{3,2},{4,5},{5,4},{6,7},{7,6},{8,9},{9,8},{10,11... | collective-permute-start | bytes 491528 | tf_op jit(solution)/shard_map/ppermute | solution.py:65
  72.7 20.9 %copy-start.22 = (bf16[32,2560]{1,0:T(8,128)(2,1)}, bf16[32,2560]{1,0:T(8,128)(2,1)S(1)}, u32[]{:S(2)}) copy-start(bf16[32,2560]{1,0:T(8,128)(2,1)S(1)} %collective-permute-done.18.refs_20_) | copy-start | bytes 491524
  72.7 9.3 %collective-permute-start.14 = (bf16[32,2560]{1,0:T(8,128)(2,1)S(1)}, bf16[32,2560]{1,0:T(8,128)(2,1)}, u32[]{:S(2)}, u32[]{:S(2)}) collective-permute-start(bf16[32,2560]{1,0:T(8,128)(2,1)S(1)} %collective-permute-done.13.refs_15_), channel_id=1, source_target_pairs={{0,1},{1,0},{2,3},{3,2},{4,5},{5,4},{6,7},{7,6},{8,9},{9,8},{10,11... | collective-permute-start | bytes 491528 | tf_op jit(solution)/shard_map/ppermute | solution.py:65
  74.3 19.4 %copy-start.24 = (bf16[32,2560]{1,0:T(8,128)(2,1)}, bf16[32,2560]{1,0:T(8,128)(2,1)S(1)}, u32[]{:S(2)}) copy-start(bf16[32,2560]{1,0:T(8,128)(2,1)S(1)} %collective-permute-done.19.refs_21_) | copy-start | bytes 491524
  74.3 7.8 %collective-permute-start.22 = (bf16[32,2560]{1,0:T(8,128)(2,1)S(1)}, bf16[32,2560]{1,0:T(8,128)(2,1)S(1)}, u32[]{:S(2)}, u32[]{:S(2)}) collective-permute-start(bf16[32,2560]{1,0:T(8,128)(2,1)S(1)} %collective-permute-done.6.refs_8_), channel_id=1, source_target_pairs={{0,8},{1,9},{2,10},{3,11},{4,12},{5,13},{6,14},{7,15},{8,0},{9,1},... | collective-permute-start | bytes 491528 | tf_op jit(solution)/shard_map/ppermute | solution.py:65
  74.3 9.1 %copy-start.25 = (bf16[32,2560]{1,0:T(8,128)(2,1)}, bf16[32,2560]{1,0:T(8,128)(2,1)S(1)}, u32[]{:S(2)}) copy-start(bf16[32,2560]{1,0:T(8,128)(2,1)S(1)} %collective-permute-done.20.refs_22_) | copy-start | bytes 491524
  74.4 8.3 %collective-permute-start.26 = (bf16[32,2560]{1,0:T(8,128)(2,1)S(1)}, bf16[32,2560]{1,0:T(8,128)(2,1)S(1)}, u32[]{:S(2)}, u32[]{:S(2)}) collective-permute-start(bf16[32,2560]{1,0:T(8,128)(2,1)S(1)} %collective-permute-done.10.refs_12_), channel_id=1, source_target_pairs={{0,8},{1,9},{2,10},{3,11},{4,12},{5,13},{6,14},{7,15},{8,0},{9,1},... | collective-permute-start | bytes 491528 | tf_op jit(solution)/shard_map/ppermute | solution.py:65
  77.3 5.4 %collective-permute-start.29 = (bf16[32,2560]{1,0:T(8,128)(2,1)S(1)}, bf16[32,2560]{1,0:T(8,128)(2,1)S(1)}, u32[]{:S(2)}, u32[]{:S(2)}) collective-permute-start(bf16[32,2560]{1,0:T(8,128)(2,1)S(1)} %collective-permute-done.13.refs_15_), channel_id=1, source_target_pairs={{0,8},{1,9},{2,10},{3,11},{4,12},{5,13},{6,14},{7,15},{8,0},{9,1},... | collective-permute-start | bytes 491528 | tf_op jit(solution)/shard_map/ppermute | solution.py:65
  79.4 3.8 %collective-permute-start.23 = (bf16[32,2560]{1,0:T(8,128)(2,1)S(1)}, bf16[32,2560]{1,0:T(8,128)(2,1)S(1)}, u32[]{:S(2)}, u32[]{:S(2)}) collective-permute-start(bf16[32,2560]{1,0:T(8,128)(2,1)S(1)} %collective-permute-done.7.refs_9_), channel_id=1, source_target_pairs={{0,8},{1,9},{2,10},{3,11},{4,12},{5,13},{6,14},{7,15},{8,0},{9,1},... | collective-permute-start | bytes 491528 | tf_op jit(solution)/shard_map/ppermute | solution.py:65
  82.1 1.4 collective-permute-start.25
  82.1 11.4 %collective-permute-start.28 = (bf16[32,2560]{1,0:T(8,128)(2,1)S(1)}, bf16[32,2560]{1,0:T(8,128)(2,1)}, u32[]{:S(2)}, u32[]{:S(2)}) collective-permute-start(bf16[32,2560]{1,0:T(8,128)(2,1)S(1)} %collective-permute-done.12.refs_14_), channel_id=1, source_target_pairs={{0,8},{1,9},{2,10},{3,11},{4,12},{5,13},{6,14},{7,15},{8,0},{9,1},... | collective-permute-start | bytes 491528 | tf_op jit(solution)/shard_map/ppermute | solution.py:65
  82.7 10.8 %collective-permute-start.21 = (bf16[32,2560]{1,0:T(8,128)(2,1)S(1)}, bf16[32,2560]{1,0:T(8,128)(2,1)}, u32[]{:S(2)}, u32[]{:S(2)}) collective-permute-start(bf16[32,2560]{1,0:T(8,128)(2,1)S(1)} %collective-permute-done.5.refs_7_), channel_id=1, source_target_pairs={{0,8},{1,9},{2,10},{3,11},{4,12},{5,13},{6,14},{7,15},{8,0},{9,1},... | collective-permute-start | bytes 491528 | tf_op jit(solution)/shard_map/ppermute | solution.py:65
  82.8 10.8 %collective-permute-start.24 = (bf16[32,2560]{1,0:T(8,128)(2,1)}, bf16[32,2560]{1,0:T(8,128)(2,1)}, u32[]{:S(2)}, u32[]{:S(2)}) collective-permute-start(bf16[32,2560]{1,0:T(8,128)(2,1)} %collective-permute-done.8.refs_10_), channel_id=1, source_target_pairs={{0,8},{1,9},{2,10},{3,11},{4,12},{5,13},{6,14},{7,15},{8,0},{9,1},... | collective-permute-start | bytes 491528 | tf_op jit(solution)/shard_map/ppermute | solution.py:65
  83.2 10.3 %collective-permute-start.27 = (bf16[32,2560]{1,0:T(8,128)(2,1)}, bf16[32,2560]{1,0:T(8,128)(2,1)}, u32[]{:S(2)}, u32[]{:S(2)}) collective-permute-start(bf16[32,2560]{1,0:T(8,128)(2,1)} %collective-permute-done.11.refs_13_), channel_id=1, source_target_pairs={{0,8},{1,9},{2,10},{3,11},{4,12},{5,13},{6,14},{7,15},{8,0},{9,1},... | collective-permute-start | bytes 491528 | tf_op jit(solution)/shard_map/ppermute | solution.py:65
  83.5 10.1 %collective-permute-start.30 = (bf16[32,2560]{1,0:T(8,128)(2,1)}, bf16[32,2560]{1,0:T(8,128)(2,1)}, u32[]{:S(2)}, u32[]{:S(2)}) collective-permute-start(bf16[32,2560]{1,0:T(8,128)(2,1)} %collective-permute-done.14.refs_16_), channel_id=1, source_target_pairs={{0,8},{1,9},{2,10},{3,11},{4,12},{5,13},{6,14},{7,15},{8,0},{9,1},... | collective-permute-start | bytes 491528 | tf_op jit(solution)/shard_map/ppermute | solution.py:65
  85.4 46.0 %all-to-all-start = ((bf16[32,64,256]{2,1,0:T(8,128)(2,1)}), bf16[32,64,256]{2,1,0:T(8,128)(2,1)S(1)}, u32[]{:S(2)}, u32[]{:S(2)}) async-start(bf16[32,64,256]{2,1,0:T(8,128)(2,1)} %broadcast_in_dim.51), calls=%async_computation | async-start | bytes 2097152 | tf_op jit(solution)/shard_map/all_to_all | solution.py:84
  131.4 27.3 %all-to-all-start.1 = ((f32[32,8,512]{2,1,0:T(8,128)}), f32[32,8,512]{2,1,0:T(8,128)S(1)}, u32[]{:S(2)}, u32[]{:S(2)}) async-start(f32[32,8,512]{2,1,0:T(8,128)} %bitcast.5), calls=%async_computation.1 | async-start | bytes 1048576 | tf_op jit(solution)/shard_map/all_to_all | solution.py:84
  150.6 8.1 %copy-start.1 = (f32[512,512]{1,0:T(8,128)S(1)}, f32[512,512]{1,0:T(8,128)}, u32[]{:S(2)}) copy-start(f32[512,512]{1,0:T(8,128)} %get-tuple-element.21.inv) | copy-start | bytes 3145732
  160.5 21.9 %all-to-all-start.2 = ((bf16[32,16,512]{2,1,0:T(8,128)(2,1)}), bf16[32,16,512]{2,1,0:T(8,128)(2,1)S(1)}, u32[]{:S(2)}, u32[]{:S(2)}) async-start(bf16[32,16,512]{2,1,0:T(8,128)(2,1)} %broadcast_in_dim.52), calls=%async_computation.2 | async-start | bytes 1048576 | tf_op jit(solution)/shard_map/all_to_all | solution.py:84
  (7 other events, 13.4 us)

commit v5 on v4

--- a/solution.py
+++ b/solution.py
@@ -60,15 +60,27 @@
         c, x = self.n["c"], self.n["x"]
         return {"y": row // c, "c": row % c, "z": col // x, "x": col % x}
 
+    def paired(self, dim):
+        return self.n[dim] & (self.n[dim] - 1) == 0
+
+    def source(self, at, dim, by):
+        return at ^ by if self.paired(dim) else (at - by) % self.n[dim]
+
     def shift(self, value, dim, by):
-        to = np.roll(self.ids, -by, axis=list(self.n).index(dim))
+        axis = list(self.n).index(dim)
+        if self.paired(dim):
+            to = np.take(self.ids, np.arange(self.n[dim]) ^ by, axis=axis)
+        else:
+            to = np.roll(self.ids, -by, axis=axis)
         return lax.ppermute(value, AXES, list(zip(self.ids.ravel(), to.ravel())))
 
     def spread(self, value, dim):
         return [self.shift(value, dim, s) for s in range(1, self.n[dim])]
 
     def take(self, chunks, dim, by=0):
-        at = (self.here()[dim] + by) % self.n[dim]
+        at = self.here()[dim]
+        if by:
+            at = at ^ by if self.paired(dim) else (at + by) % self.n[dim]
         return lax.dynamic_index_in_dim(chunks, at, list(self.n).index(dim), keepdims=True)
 
     def sends(self, chunks, dim):
@@ -94,8 +106,7 @@
     cap = out.shape[0]
     width = points.shape[1]
 
-    def copies(i):
-        base = pl.multiple_of((slots[0, i] // ALIGN) * ALIGN, ALIGN)
+    def copies(i, base):
         return (
             pltpu.make_async_copy(
                 points.at[pl.ds(base, ALIGN), :], pbuf.at[pl.ds(i * ALIGN, ALIGN), :], psem.at[i]
@@ -106,7 +117,7 @@
         )
 
     for i in range(cap):
-        for copy in copies(i):
+        for copy in copies(i, pl.multiple_of((slots[0, i] // ALIGN) * ALIGN, ALIGN)):
             copy.start()
     r = lax.broadcasted_iota(jnp.int32, (cap, cap * ALIGN), 0)
     q = lax.broadcasted_iota(jnp.int32, (cap, cap * ALIGN), 1)
@@ -115,7 +126,7 @@
         target = jnp.where(r == i, slots[0, i] % ALIGN + i * ALIGN, target)
     pick = (q == target).astype(f32).astype(bf16)
     for i in range(cap):
-        for copy in copies(i):
+        for copy in copies(i, 0):
             copy.wait()
     rows = dot(pick, pbuf[...]).astype(bf16)
     out[:, :width] = normalize(rows)
@@ -236,100 +247,118 @@
     )(turned, points, factor, targets)
 
 
+GROUP = 64
+
+
 def across(v):
     return jnp.broadcast_to(v, (8, TILE))
 
 
-def base8(tile, lane0):
-    e = [[None] * 8 for _ in range(8)]
+def lanes(tile, lane0):
+    return [across(tile[:, lane0 + s : lane0 + s + 1]) for s in range(8)]
+
+
+def eliminate(tile, side, others, lane0, rowid, scratch):
+    col = lanes(tile, lane0)
     for s in range(8):
-        col = across(tile[:, lane0 + s : lane0 + s + 1])
-        for t in range(s, 8):
-            e[t][s] = across(col[t : t + 1, :])
-    x = [[None] * 8 for _ in range(8)]
-    low = [[None] * 8 for _ in range(8)]
+        scratch[8 * s : 8 * s + 8, :] = col[s]
+    e = [
+        [scratch[pl.ds(8 * s + t, 8, stride=0), :] if t >= s else None for s in range(8)]
+        for t in range(8)
+    ]
+    below = [lanes(t, lane0) for t, _ in others]
+    out = [list(o) for o in others]
+    scale = None
     for s in range(8):
         r = lax.rsqrt(e[s][s])
+        scale = r if s == 0 else jnp.where(rowid == s, r, scale)
+        low = [None] * 8
         for t in range(s + 1, 8):
-            low[t][s] = e[t][s] * r
+            low[t] = e[t][s] * r
         for u in range(s + 1, 8):
             for t in range(u, 8):
-                e[t][u] = e[t][u] - low[t][s] * low[u][s]
-        for c in range(s):
-            acc = low[s][c] * x[c][c]
-            for u in range(c + 1, s):
-                acc = acc + low[s][u] * x[u][c]
-            x[s][c] = -(r * acc)
-        x[s][s] = r
-    return x
-
-
-def columns(x, rowid):
-    out = []
-    for s in range(8):
-        c = jnp.where(rowid == s, x[s][s], 0.0)
-        for t in range(s + 1, 8):
-            c = jnp.where(rowid == t, x[t][s], c)
-        out.append(c)
-    return out
-
-
-def diagonal_block(s_ref, w_ref):
-    n, group = TILE, 32
+                e[t][u] = e[t][u] - low[t] * low[u]
+        row, wide = across(tile[s : s + 1, :]) * r, across(side[s : s + 1, :]) * r
+        if s < 7:
+            mine = jnp.where(rowid > s, col[s], 0.0) * r
+            tile = tile - mine * row
+            side = side - mine * wide
+            for u in range(s + 1, 8):
+                col[u] = col[u] - mine * low[u]
+        for k, b in enumerate(below):
+            m = b[s] * r
+            out[k][0] = out[k][0] - m * row
+            out[k][1] = out[k][1] - m * wide
+            for u in range(s + 1, 8):
+                b[u] = b[u] - m * low[u]
+    return tile * scale, side * scale, out
+
+
+def diagonal_block(s_ref, w_ref, scratch):
+    n, count = TILE, GROUP // 8
     rowid = lax.broadcasted_iota(jnp.int32, (8, n), 0)
     ri = lax.broadcasted_iota(jnp.int32, (n, n), 0)
     ci = lax.broadcasted_iota(jnp.int32, (n, n), 1)
     w_ref[...] = jnp.where(ri == ci, 1.0, 0.0).astype(f32)
-    for g in range(0, n, group):
-        tiles = [s_ref[g + 8 * i : g + 8 * i + 8, :] for i in range(4)]
-        sides = [w_ref[g + 8 * i : g + 8 * i + 8, :] for i in range(4)]
-        for j in range(4):
-            lane0 = g + 8 * j
-            x = base8(tiles[j], lane0)
-            cols = columns(x, rowid)
-            u = cols[0] * across(tiles[j][0:1, :])
-            q = cols[0] * across(sides[j][0:1, :])
-            for s in range(1, 8):
-                u = u + cols[s] * across(tiles[j][s : s + 1, :])
-                q = q + cols[s] * across(sides[j][s : s + 1, :])
-            tiles[j], sides[j] = u, q
-            for i in range(j + 1, 4):
-                b = [across(tiles[i][:, lane0 + k : lane0 + k + 1]) for k in range(8)]
-                t, v = tiles[i], sides[i]
-                for s in range(8):
-                    m = x[s][0] * b[0]
-                    for k in range(1, s + 1):
-                        m = m + x[s][k] * b[k]
-                    t = t - m * across(u[s : s + 1, :])
-                    v = v - m * across(q[s : s + 1, :])
-                tiles[i], sides[i] = t, v
-        ug = jnp.concatenate(tiles, 0)
-        vg = jnp.concatenate(sides, 0)
-        w_ref[g : g + group, :] = vg
-        if g + group < n:
-            lo = g + group
+    for g in range(0, n, GROUP):
+        tiles = [s_ref[g + 8 * i : g + 8 * i + 8, :] for i in range(count)]
+        sides = [w_ref[g + 8 * i : g + 8 * i + 8, :] for i in range(count)]
+        for j in range(count):
+            rest = list(zip(tiles[j + 1 :], sides[j + 1 :]))
+            tiles[j], sides[j], rest = eliminate(
+                tiles[j], sides[j], rest, g + 8 * j, rowid, scratch.at[j % 2]
+            )
+            tiles[j + 1 :] = [t for t, _ in rest]
+            sides[j + 1 :] = [v for _, v in rest]
+        ug, vg = jnp.concatenate(tiles, 0), jnp.concatenate(sides, 0)
+        w_ref[g : g + GROUP, :] = vg
+        if g + GROUP < n:
+            lo = g + GROUP
             upd = dot(ug, jnp.concatenate([ug, vg], 1), 0, 0, exact=True)
             s_ref[lo:, :] = s_ref[lo:, :] - upd[lo:, :n]
             w_ref[lo:, :] = w_ref[lo:, :] - upd[lo:, n:]
 
 
-def factor_kernel(first, last, a_in, r_in, a_ref, r_ref, s_ref, w_ref):
+def factor_kernel(first, last, a_in, r_in, a_ref, r_ref, s_ref, w_ref, scratch):
     n, blocks = TILE, BLOCK // TILE
+    mul = functools.partial(dot, exact=True)
     a_ref[...] = a_in[...]
     r_ref[...] = r_in[...]
+
+    def finish(k, inv, u):
+        o, p, q = n * k, n * (k + 1), n * (k + 2)
+        if k:
+            r_ref[o:p, :o] = mul(inv, r_ref[o:p, :o])
+        r_ref[o:p, o:p] = inv
+        if k < blocks - 1:
+            done = r_ref[o:p, :p]
+            r_ref[p:q, :p] = r_ref[p:q, :p] - mul(u, done, 0, 0)
+            if k < blocks - 2:
+                v = mul(inv, a_ref[o:p, q:])
+                a_ref[p:q, q:] = a_ref[p:q, q:] - mul(u, v, 0, 0)
+                a_ref[q:, q:] = a_ref[q:, q:] - mul(v, v, 0, 0)
+                r_ref[q:, :p] = r_ref[q:, :p] - mul(v, done, 0, 0)
+
+    s_ref[first % 2] = a_ref[n * first : n * first + n, n * first : n * first + n]
+    if first:
+        o, p = n * (first - 1), n * first
+        finish(first - 1, r_ref[o:p, o:p], a_ref[o:p, p : p + n])
     for k in range(first, last):
-        o = n * k
-        s_ref[...] = a_ref[o : o + n, o : o + n]
-        diagonal_block(s_ref, w_ref)
-        inv = w_ref[...]
-        if k:
-            r_ref[o : o + n, :o] = dot(inv, r_ref[o : o + n, :o], exact=True)
-        r_ref[o : o + n, o : o + n] = inv
+        o, p, q = n * k, n * (k + 1), n * (k + 2)
+        w = w_ref.at[k % 2]
+        diagonal_block(s_ref.at[k % 2], w, scratch)
+        inv, u = w[...], None
         if k < blocks - 1:
-            u = dot(inv, a_ref[o : o + n, o + n :], exact=True)
-            wk = r_ref[o : o + n, : o + n]
-            a_ref[o + n :, o + n :] = a_ref[o + n :, o + n :] - dot(u, u, 0, 0, exact=True)
-            r_ref[o + n :, : o + n] = r_ref[o + n :, : o + n] - dot(u, wk, 0, 0, exact=True)
+            u = mul(inv, a_ref[o:p, p:q])
+            ahead = a_ref[p:q, p:q] - mul(u, u, 0, 0)
+            if k + 1 < last:
+                s_ref[(k + 1) % 2] = ahead
+            else:
+                a_ref[p:q, p:q] = ahead
+                a_ref[o:p, p:q] = u
+                r_ref[o:p, o:p] = inv
+        if k + 1 < last or k == blocks - 1:
+            finish(k, inv, u)
 
 
 def factor_step(a, r, first, last):
@@ -338,7 +367,7 @@
         out_shape=(jax.ShapeDtypeStruct(a.shape, f32),) * 2,
         in_specs=[VMEM] * 2,
         out_specs=(VMEM,) * 2,
-        scratch_shapes=[pltpu.VMEM((TILE, TILE), f32)] * 2,
+        scratch_shapes=[pltpu.VMEM((2, TILE, TILE), f32)] * 2 + [pltpu.VMEM((2, 64, TILE), f32)],
         input_output_aliases={0: 0, 1: 1},
         cost_estimate=pl.CostEstimate(
             flops=12 * 10**9, bytes_accessed=4 * 10**6, transcendentals=0
@@ -401,6 +430,38 @@
             flops=4 * 10**9, bytes_accessed=8 * 10**6, transcendentals=0
         ),
     )(inv, high, low)
+
+
+def parcel_kernel(parts, inv, norm, out):
+    t = parts.shape[1]
+    z = parts[0]
+    for k in range(1, parts.shape[0]):
+        z = z + parts[k]
+    cross = dot(z, inv[...], 1, 1, exact=True)
+    n0 = norm[...].astype(bf16).astype(f32)
+    n1 = (norm[...] - n0).astype(bf16).astype(f32)
+    n2 = norm[...] - n0 - n1
+    row = lax.broadcasted_iota(jnp.int32, (out.shape[1], cross.shape[1]), 0)
+    own = jnp.concatenate([cross] * (out.shape[1] // t), 0)
+    for k, v in enumerate((n0, n1, n2)):
+        own = jnp.where(row == t + k, jnp.broadcast_to(v, own.shape), own)
+    own = own.astype(bf16)
+    for k in range(out.shape[0]):
+        out[k] = own
+
+
+def make_parcel(parts, inv, norm):
+    devices, t, block = parts.shape
+    rows = t * -(-(-(-(t + 3) // 16) * 16) // t)
+    return pl.pallas_call(
+        parcel_kernel,
+        out_shape=jax.ShapeDtypeStruct((devices, rows, block), bf16),
+        in_specs=[VMEM] * 3,
+        out_specs=VMEM,
+        cost_estimate=pl.CostEstimate(
+            flops=10**8, bytes_accessed=2 * 10**6, transcendentals=0
+        ),
+    )(parts, inv, norm)
 
 
 def finish_kernel(base, turned, coef, out):
@@ -487,7 +548,7 @@
     shifts = np.array(origins)
     dev = jnp.zeros((len(origins),), jnp.int32)
     for k, dim in enumerate("yczx"):
-        dev = dev * n[dim] + (me[dim] - shifts[:, k]) % n[dim]
+        dev = dev * n[dim] + grid.source(me[dim], dim, jnp.asarray(shifts[:, k], jnp.int32))
     ends = jnp.cumsum(pivot_counts)
     onehot = dev[:, None] == jnp.arange(devices, dtype=jnp.int32)[None, :]
     count = jnp.sum(jnp.where(onehot, pivot_counts[None, :], 0), axis=1)
@@ -508,7 +569,6 @@
     coef_held = coef_held.reshape(held, nt)
     t = nt // devices
     z_parts = grid.exchange(z.reshape(devices, t, BLOCK))
-    z_own = jnp.sum(z_parts, axis=0)
 
     inverse = jnp.zeros((BLOCK, BLOCK), f32)
     middle = BLOCK // TILE // 2
@@ -516,12 +576,8 @@
     ridged, inverse = factor_step(ridged, inverse, middle, BLOCK // TILE)
 
     new_columns, new_turned, norm_own = make_columns(inverse, high, low)
-    cross_own = dot(z_own, inverse, 1, 1, exact=True)
-    nh, nl = split(norm_own)
-    nl2 = (norm_own - nh.astype(f32) - nl.astype(f32)).astype(bf16)
-    late = jnp.concatenate([cross_own.astype(bf16), nh, nl, nl2], axis=0)
-    late = jnp.pad(late, ((0, -late.shape[0] % 16), (0, 0)))
-    every = grid.everywhere(late).astype(f32)
+    parcel = make_parcel(z_parts, inverse, norm_own)
+    every = grid.exchange(parcel).astype(f32)
     norm_new = jnp.sum(every[:, t : t + 3], axis=(0, 1))
     coef_new = (every[:, :t].reshape(nt, BLOCK) / (norm_new + damping)[None, :]).astype(bf16)
 

time: 188 us -> 176 us (0.936)
  Pallas kernels: 65.2 us -> 60.8 us
  starting transfers between devices: 49.3 us -> 46.8 us
  waiting for transfers between devices: 43.9 us -> 41.4 us
    pallas_call x2, Pallas kernels: 28 us -> 20.4 us  [factor_step(): pl.pallas_call(functools.partial(factor_kernel, first, last), out_shape=(...]
    all_to_all x3, starting transfers between devices: 19.6 us -> 14.8 us  [exchange(): return lax.all_to_all(parts, AXES, 0, 0, tiled=True)]
    pallas_call x0 -> x1, Pallas kernels: none -> 3.16 us  [make_parcel(): pl.pallas_call(parcel_kernel, out_shape=jax.ShapeDtypeStruct((devices, ro...]
    ppermute x37, waiting for transfers between devices: 35 us -> 32.3 us  [shift(): return lax.ppermute(value, AXES, list(zip(self.ids.ravel(), to.ravel())))]
    ppermute x37, starting transfers between devices: 29.6 us -> 31.9 us  [shift(): return lax.ppermute(value, AXES, list(zip(self.ids.ravel(), to.ravel())))]
    dot_general x3 -> x2, matrix products: 10.9 us -> 9.73 us  [dot(): lax.dot_general(a, b, (((da,), (db,)), ((), ())), precision=lax.Precision...]
  transfers between devices with their start and end apart: 40 -> 40, of which waited for: 13 -> 14; matrix products, arithmetic and copies ran while one was open for 8% -> 8% of each run, Pallas kernels for 31% -> 28%
where the time goes in v5:
time: 176 us; the launch traced here: 175 us
  Pallas kernels  60.8 us (35%)
  starting transfers between devices  46.8 us (27%)
  waiting for transfers between devices  41.4 us (24%)
  other arithmetic  10 us (6%)
  matrix products  9.73 us (6%)
  local copies, waits for them, and re-layouts  5.52 us (3%)
    ppermute x37, waiting for transfers between devices, shift(): return lax.ppermute(value, AXES, list(zip(self.ids.ravel(), to.ravel())))  32.3 us
    ppermute x37, starting transfers between devices, shift(): return lax.ppermute(value, AXES, list(zip(self.ids.ravel(), to.ravel())))  31.9 us
    pallas_call x2, Pallas kernels, factor_step(): pl.pallas_call(functools.partial(factor_kernel, first, last), out_shape=(...  20.4 us
    all_to_all x3, starting transfers between devices, exchange(): return lax.all_to_all(parts, AXES, 0, 0, tiled=True)  14.8 us
    pallas_call x1, Pallas kernels, downdate(): pl.pallas_call(downdate_kernel, grid=(pts // blk,), out_shape=(jax.ShapeD...  12.7 us
    dot_general x2, matrix products, dot(): lax.dot_general(a, b, (((da,), (db,)), ((), ())), precision=lax.Precision...  9.73 us
    pallas_call x1, Pallas kernels, prepare(): pl.pallas_call(functools.partial(prepare_kernel, len(pieces), width), out...  9.25 us
    all_to_all x3, waiting for transfers between devices, exchange(): return lax.all_to_all(parts, AXES, 0, 0, tiled=True)  9.14 us
  transfers between devices with their start and end apart: 40, of which 14 were waited for; matrix products, arithmetic and copies ran while one was open for 8% of the time, Pallas kernels for 28%

profile of v5, /device:TPU:0, one launch (start us, length us, event | category | flops | bytes accessed | tf_op | source)
XLA Modules:
  0.0 175.4 jit_solution(2631659198199087938)
XLA Ops:
  0.7 4.4 %shard_map.104.refs_1_ = bf16[32,2560]{1,0:T(8,128)(2,1)} custom-call(s32[1,32]{1,0:T(1,128)} %slots.1, bf16[2048,512]{1,0:T(8,128)(2,1)} %points.3, bf16[2048,2048]{1,0:T(8,128)(2,1)} %factor.3), custom_call_target="tpu_custom_call" | custom-call | flops 100000000 | bytes 3000000 | tf_op jit(solution)/shard_map/pallas_call | solution.py:139
  5.1 5.3 %multiply_reduce_fusion = f32[2048]{0:T(1024)S(1)} fusion(bf16[2048,2048]{1,0:T(8,128)(2,1)} %factor.3), kind=kLoop, calls=%fused_computation | loop fusion | flops 12580864 | bytes 8396800 | tf_op jit(solution)/shard_map/reduce_sum | solution.py:498
  10.4 0.5 copy-done
  10.8 2.6 %fusion.8 = f32[2048,256]{1,0:T(8,128)S(1)} fusion(bf16[2048,2048]{1,0:T(8,128)(2,1)S(1)} %copy-done, bf16[2048,256]{1,0:T(8,128)(2,1)S(1)} %copy-done.9), kind=kOutput, calls=%fused_computation.34 | convolution fusion | flops 2147483648 | bytes 11534336 | tf_op jit(solution)/shard_map/dot_general | solution.py:28
  13.7 1.1 fusion.1
  14.8 0.5 collective-permute-start.31
  15.3 2.6 %collective-permute-start = (bf16[32,2560]{1,0:T(8,128)(2,1)}, bf16[32,2560]{1,0:T(8,128)(2,1)}, u32[]{:S(2)}, u32[]{:S(2)}) collective-permute-start(bf16[32,2560]{1,0:T(8,128)(2,1)} %shard_map.104.refs_1_), channel_id=1, source_target_pairs={{0,2},{1,3},{2,0},{3,1},{4,6},{5,7},{6,4},{7,5},{8,10},{9,11},{10,... | collective-permute-start | bytes 491528 | tf_op jit(solution)/shard_map/ppermute | solution.py:75
  17.9 2.6 %collective-permute-start.1 = (bf16[32,2560]{1,0:T(8,128)(2,1)}, bf16[32,2560]{1,0:T(8,128)(2,1)}, u32[]{:S(2)}, u32[]{:S(2)}) collective-permute-start(bf16[32,2560]{1,0:T(8,128)(2,1)} %shard_map.104.refs_1_), channel_id=1, source_target_pairs={{0,4},{1,5},{2,6},{3,7},{4,0},{5,1},{6,2},{7,3},{8,12},{9,13},{10,... | collective-permute-start | bytes 491528 | tf_op jit(solution)/shard_map/ppermute | solution.py:75
  20.5 0.7 copy.19
  21.1 0.8 reduce-window.9
  21.9 0.6 reduce
  22.5 0.7 sub.21
  23.6 1.9 %collective-permute-start.33 = (bf16[2,1,1,2,72,256]{5,4,3,2,1,0:T(8,128)(2,1)S(1)}, bf16[2,1,1,2,72,256]{5,4,3,2,1,0:T(8,128)(2,1)S(1)}, u32[]{:S(2)}, u32[]{:S(2)}) collective-permute-start(bf16[2,1,1,2,72,256]{5,4,3,2,1,0:T(8,128)(2,1)S(1)} %get-tuple-element.36), channel_id=1, source_target_pairs={{0,4},{1,5},{2,6},{3,7},{4,0},{5,1},{6,2},{7,3},{8,12},{9,13},{10,... | collective-permute-start | bytes 442376 | tf_op jit(solution)/shard_map/ppermute | solution.py:75
  25.5 2.5 %collective-permute-start.32 = (bf16[2,1,1,2,72,256]{5,4,3,2,1,0:T(8,128)(2,1)S(1)}, bf16[2,1,1,2,72,256]{5,4,3,2,1,0:T(8,128)(2,1)S(1)}, u32[]{:S(2)}, u32[]{:S(2)}) collective-permute-start(bf16[2,1,1,2,72,256]{5,4,3,2,1,0:T(8,128)(2,1)S(1)} %get-tuple-element.34), channel_id=1, source_target_pairs={{0,2},{1,3},{2,0},{3,1},{4,6},{5,7},{6,4},{7,5},{8,10},{9,11},{10,... | collective-permute-start | bytes 442376 | tf_op jit(solution)/shard_map/ppermute | solution.py:75
  28.0 4.4 %collective-permute-done.34 = bf16[2,1,1,2,72,256]{5,4,3,2,1,0:T(8,128)(2,1)S(1)} collective-permute-done((bf16[2,1,1,2,72,256]{5,4,3,2,1,0:T(8,128)(2,1)S(1)}, bf16[2,1,1,2,72,256]{5,4,3,2,1,0:T(8,128)(2,1)S(1)}, u32[]{:S(2)}, u32[]{:S(2)}) %collective-permute-start.34) | collective-permute-done | bytes 147488 | tf_op jit(solution)/shard_map/ppermute | solution.py:75
  32.4 1.3 collective-permute-start.2
  33.8 11.4 %collective-permute-done.33 = bf16[2,1,1,2,72,256]{5,4,3,2,1,0:T(8,128)(2,1)S(1)} collective-permute-done((bf16[2,1,1,2,72,256]{5,4,3,2,1,0:T(8,128)(2,1)S(1)}, bf16[2,1,1,2,72,256]{5,4,3,2,1,0:T(8,128)(2,1)S(1)}, u32[]{:S(2)}, u32[]{:S(2)}) %collective-permute-start.33) | collective-permute-done | bytes 147488 | tf_op jit(solution)/shard_map/ppermute | solution.py:75
  45.2 1.5 collective-permute-start.3
  46.8 0.6 collective-permute-start.35
  47.6 1.6 collective-permute-start.4
  49.2 2.8 %collective-permute-done.3.refs_5_ = bf16[32,2560]{1,0:T(8,128)(2,1)S(1)} collective-permute-done((bf16[32,2560]{1,0:T(8,128)(2,1)S(1)}, bf16[32,2560]{1,0:T(8,128)(2,1)S(1)}, u32[]{:S(2)}, u32[]{:S(2)}) %collective-permute-start.3) | collective-permute-done | bytes 163872 | tf_op jit(solution)/shard_map/ppermute | solution.py:75
  52.0 0.8 collective-permute-done.35
  52.7 1.5 collective-permute-start.5
  54.3 1.6 collective-permute-start.6
  55.9 0.5 collective-permute-start.7
  56.4 0.5 collective-permute-start.9
  56.9 1.5 collective-permute-start.10
  58.4 0.8 collective-permute-done.5.refs_7_
  59.3 2.0 %collective-permute-start.36 = (bf16[1,1,1,1,72,256]{5,4,3,2,1,0:T(8,128)(2,1)S(1)}, bf16[1,1,1,1,72,256]{5,4,3,2,1,0:T(8,128)(2,1)S(1)}, u32[]{:S(2)}, u32[]{:S(2)}) collective-permute-start(bf16[1,1,1,1,72,256]{5,4,3,2,1,0:T(8,128)(2,1)S(1)} %dynamic-slice_convert_fusion.4), channel_id=1, source_target_pairs={{0,16},{1,17},{2,18},{3,19},{4,20},{5,21},{6,22},{7,23},{8,24},{9,... | collective-permute-start | bytes 110600 | tf_op jit(solution)/shard_map/ppermute | solution.py:75
  61.4 0.7 select_n.94.refs_0_
  62.1 1.5 collective-permute-start.12
  63.6 1.3 collective-permute-start.13
  64.8 0.3 collective-permute-done.9.refs_11_
  65.2 1.5 collective-permute-done.10.refs_12_
  66.7 0.8 collective-permute-done.36
  67.5 0.6 collective-permute-start.19
  68.1 1.8 %collective-permute-done.13.refs_15_ = bf16[32,2560]{1,0:T(8,128)(2,1)S(1)} collective-permute-done((bf16[32,2560]{1,0:T(8,128)(2,1)S(1)}, bf16[32,2560]{1,0:T(8,128)(2,1)S(1)}, u32[]{:S(2)}, u32[]{:S(2)}) %collective-permute-start.13) | collective-permute-done | bytes 163872 | tf_op jit(solution)/shard_map/ppermute | solution.py:75
  69.9 1.6 collective-permute-start.8
  71.5 1.5 collective-permute-start.11
  73.0 0.5 collective-permute-start.14
  73.7 0.5 collective-permute-start.26
  74.1 2.5 %collective-permute-done.8.refs_10_ = bf16[32,2560]{1,0:T(8,128)(2,1)} collective-permute-done((bf16[32,2560]{1,0:T(8,128)(2,1)S(1)}, bf16[32,2560]{1,0:T(8,128)(2,1)}, u32[]{:S(2)}, u32[]{:S(2)}) %collective-permute-start.8) | collective-permute-done | bytes 163872 | tf_op jit(solution)/shard_map/ppermute | solution.py:75
  76.6 2.1 %collective-permute-done.11.refs_13_ = bf16[32,2560]{1,0:T(8,128)(2,1)} collective-permute-done((bf16[32,2560]{1,0:T(8,128)(2,1)S(1)}, bf16[32,2560]{1,0:T(8,128)(2,1)}, u32[]{:S(2)}, u32[]{:S(2)}) %collective-permute-start.11) | collective-permute-done | bytes 163872 | tf_op jit(solution)/shard_map/ppermute | solution.py:75
  78.7 2.7 %collective-permute-done.14.refs_16_ = bf16[32,2560]{1,0:T(8,128)(2,1)} collective-permute-done((bf16[32,2560]{1,0:T(8,128)(2,1)S(1)}, bf16[32,2560]{1,0:T(8,128)(2,1)}, u32[]{:S(2)}, u32[]{:S(2)}) %collective-permute-start.14) | collective-permute-done | bytes 163872 | tf_op jit(solution)/shard_map/ppermute | solution.py:75
  81.4 0.6 collective-permute-start.29
  82.1 0.4 collective-permute-start.24
  82.5 0.3 collective-permute-done.25.refs_27_
  82.9 0.4 collective-permute-start.30
  83.7 1.1 broadcast_in_dim.45
  84.8 3.3 %all-to-all-start = ((bf16[32,64,256]{2,1,0:T(8,128)(2,1)}), bf16[32,64,256]{2,1,0:T(8,128)(2,1)S(1)}, u32[]{:S(2)}, u32[]{:S(2)}) async-start(bf16[32,64,256]{2,1,0:T(8,128)(2,1)} %broadcast_in_dim.45), calls=%async_computation | async-start | bytes 2097152 | tf_op jit(solution)/shard_map/all_to_all | solution.py:96
  88.4 9.2 %shard_map.105 = (bf16[2560,512]{1,0:T(8,128)(2,1)}, f32[512,512]{1,0:T(8,128)}) custom-call(s32[1,1024]{1,0:T(1,128)} %select_n.94.refs_0_, bf16[32,2560]{1,0:T(8,128)(2,1)} %shard_map.104.refs_1_, bf16[32,2560]{1,0:T(8,128)(2,1)} %collective-permute-done.refs_2_, bf16[32,2560]{1,0:T(8,128)(2,1)} %collective-permute-done.1.refs_3_, ...), custom_call_target="tpu_custom_call" | custom-call | flops 6000000000 | bytes 10000000 | tf_op jit(solution)/shard_map/pallas_call | solution.py:183
  97.6 12.7 %shard_map.108 = (bf16[2048,512]{1,0:T(8,128)(2,1)}, bf16[2048,512]{1,0:T(8,128)(2,1)}, f32[256,512]{1,0:T(8,128)}) custom-call(bf16[2560,512]{1,0:T(8,128)(2,1)} %get-tuple-element.22.turned, bf16[2048,512]{1,0:T(8,128)(2,1)} %points.3, bf16[2048,2048]{1,0:T(8,128)(2,1)} %factor.3, bf16[2048,256]{1,0:T(8,128)(2,1)} %targets.1), custom_call_target="tpu_custom_call" | custom-call | flops 6000000000 | bytes 16000000 | tf_op jit(solution)/shard_map/pallas_call | solution.py:225
  110.3 1.1 broadcast_in_dim.44.r_in
  111.4 10.2 %shard_map.106 = (f32[512,512]{1,0:T(8,128)}, f32[512,512]{1,0:T(8,128)}) custom-call(f32[512,512]{1,0:T(8,128)} %get-tuple-element.18.a_in, f32[512,512]{1,0:T(8,128)} %broadcast_in_dim.44.r_in), custom_call_target="tpu_custom_call", output_to_operand_aliasing={{0}: (0, {}), {1}: (1, {})} | custom-call | flops 12000000000 | bytes 4000000 | tf_op jit(solution)/shard_map/pallas_call | solution.py:365
  121.7 5.9 %all-to-all-start.1 = ((f32[32,8,512]{2,1,0:T(8,128)}), f32[32,8,512]{2,1,0:T(8,128)S(1)}, u32[]{:S(2)}, u32[]{:S(2)}) async-start(f32[32,8,512]{2,1,0:T(8,128)} %bitcast.5), calls=%async_computation.1 | async-start | bytes 1048576 | tf_op jit(solution)/shard_map/all_to_all | solution.py:96
  127.6 10.2 %shard_map.107 = (f32[512,512]{1,0:T(8,128)}, f32[512,512]{1,0:T(8,128)}) custom-call(f32[512,512]{1,0:T(8,128)} %get-tuple-element.19.a_in, f32[512,512]{1,0:T(8,128)} %get-tuple-element.20.r_in), custom_call_target="tpu_custom_call", output_to_operand_aliasing={{0}: (0, {}), {1}: (1, {})} | custom-call | flops 12000000000 | bytes 4000000 | tf_op jit(solution)/shard_map/pallas_call | solution.py:365
  137.8 7.2 %shard_map.109 = (bf16[512,2048]{1,0:T(8,128)(2,1)}, bf16[2048,512]{1,0:T(8,128)(2,1)}, f32[1,512]{1,0:T(1,128)}) custom-call(f32[512,512]{1,0:T(8,128)} %get-tuple-element.21.inv, bf16[2048,512]{1,0:T(8,128)(2,1)} %get-tuple-element.23.high, bf16[2048,512]{1,0:T(8,128)(2,1)} %get-tuple-element.24.low), custom_call_target="tpu_custom_call" | custom-call | flops 4000000000 | bytes 8000000 | tf_op jit(solution)/shard_map/pallas_call | solution.py:406
  145.0 0.8 copy-done.1
  145.7 3.2 %shard_map.110 = bf16[32,16,512]{2,1,0:T(8,128)(2,1)} custom-call(f32[32,8,512]{2,1,0:T(8,128)} %copy-done.1, f32[512,512]{1,0:T(8,128)} %get-tuple-element.21.inv, f32[1,512]{1,0:T(1,128)} %get-tuple-element.31.norm), custom_call_target="tpu_custom_call" | custom-call | flops 100000000 | bytes 2000000 | tf_op jit(solution)/shard_map/pallas_call | solution.py:456
  148.9 5.6 %all-to-all-start.2 = ((bf16[32,16,512]{2,1,0:T(8,128)(2,1)}), bf16[32,16,512]{2,1,0:T(8,128)(2,1)S(1)}, u32[]{:S(2)}, u32[]{:S(2)}) async-start(bf16[32,16,512]{2,1,0:T(8,128)(2,1)} %shard_map.110), calls=%async_computation.2 | async-start | bytes 1048576 | tf_op jit(solution)/shard_map/all_to_all | solution.py:96
  154.5 7.1 %fusion.base = f32[2048,256]{1,0:T(8,128)} fusion(bf16[2048,2048]{1,0:T(8,128)(2,1)} %factor.3, bf16[2048,256]{1,0:T(8,128)(2,1)S(1)} %bitcast.34, bf16[2048,256]{1,0:T(8,128)(2,1)S(1)} %copy-done.10), kind=kOutput, calls=%fused_computation.4 | convolution fusion | flops 2148532224 | bytes 12582912 | tf_op jit(solution)/shard_map/dot_general | solution.py:28
  161.6 9.1 %all-to-all-done.2 = bf16[32,16,512]{2,1,0:T(8,128)(2,1)S(1)} async-done(((bf16[32,16,512]{2,1,0:T(8,128)(2,1)}), bf16[32,16,512]{2,1,0:T(8,128)(2,1)S(1)}, u32[]{:S(2)}, u32[]{:S(2)}) %all-to-all-start.2) | async-done | bytes 524320 | tf_op jit(solution)/shard_map/all_to_all | solution.py:96
  170.9 0.8 fusion.5.coef
  171.7 3.7 %shard_map.111 = f32[2048,256]{1,0:T(8,128)} custom-call(f32[2048,256]{1,0:T(8,128)} %fusion.base, bf16[2048,512]{1,0:T(8,128)(2,1)} %get-tuple-element.29.turned, bf16[256,512]{1,0:T(8,128)(2,1)} %fusion.5.coef), custom_call_target="tpu_custom_call" | custom-call | flops 1000000000 | bytes 8000000 | tf_op jit(solution)/shard_map/pallas_call | solution.py:474
  (120 shorter events, 1.9 us)
Async XLA Ops:
  0.6 9.7 %copy-start.9 = (bf16[2048,256]{1,0:T(8,128)(2,1)S(1)}, bf16[2048,256]{1,0:T(8,128)(2,1)}, u32[]{:S(2)}) copy-start(bf16[2048,256]{1,0:T(8,128)(2,1)} %targets.1) | copy-start | bytes 3145732
  5.1 5.8 %copy-start = (bf16[2048,2048]{1,0:T(8,128)(2,1)S(1)}, bf16[2048,2048]{1,0:T(8,128)(2,1)}, u32[]{:S(2)}) copy-start(bf16[2048,2048]{1,0:T(8,128)(2,1)} %factor.3) | copy-start | bytes 25165828
  13.6 6.9 %copy-start.3 = (s32[32]{0:T(128)S(1)}, s32[32]{0:T(128)}, u32[]{:S(2)}) copy-start(s32[32]{0:T(128)} %param.13) | copy-start | bytes 388
  14.8 8.4 %collective-permute-start.31 = (f32[2,1,4,2,72,256]{5,4,3,2,1,0:T(8,128)}, f32[2,1,4,2,72,256]{5,4,3,2,1,0:T(8,128)S(1)}, u32[]{:S(2)}, u32[]{:S(2)}) collective-permute-start(f32[2,1,4,2,72,256]{5,4,3,2,1,0:T(8,128)} %fusion.1), channel_id=1, source_target_pairs={{0,8},{1,9},{2,10},{3,11},{4,12},{5,13},{6,14},{7,15},{8,0},{9,1},... | collective-permute-start | bytes 3538952 | tf_op jit(solution)/shard_map/ppermute | solution.py:75
  15.3 32.3 %collective-permute-start = (bf16[32,2560]{1,0:T(8,128)(2,1)}, bf16[32,2560]{1,0:T(8,128)(2,1)}, u32[]{:S(2)}, u32[]{:S(2)}) collective-permute-start(bf16[32,2560]{1,0:T(8,128)(2,1)} %shard_map.104.refs_1_), channel_id=1, source_target_pairs={{0,2},{1,3},{2,0},{3,1},{4,6},{5,7},{6,4},{7,5},{8,10},{9,11},{10,... | collective-permute-start | bytes 491528 | tf_op jit(solution)/shard_map/ppermute | solution.py:75
  17.9 36.4 %collective-permute-start.1 = (bf16[32,2560]{1,0:T(8,128)(2,1)}, bf16[32,2560]{1,0:T(8,128)(2,1)}, u32[]{:S(2)}, u32[]{:S(2)}) collective-permute-start(bf16[32,2560]{1,0:T(8,128)(2,1)} %shard_map.104.refs_1_), channel_id=1, source_target_pairs={{0,4},{1,5},{2,6},{3,7},{4,0},{5,1},{6,2},{7,3},{8,12},{9,13},{10,... | collective-permute-start | bytes 491528 | tf_op jit(solution)/shard_map/ppermute | solution.py:75
  23.2 4.7 %copy-start.7 = (s32[32]{0:T(128)S(1)}, s32[32]{0:T(128)}, u32[]{:S(2)}) copy-start(s32[32]{0:T(128)} %constant.118.clone) | copy-start | bytes 388
  23.2 4.7 %copy-start.8 = (s32[32]{0:T(128)S(1)}, s32[32]{0:T(128)}, u32[]{:S(2)}) copy-start(s32[32]{0:T(128)} %constant.117.clone) | copy-start | bytes 388
  23.2 9.2 %copy-start.2 = (bf16[32,2560]{1,0:T(8,128)(2,1)S(1)}, bf16[32,2560]{1,0:T(8,128)(2,1)}, u32[]{:S(2)}) copy-start(bf16[32,2560]{1,0:T(8,128)(2,1)} %shard_map.104.refs_1_) | copy-start | bytes 491524
  23.2 24.2 %copy-start.4 = (s32[32]{0:T(128)S(1)}, s32[32]{0:T(128)}, u32[]{:S(2)}) copy-start(s32[32]{0:T(128)} %param.13) | copy-start | bytes 388
  23.5 8.9 %collective-permute-start.34 = (bf16[2,1,1,2,72,256]{5,4,3,2,1,0:T(8,128)(2,1)S(1)}, bf16[2,1,1,2,72,256]{5,4,3,2,1,0:T(8,128)(2,1)S(1)}, u32[]{:S(2)}, u32[]{:S(2)}) collective-permute-start(bf16[2,1,1,2,72,256]{5,4,3,2,1,0:T(8,128)(2,1)S(1)} %get-tuple-element.35), channel_id=1, source_target_pairs={{0,6},{1,7},{2,4},{3,5},{4,2},{5,3},{6,0},{7,1},{8,14},{9,15},{10,... | collective-permute-start | bytes 442376 | tf_op jit(solution)/shard_map/ppermute | solution.py:75
  23.6 21.6 %collective-permute-start.33 = (bf16[2,1,1,2,72,256]{5,4,3,2,1,0:T(8,128)(2,1)S(1)}, bf16[2,1,1,2,72,256]{5,4,3,2,1,0:T(8,128)(2,1)S(1)}, u32[]{:S(2)}, u32[]{:S(2)}) collective-permute-start(bf16[2,1,1,2,72,256]{5,4,3,2,1,0:T(8,128)(2,1)S(1)} %get-tuple-element.36), channel_id=1, source_target_pairs={{0,4},{1,5},{2,6},{3,7},{4,0},{5,1},{6,2},{7,3},{8,12},{9,13},{10,... | collective-permute-start | bytes 442376 | tf_op jit(solution)/shard_map/ppermute | solution.py:75
  25.5 21.2 %collective-permute-start.32 = (bf16[2,1,1,2,72,256]{5,4,3,2,1,0:T(8,128)(2,1)S(1)}, bf16[2,1,1,2,72,256]{5,4,3,2,1,0:T(8,128)(2,1)S(1)}, u32[]{:S(2)}, u32[]{:S(2)}) collective-permute-start(bf16[2,1,1,2,72,256]{5,4,3,2,1,0:T(8,128)(2,1)S(1)} %get-tuple-element.34), channel_id=1, source_target_pairs={{0,2},{1,3},{2,0},{3,1},{4,6},{5,7},{6,4},{7,5},{8,10},{9,11},{10,... | collective-permute-start | bytes 442376 | tf_op jit(solution)/shard_map/ppermute | solution.py:75
  32.4 23.5 %collective-permute-start.2 = (bf16[32,2560]{1,0:T(8,128)(2,1)S(1)}, bf16[32,2560]{1,0:T(8,128)(2,1)S(1)}, u32[]{:S(2)}, u32[]{:S(2)}) collective-permute-start(bf16[32,2560]{1,0:T(8,128)(2,1)S(1)} %copy-done.2), channel_id=1, source_target_pairs={{0,6},{1,7},{2,4},{3,5},{4,2},{5,3},{6,0},{7,1},{8,14},{9,15},{10,... | collective-permute-start | bytes 491528 | tf_op jit(solution)/shard_map/ppermute | solution.py:75
  45.2 6.7 %collective-permute-start.3 = (bf16[32,2560]{1,0:T(8,128)(2,1)S(1)}, bf16[32,2560]{1,0:T(8,128)(2,1)S(1)}, u32[]{:S(2)}, u32[]{:S(2)}) collective-permute-start(bf16[32,2560]{1,0:T(8,128)(2,1)S(1)} %copy-done.2), channel_id=1, source_target_pairs={{0,1},{1,0},{2,3},{3,2},{4,5},{5,4},{6,7},{7,6},{8,9},{9,8},{10,11... | collective-permute-start | bytes 491528 | tf_op jit(solution)/shard_map/ppermute | solution.py:75
  46.8 5.9 %collective-permute-start.35 = (bf16[2,1,1,1,72,256]{5,4,3,2,1,0:T(8,128)(2,1)S(1)}, bf16[2,1,1,1,72,256]{5,4,3,2,1,0:T(8,128)(2,1)S(1)}, u32[]{:S(2)}, u32[]{:S(2)}) collective-permute-start(bf16[2,1,1,1,72,256]{5,4,3,2,1,0:T(8,128)(2,1)S(1)} %dynamic-slice_convert_fusion.3), channel_id=1, source_target_pairs={{0,1},{1,0},{2,3},{3,2},{4,5},{5,4},{6,7},{7,6},{8,9},{9,8},{10,11... | collective-permute-start | bytes 221192 | tf_op jit(solution)/shard_map/ppermute | solution.py:75
  47.6 8.8 %collective-permute-start.4 = (bf16[32,2560]{1,0:T(8,128)(2,1)S(1)}, bf16[32,2560]{1,0:T(8,128)(2,1)S(1)}, u32[]{:S(2)}, u32[]{:S(2)}) collective-permute-start(bf16[32,2560]{1,0:T(8,128)(2,1)S(1)} %copy-done.2), channel_id=1, source_target_pairs={{0,16},{1,17},{2,18},{3,19},{4,20},{5,21},{6,22},{7,23},{8,24},{9,... | collective-permute-start | bytes 491528 | tf_op jit(solution)/shard_map/ppermute | solution.py:75
  51.9 36.3 %copy-start.12 = (bf16[32,2560]{1,0:T(8,128)(2,1)}, bf16[32,2560]{1,0:T(8,128)(2,1)S(1)}, u32[]{:S(2)}) copy-start(bf16[32,2560]{1,0:T(8,128)(2,1)S(1)} %collective-permute-done.3.refs_5_) | copy-start | bytes 491524
  51.9 5.0 %collective-permute-start.15 = (bf16[32,2560]{1,0:T(8,128)(2,1)S(1)}, bf16[32,2560]{1,0:T(8,128)(2,1)S(1)}, u32[]{:S(2)}, u32[]{:S(2)}) collective-permute-start(bf16[32,2560]{1,0:T(8,128)(2,1)S(1)} %copy-done.2), channel_id=1, source_target_pairs={{0,8},{1,9},{2,10},{3,11},{4,12},{5,13},{6,14},{7,15},{8,0},{9,1},... | collective-permute-start | bytes 491528 | tf_op jit(solution)/shard_map/ppermute | solution.py:75
  52.7 6.5 %collective-permute-start.5 = (bf16[32,2560]{1,0:T(8,128)(2,1)S(1)}, bf16[32,2560]{1,0:T(8,128)(2,1)S(1)}, u32[]{:S(2)}, u32[]{:S(2)}) collective-permute-start(bf16[32,2560]{1,0:T(8,128)(2,1)S(1)} %collective-permute-done.3.refs_5_), channel_id=1, source_target_pairs={{0,16},{1,17},{2,18},{3,19},{4,20},{5,21},{6,22},{7,23},{8,24},{9,... | collective-permute-start | bytes 491528 | tf_op jit(solution)/shard_map/ppermute | solution.py:75
  54.3 7.8 %collective-permute-start.6 = (bf16[32,2560]{1,0:T(8,128)(2,1)}, bf16[32,2560]{1,0:T(8,128)(2,1)S(1)}, u32[]{:S(2)}, u32[]{:S(2)}) collective-permute-start(bf16[32,2560]{1,0:T(8,128)(2,1)} %collective-permute-done.refs_2_), channel_id=1, source_target_pairs={{0,1},{1,0},{2,3},{3,2},{4,5},{5,4},{6,7},{7,6},{8,9},{9,8},{10,11... | collective-permute-start | bytes 491528 | tf_op jit(solution)/shard_map/ppermute | solution.py:75
  55.9 32.4 %copy-start.11 = (bf16[32,2560]{1,0:T(8,128)(2,1)}, bf16[32,2560]{1,0:T(8,128)(2,1)S(1)}, u32[]{:S(2)}) copy-start(bf16[32,2560]{1,0:T(8,128)(2,1)S(1)} %collective-permute-done.2.refs_4_) | copy-start | bytes 491524
  55.9 7.7 %collective-permute-start.7 = (bf16[32,2560]{1,0:T(8,128)(2,1)}, bf16[32,2560]{1,0:T(8,128)(2,1)S(1)}, u32[]{:S(2)}, u32[]{:S(2)}) collective-permute-start(bf16[32,2560]{1,0:T(8,128)(2,1)} %collective-permute-done.refs_2_), channel_id=1, source_target_pairs={{0,16},{1,17},{2,18},{3,19},{4,20},{5,21},{6,22},{7,23},{8,24},{9,... | collective-permute-start | bytes 491528 | tf_op jit(solution)/shard_map/ppermute | solution.py:75
  56.4 31.9 %copy-start.13 = (bf16[32,2560]{1,0:T(8,128)(2,1)}, bf16[32,2560]{1,0:T(8,128)(2,1)S(1)}, u32[]{:S(2)}) copy-start(bf16[32,2560]{1,0:T(8,128)(2,1)S(1)} %collective-permute-done.4.refs_6_) | copy-start | bytes 491524
  56.4 8.8 %collective-permute-start.9 = (bf16[32,2560]{1,0:T(8,128)(2,1)}, bf16[32,2560]{1,0:T(8,128)(2,1)S(1)}, u32[]{:S(2)}, u32[]{:S(2)}) collective-permute-start(bf16[32,2560]{1,0:T(8,128)(2,1)} %collective-permute-done.1.refs_3_), channel_id=1, source_target_pairs={{0,1},{1,0},{2,3},{3,2},{4,5},{5,4},{6,7},{7,6},{8,9},{9,8},{10,11... | collective-permute-start | bytes 491528 | tf_op jit(solution)/shard_map/ppermute | solution.py:75
  56.9 31.3 %copy-start.14 = (bf16[32,2560]{1,0:T(8,128)(2,1)}, bf16[32,2560]{1,0:T(8,128)(2,1)S(1)}, u32[]{:S(2)}) copy-start(bf16[32,2560]{1,0:T(8,128)(2,1)S(1)} %collective-permute-done.15.refs_17_) | copy-start | bytes 491524
  56.9 9.7 %collective-permute-start.10 = (bf16[32,2560]{1,0:T(8,128)(2,1)}, bf16[32,2560]{1,0:T(8,128)(2,1)S(1)}, u32[]{:S(2)}, u32[]{:S(2)}) collective-permute-start(bf16[32,2560]{1,0:T(8,128)(2,1)} %collective-permute-done.1.refs_3_), channel_id=1, source_target_pairs={{0,16},{1,17},{2,18},{3,19},{4,20},{5,21},{6,22},{7,23},{8,24},{9,... | collective-permute-start | bytes 491528 | tf_op jit(solution)/shard_map/ppermute | solution.py:75
  59.3 29.0 %copy-start.15 = (bf16[32,2560]{1,0:T(8,128)(2,1)}, bf16[32,2560]{1,0:T(8,128)(2,1)S(1)}, u32[]{:S(2)}) copy-start(bf16[32,2560]{1,0:T(8,128)(2,1)S(1)} %collective-permute-done.5.refs_7_) | copy-start | bytes 491524
  59.3 8.2 %collective-permute-start.36 = (bf16[1,1,1,1,72,256]{5,4,3,2,1,0:T(8,128)(2,1)S(1)}, bf16[1,1,1,1,72,256]{5,4,3,2,1,0:T(8,128)(2,1)S(1)}, u32[]{:S(2)}, u32[]{:S(2)}) collective-permute-start(bf16[1,1,1,1,72,256]{5,4,3,2,1,0:T(8,128)(2,1)S(1)} %dynamic-slice_convert_fusion.4), channel_id=1, source_target_pairs={{0,16},{1,17},{2,18},{3,19},{4,20},{5,21},{6,22},{7,23},{8,24},{9,... | collective-permute-start | bytes 110600 | tf_op jit(solution)/shard_map/ppermute | solution.py:75
  62.1 26.2 %copy-start.16 = (bf16[32,2560]{1,0:T(8,128)(2,1)}, bf16[32,2560]{1,0:T(8,128)(2,1)S(1)}, u32[]{:S(2)}) copy-start(bf16[32,2560]{1,0:T(8,128)(2,1)S(1)} %collective-permute-done.6.refs_8_) | copy-start | bytes 491524
  62.1 5.4 %collective-permute-start.12 = (bf16[32,2560]{1,0:T(8,128)(2,1)S(1)}, bf16[32,2560]{1,0:T(8,128)(2,1)S(1)}, u32[]{:S(2)}, u32[]{:S(2)}) collective-permute-start(bf16[32,2560]{1,0:T(8,128)(2,1)S(1)} %collective-permute-done.2.refs_4_), channel_id=1, source_target_pairs={{0,1},{1,0},{2,3},{3,2},{4,5},{5,4},{6,7},{7,6},{8,9},{9,8},{10,11... | collective-permute-start | bytes 491528 | tf_op jit(solution)/shard_map/ppermute | solution.py:75
  63.6 24.7 %copy-start.17 = (bf16[32,2560]{1,0:T(8,128)(2,1)}, bf16[32,2560]{1,0:T(8,128)(2,1)S(1)}, u32[]{:S(2)}) copy-start(bf16[32,2560]{1,0:T(8,128)(2,1)S(1)} %collective-permute-done.7.refs_9_) | copy-start | bytes 491524
  63.6 6.3 %collective-permute-start.13 = (bf16[32,2560]{1,0:T(8,128)(2,1)S(1)}, bf16[32,2560]{1,0:T(8,128)(2,1)S(1)}, u32[]{:S(2)}, u32[]{:S(2)}) collective-permute-start(bf16[32,2560]{1,0:T(8,128)(2,1)S(1)} %collective-permute-done.2.refs_4_), channel_id=1, source_target_pairs={{0,16},{1,17},{2,18},{3,19},{4,20},{5,21},{6,22},{7,23},{8,24},{9,... | collective-permute-start | bytes 491528 | tf_op jit(solution)/shard_map/ppermute | solution.py:75
  65.2 23.1 %copy-start.18 = (bf16[32,2560]{1,0:T(8,128)(2,1)}, bf16[32,2560]{1,0:T(8,128)(2,1)S(1)}, u32[]{:S(2)}) copy-start(bf16[32,2560]{1,0:T(8,128)(2,1)S(1)} %collective-permute-done.9.refs_11_) | copy-start | bytes 491524
  65.2 4.7 %collective-permute-start.16 = (bf16[32,2560]{1,0:T(8,128)(2,1)}, bf16[32,2560]{1,0:T(8,128)(2,1)S(1)}, u32[]{:S(2)}, u32[]{:S(2)}) collective-permute-start(bf16[32,2560]{1,0:T(8,128)(2,1)} %collective-permute-done.refs_2_), channel_id=1, source_target_pairs={{0,8},{1,9},{2,10},{3,11},{4,12},{5,13},{6,14},{7,15},{8,0},{9,1},... | collective-permute-start | bytes 491528 | tf_op jit(solution)/shard_map/ppermute | solution.py:75
  66.7 21.6 %copy-start.19 = (bf16[32,2560]{1,0:T(8,128)(2,1)}, bf16[32,2560]{1,0:T(8,128)(2,1)S(1)}, u32[]{:S(2)}) copy-start(bf16[32,2560]{1,0:T(8,128)(2,1)S(1)} %collective-permute-done.10.refs_12_) | copy-start | bytes 491524
  66.7 4.8 %collective-permute-start.17 = (bf16[32,2560]{1,0:T(8,128)(2,1)}, bf16[32,2560]{1,0:T(8,128)(2,1)S(1)}, u32[]{:S(2)}, u32[]{:S(2)}) collective-permute-start(bf16[32,2560]{1,0:T(8,128)(2,1)} %collective-permute-done.1.refs_3_), channel_id=1, source_target_pairs={{0,8},{1,9},{2,10},{3,11},{4,12},{5,13},{6,14},{7,15},{8,0},{9,1},... | collective-permute-start | bytes 491528 | tf_op jit(solution)/shard_map/ppermute | solution.py:75
  67.5 5.5 %collective-permute-start.18 = (bf16[32,2560]{1,0:T(8,128)(2,1)S(1)}, bf16[32,2560]{1,0:T(8,128)(2,1)S(1)}, u32[]{:S(2)}, u32[]{:S(2)}) collective-permute-start(bf16[32,2560]{1,0:T(8,128)(2,1)S(1)} %collective-permute-done.2.refs_4_), channel_id=1, source_target_pairs={{0,8},{1,9},{2,10},{3,11},{4,12},{5,13},{6,14},{7,15},{8,0},{9,1},... | collective-permute-start | bytes 491528 | tf_op jit(solution)/shard_map/ppermute | solution.py:75
  67.5 20.8 %copy-start.20 = (bf16[32,2560]{1,0:T(8,128)(2,1)}, bf16[32,2560]{1,0:T(8,128)(2,1)S(1)}, u32[]{:S(2)}) copy-start(bf16[32,2560]{1,0:T(8,128)(2,1)S(1)} %collective-permute-done.12.refs_14_) | copy-start | bytes 491524
  67.5 6.1 %collective-permute-start.19 = (bf16[32,2560]{1,0:T(8,128)(2,1)S(1)}, bf16[32,2560]{1,0:T(8,128)(2,1)S(1)}, u32[]{:S(2)}, u32[]{:S(2)}) collective-permute-start(bf16[32,2560]{1,0:T(8,128)(2,1)S(1)} %collective-permute-done.3.refs_5_), channel_id=1, source_target_pairs={{0,8},{1,9},{2,10},{3,11},{4,12},{5,13},{6,14},{7,15},{8,0},{9,1},... | collective-permute-start | bytes 491528 | tf_op jit(solution)/shard_map/ppermute | solution.py:75
  69.9 18.4 %copy-start.21 = (bf16[32,2560]{1,0:T(8,128)(2,1)}, bf16[32,2560]{1,0:T(8,128)(2,1)S(1)}, u32[]{:S(2)}) copy-start(bf16[32,2560]{1,0:T(8,128)(2,1)S(1)} %collective-permute-done.13.refs_15_) | copy-start | bytes 491524
  69.9 3.7 %collective-permute-start.20 = (bf16[32,2560]{1,0:T(8,128)(2,1)S(1)}, bf16[32,2560]{1,0:T(8,128)(2,1)S(1)}, u32[]{:S(2)}, u32[]{:S(2)}) collective-permute-start(bf16[32,2560]{1,0:T(8,128)(2,1)S(1)} %collective-permute-done.4.refs_6_), channel_id=1, source_target_pairs={{0,8},{1,9},{2,10},{3,11},{4,12},{5,13},{6,14},{7,15},{8,0},{9,1},... | collective-permute-start | bytes 491528 | tf_op jit(solution)/shard_map/ppermute | solution.py:75
  69.9 18.4 %copy-start.22 = (bf16[32,2560]{1,0:T(8,128)(2,1)}, bf16[32,2560]{1,0:T(8,128)(2,1)S(1)}, u32[]{:S(2)}) copy-start(bf16[32,2560]{1,0:T(8,128)(2,1)S(1)} %collective-permute-done.16.refs_18_) | copy-start | bytes 491524
  69.9 6.7 %collective-permute-start.8 = (bf16[32,2560]{1,0:T(8,128)(2,1)S(1)}, bf16[32,2560]{1,0:T(8,128)(2,1)}, u32[]{:S(2)}, u32[]{:S(2)}) collective-permute-start(bf16[32,2560]{1,0:T(8,128)(2,1)S(1)} %collective-permute-done.6.refs_8_), channel_id=1, source_target_pairs={{0,16},{1,17},{2,18},{3,19},{4,20},{5,21},{6,22},{7,23},{8,24},{9,... | collective-permute-start | bytes 491528 | tf_op jit(solution)/shard_map/ppermute | solution.py:75
  71.5 16.8 %copy-start.23 = (bf16[32,2560]{1,0:T(8,128)(2,1)}, bf16[32,2560]{1,0:T(8,128)(2,1)S(1)}, u32[]{:S(2)}) copy-start(bf16[32,2560]{1,0:T(8,128)(2,1)S(1)} %collective-permute-done.17.refs_19_) | copy-start | bytes 491524
  71.5 7.2 %collective-permute-start.11 = (bf16[32,2560]{1,0:T(8,128)(2,1)S(1)}, bf16[32,2560]{1,0:T(8,128)(2,1)}, u32[]{:S(2)}, u32[]{:S(2)}) collective-permute-start(bf16[32,2560]{1,0:T(8,128)(2,1)S(1)} %collective-permute-done.10.refs_12_), channel_id=1, source_target_pairs={{0,1},{1,0},{2,3},{3,2},{4,5},{5,4},{6,7},{7,6},{8,9},{9,8},{10,11... | collective-permute-start | bytes 491528 | tf_op jit(solution)/shard_map/ppermute | solution.py:75
  73.0 15.4 %copy-start.24 = (bf16[32,2560]{1,0:T(8,128)(2,1)}, bf16[32,2560]{1,0:T(8,128)(2,1)S(1)}, u32[]{:S(2)}) copy-start(bf16[32,2560]{1,0:T(8,128)(2,1)S(1)} %collective-permute-done.18.refs_20_) | copy-start | bytes 491524
  73.0 8.4 %collective-permute-start.14 = (bf16[32,2560]{1,0:T(8,128)(2,1)S(1)}, bf16[32,2560]{1,0:T(8,128)(2,1)}, u32[]{:S(2)}, u32[]{:S(2)}) collective-permute-start(bf16[32,2560]{1,0:T(8,128)(2,1)S(1)} %collective-permute-done.13.refs_15_), channel_id=1, source_target_pairs={{0,1},{1,0},{2,3},{3,2},{4,5},{5,4},{6,7},{7,6},{8,9},{9,8},{10,11... | collective-permute-start | bytes 491528 | tf_op jit(solution)/shard_map/ppermute | solution.py:75
  73.6 14.8 %copy-start.25 = (bf16[32,2560]{1,0:T(8,128)(2,1)}, bf16[32,2560]{1,0:T(8,128)(2,1)S(1)}, u32[]{:S(2)}) copy-start(bf16[32,2560]{1,0:T(8,128)(2,1)S(1)} %collective-permute-done.19.refs_21_) | copy-start | bytes 491524
  73.6 8.4 %collective-permute-start.22 = (bf16[32,2560]{1,0:T(8,128)(2,1)S(1)}, bf16[32,2560]{1,0:T(8,128)(2,1)S(1)}, u32[]{:S(2)}, u32[]{:S(2)}) collective-permute-start(bf16[32,2560]{1,0:T(8,128)(2,1)S(1)} %collective-permute-done.6.refs_8_), channel_id=1, source_target_pairs={{0,8},{1,9},{2,10},{3,11},{4,12},{5,13},{6,14},{7,15},{8,0},{9,1},... | collective-permute-start | bytes 491528 | tf_op jit(solution)/shard_map/ppermute | solution.py:75
  73.7 9.3 %copy-start.26 = (bf16[32,2560]{1,0:T(8,128)(2,1)}, bf16[32,2560]{1,0:T(8,128)(2,1)S(1)}, u32[]{:S(2)}) copy-start(bf16[32,2560]{1,0:T(8,128)(2,1)S(1)} %collective-permute-done.20.refs_22_) | copy-start | bytes 491524
  73.7 9.3 %collective-permute-start.26 = (bf16[32,2560]{1,0:T(8,128)(2,1)S(1)}, bf16[32,2560]{1,0:T(8,128)(2,1)S(1)}, u32[]{:S(2)}, u32[]{:S(2)}) collective-permute-start(bf16[32,2560]{1,0:T(8,128)(2,1)S(1)} %collective-permute-done.10.refs_12_), channel_id=1, source_target_pairs={{0,8},{1,9},{2,10},{3,11},{4,12},{5,13},{6,14},{7,15},{8,0},{9,1},... | collective-permute-start | bytes 491528 | tf_op jit(solution)/shard_map/ppermute | solution.py:75
  76.6 4.8 %collective-permute-start.21 = (bf16[32,2560]{1,0:T(8,128)(2,1)S(1)}, bf16[32,2560]{1,0:T(8,128)(2,1)S(1)}, u32[]{:S(2)}, u32[]{:S(2)}) collective-permute-start(bf16[32,2560]{1,0:T(8,128)(2,1)S(1)} %collective-permute-done.5.refs_7_), channel_id=1, source_target_pairs={{0,8},{1,9},{2,10},{3,11},{4,12},{5,13},{6,14},{7,15},{8,0},{9,1},... | collective-permute-start | bytes 491528 | tf_op jit(solution)/shard_map/ppermute | solution.py:75
  78.7 3.4 %collective-permute-start.23 = (bf16[32,2560]{1,0:T(8,128)(2,1)S(1)}, bf16[32,2560]{1,0:T(8,128)(2,1)S(1)}, u32[]{:S(2)}, u32[]{:S(2)}) collective-permute-start(bf16[32,2560]{1,0:T(8,128)(2,1)S(1)} %collective-permute-done.7.refs_9_), channel_id=1, source_target_pairs={{0,8},{1,9},{2,10},{3,11},{4,12},{5,13},{6,14},{7,15},{8,0},{9,1},... | collective-permute-start | bytes 491528 | tf_op jit(solution)/shard_map/ppermute | solution.py:75
  81.4 1.4 collective-permute-start.25
  81.4 6.8 %collective-permute-start.29 = (bf16[32,2560]{1,0:T(8,128)(2,1)S(1)}, bf16[32,2560]{1,0:T(8,128)(2,1)}, u32[]{:S(2)}, u32[]{:S(2)}) collective-permute-start(bf16[32,2560]{1,0:T(8,128)(2,1)S(1)} %collective-permute-done.13.refs_15_), channel_id=1, source_target_pairs={{0,8},{1,9},{2,10},{3,11},{4,12},{5,13},{6,14},{7,15},{8,0},{9,1},... | collective-permute-start | bytes 491528 | tf_op jit(solution)/shard_map/ppermute | solution.py:75
  82.0 6.2 %collective-permute-start.28 = (bf16[32,2560]{1,0:T(8,128)(2,1)S(1)}, bf16[32,2560]{1,0:T(8,128)(2,1)}, u32[]{:S(2)}, u32[]{:S(2)}) collective-permute-start(bf16[32,2560]{1,0:T(8,128)(2,1)S(1)} %collective-permute-done.12.refs_14_), channel_id=1, source_target_pairs={{0,8},{1,9},{2,10},{3,11},{4,12},{5,13},{6,14},{7,15},{8,0},{9,1},... | collective-permute-start | bytes 491528 | tf_op jit(solution)/shard_map/ppermute | solution.py:75
  82.1 6.1 %collective-permute-start.24 = (bf16[32,2560]{1,0:T(8,128)(2,1)}, bf16[32,2560]{1,0:T(8,128)(2,1)}, u32[]{:S(2)}, u32[]{:S(2)}) collective-permute-start(bf16[32,2560]{1,0:T(8,128)(2,1)} %collective-permute-done.8.refs_10_), channel_id=1, source_target_pairs={{0,8},{1,9},{2,10},{3,11},{4,12},{5,13},{6,14},{7,15},{8,0},{9,1},... | collective-permute-start | bytes 491528 | tf_op jit(solution)/shard_map/ppermute | solution.py:75
  82.8 5.4 %collective-permute-start.27 = (bf16[32,2560]{1,0:T(8,128)(2,1)}, bf16[32,2560]{1,0:T(8,128)(2,1)}, u32[]{:S(2)}, u32[]{:S(2)}) collective-permute-start(bf16[32,2560]{1,0:T(8,128)(2,1)} %collective-permute-done.11.refs_13_), channel_id=1, source_target_pairs={{0,8},{1,9},{2,10},{3,11},{4,12},{5,13},{6,14},{7,15},{8,0},{9,1},... | collective-permute-start | bytes 491528 | tf_op jit(solution)/shard_map/ppermute | solution.py:75
  82.9 5.3 %collective-permute-start.30 = (bf16[32,2560]{1,0:T(8,128)(2,1)}, bf16[32,2560]{1,0:T(8,128)(2,1)}, u32[]{:S(2)}, u32[]{:S(2)}) collective-permute-start(bf16[32,2560]{1,0:T(8,128)(2,1)} %collective-permute-done.14.refs_16_), channel_id=1, source_target_pairs={{0,8},{1,9},{2,10},{3,11},{4,12},{5,13},{6,14},{7,15},{8,0},{9,1},... | collective-permute-start | bytes 491528 | tf_op jit(solution)/shard_map/ppermute | solution.py:75
  84.8 36.8 %all-to-all-start = ((bf16[32,64,256]{2,1,0:T(8,128)(2,1)}), bf16[32,64,256]{2,1,0:T(8,128)(2,1)S(1)}, u32[]{:S(2)}, u32[]{:S(2)}) async-start(bf16[32,64,256]{2,1,0:T(8,128)(2,1)} %broadcast_in_dim.45), calls=%async_computation | async-start | bytes 2097152 | tf_op jit(solution)/shard_map/all_to_all | solution.py:96
  121.7 23.3 %all-to-all-start.1 = ((f32[32,8,512]{2,1,0:T(8,128)}), f32[32,8,512]{2,1,0:T(8,128)S(1)}, u32[]{:S(2)}, u32[]{:S(2)}) async-start(f32[32,8,512]{2,1,0:T(8,128)} %bitcast.5), calls=%async_computation.1 | async-start | bytes 1048576 | tf_op jit(solution)/shard_map/all_to_all | solution.py:96
  144.9 9.6 %copy-start.10 = (bf16[2048,256]{1,0:T(8,128)(2,1)S(1)}, bf16[2048,256]{1,0:T(8,128)(2,1)}, u32[]{:S(2)}) copy-start(bf16[2048,256]{1,0:T(8,128)(2,1)} %targets.1) | copy-start | bytes 3145732
  148.9 21.9 %all-to-all-start.2 = ((bf16[32,16,512]{2,1,0:T(8,128)(2,1)}), bf16[32,16,512]{2,1,0:T(8,128)(2,1)S(1)}, u32[]{:S(2)}, u32[]{:S(2)}) async-start(bf16[32,16,512]{2,1,0:T(8,128)(2,1)} %shard_map.110), calls=%async_computation.2 | async-start | bytes 1048576 | tf_op jit(solution)/shard_map/all_to_all | solution.py:96
  (8 other events, 16.3 us)
